TPU v7x, 32 devices: a whole 2x2x4 slice. The times are simulated.
32 devices in a mesh: fsdp: 32 (over z, y, x, core).
Axes of the slice: x: 2, y: 2, z: 4, core: 2. Of those that a mesh axis runs over, the one named last changes fastest.
Arguments:
- inputs: bfloat16 [32768, 768], P('fsdp'), may hold values from -6 to 6
- cotangent: bfloat16 [32768, 768], P('fsdp'), may hold values from -6 to 6
- lengths: int32 [64, 8], P('fsdp'), may hold values from 0 to 128, as said below
- timesteps: int32 [64, 8], P('fsdp'), may hold values from 0 to 1999
- time_weight: bfloat16 [128, 768], P(None, 'fsdp'), may hold values from -0.5 to 0.5
- time_bias: bfloat16 [768], P('fsdp'), may hold values from -1.1953125 to 1.1953125
- query_weight: bfloat16 [768, 768], P('fsdp'), may hold values from -0.21875 to 0.21875
- query_bias: bfloat16 [768], P('fsdp'), may hold values from -1.1953125 to 1.1953125
- key_weight: bfloat16 [768, 768], P('fsdp'), may hold values from -0.21875 to 0.21875
- value_weight: bfloat16 [768, 768], P('fsdp'), may hold values from -0.21875 to 0.21875
- value_bias: bfloat16 [768], P('fsdp'), may hold values from -1.1953125 to 1.1953125
- out_weight: bfloat16 [768, 768], P('fsdp'), may hold values from -0.875 to 0.875
- out_bias: bfloat16 [768], P('fsdp'), may hold values from -1.1953125 to 1.1953125
- mid_gain: bfloat16 [768], P('fsdp'), may hold values from 0.5 to 1.5
- mid_shift: bfloat16 [768], P('fsdp'), may hold values from -1.1953125 to 1.1953125
- up_weight: bfloat16 [768, 3072], P('fsdp'), may hold values from -0.21875 to 0.21875
- up_bias: bfloat16 [3072], P('fsdp'), may hold values from -1.1953125 to 1.1953125
- down_weight: bfloat16 [3072, 768], P('fsdp'), may hold values from -0.109375 to 0.109375
- down_bias: bfloat16 [768], P('fsdp'), may hold values from -1.1953125 to 1.1953125
- last_gain: bfloat16 [768], P('fsdp'), may hold values from 0.5 to 1.5
- last_shift: bfloat16 [768], P('fsdp'), may hold values from -1.1953125 to 1.1953125
Outputs:
- layer_out: bfloat16 [32768, 768], P('fsdp')
- input_grad: float32 [32768, 768], P('fsdp')
- time_weight_grad: float32 [128, 768], P(None, 'fsdp')
- query_weight_grad: float32 [768, 768], P('fsdp')
- key_weight_grad: float32 [768, 768], P('fsdp')
- value_weight_grad: float32 [768, 768], P('fsdp')
- out_weight_grad: float32 [768, 768], P('fsdp')
- up_weight_grad: float32 [768, 3072], P('fsdp')
- down_weight_grad: float32 [3072, 768], P('fsdp')
- time_bias_grad: float32 [768], P('fsdp')
- query_bias_grad: float32 [768], P('fsdp')
- value_bias_grad: float32 [768], P('fsdp')
- out_bias_grad: float32 [768], P('fsdp')
- mid_gain_grad: float32 [768], P('fsdp')
- mid_shift_grad: float32 [768], P('fsdp')
- up_bias_grad: float32 [3072], P('fsdp')
- down_bias_grad: float32 [768], P('fsdp')
- last_gain_grad: float32 [768], P('fsdp')
- last_shift_grad: float32 [768], P('fsdp')
Inputs may be any that keep to these rules, and one draw needn't show every extreme that they name: Each row gives the lengths of the sequences packed in order into one block of 512 rows; every entry is 0, 64 or 128, the row sums to 512, and every row holds at least one entry of each nonzero length. `timesteps`: the diffusion step of the sequence in each slot; slots of length 0 carry a step too.
All inputs are finite; a program needn't handle non-finite values.
Results may differ from a plain program's by a relative error of at most 0.017.
Values may be sent and summed in bfloat16 or wider, within the bound.
No kernel may reach another device: no remote copies, remote signals or barrier semaphores. Data moves between devices by JAX's collectives and lax.ppermute only.
A program may use at most 128 MiB of HBM per device.

v0:
```python
import functools
import math

import jax
import jax.numpy as jnp
from jax import lax
from jax.experimental import pallas as pl
from jax.experimental.pallas import tpu as pltpu
from jax.sharding import PartitionSpec as P

D = 768
HEAD = 64
HEADS = 12
FF = 3072
TDIM = 128
SLOTS = 8
BLOCK = 512
HALF = D // 2
QKV = 3 * HALF
CHIPS = 16
EPS = 1e-05
NEG = -1e30
HIGH = lax.Precision.HIGHEST
SQRT_HALF = 0.7071067811865476
INV_ROOT_TAU = 0.3989422804014327
WINDOWS = (0, 64, 192, 256)
F32 = jnp.float32
BF16 = jnp.bfloat16
ANY = pl.BlockSpec(memory_space=pl.ANY)
OWN_ROW, OTHER_ROW, OWN_POS, OTHER_POS, CORE_AT = 0, 16, 32, 48, 64


def nn(left, right):
    return lax.dot_general(left, right, (((1,), (0,)), ((), ())), preferred_element_type=F32)


def nt(left, right):
    return lax.dot_general(left, right, (((1,), (1,)), ((), ())), preferred_element_type=F32)


def tn(left, right):
    return lax.dot_general(left, right, (((0,), (0,)), ((), ())), preferred_element_type=F32)


def mean(values):
    return jnp.sum(values, axis=-1, keepdims=True) * (1.0 / D)


def normalize(values):
    center = values - mean(values)
    inverse = lax.rsqrt(mean(center * center) + EPS)
    return center * inverse, inverse


def norm_back(grad, normed, inverse):
    return inverse * (grad - mean(grad) - normed * mean(grad * normed))


def column_sum(values):
    return jnp.sum(values, axis=0, keepdims=True)


def piece_copies(tbl, refs, weight, sems, rows, parts):
    own_low, own_high, other_low, other_high = refs
    core = tbl[CORE_AT]
    copies = []
    for kind, (low, high) in enumerate(((own_low, own_high), (other_low, other_high))):
        half = core if kind == 0 else 1 - core
        for j in range(CHIPS):
            piece = (low if j < CHIPS // 2 else high).at[j % (CHIPS // 2)]
            at = pl.ds(pl.multiple_of(tbl[kind * CHIPS + j] * rows, rows), rows)
            for k, (start, width, base) in enumerate(parts):
                cols = pl.ds(pl.multiple_of(base + half * width, 128), width)
                copies.append(
                    pltpu.make_async_copy(piece.at[:, pl.ds(start, width)], weight.at[at, cols], sems.at[k, kind * CHIPS + j])
                )
    return copies


def lane_masks():
    lane = lax.broadcasted_iota(jnp.int32, (1, 2 * HEAD), 1)
    first = jnp.where(lane < HEAD, 1.0, 0.0)
    return first.astype(BF16), (1.0 - first).astype(BF16), lane < HEAD


def split_bf16(values):
    high = values.astype(BF16)
    rest = values - high.astype(F32)
    return high, rest.astype(BF16), rest


def project_kernel(
    tbl, x_ref, pick_ref, embed_ref, own_low, own_high, other_low, other_high,
    hidden_ref, low_ref, qkv_ref, vec_ref, w_ref, weight, sems, out_sem,
):
    step = pl.program_id(0)
    save = pltpu.make_async_copy(weight.at[:, pl.ds(0, 2 * QKV)], w_ref, out_sem.at[0])

    @pl.when(step == 0)
    def _():
        parts = ((0, QKV, 0), (QKV, TDIM, 2 * QKV))
        copies = piece_copies(tbl, (own_low, own_high, other_low, other_high), weight, sems, 48, parts)
        for copy in copies:
            copy.start()
        for copy in copies:
            copy.wait()
        save.start()
        vec_ref[...] = weight[:, 2 * QKV + TDIM :].astype(F32).T[:16, :]

    slots = nt(embed_ref[...], weight[:, 2 * QKV : 2 * QKV + TDIM]) + vec_ref[8:9, :]
    high, middle, rest = split_bf16(slots)
    low = (rest - middle.astype(F32)).astype(BF16)
    picks = pick_ref[...]
    slot = nn(jnp.concatenate([picks, picks, picks], axis=1), jnp.concatenate([high, middle, low], axis=0))
    hidden_ref[...] = x_ref[...].astype(F32) + slot
    low_ref[...] = hidden_ref[...].astype(BF16)

    def place(y, run):
        half, kind = divmod(run, 3)
        cols = slice(HALF * half, HALF * half + HALF)
        if kind == 0:
            y = (y + vec_ref[0:1, cols]).astype(BF16) * jnp.asarray(HEAD**-0.5, BF16)
        elif kind == 2:
            y = y + vec_ref[1:2, cols]
        qkv_ref[:, HALF * run : HALF * run + HALF] = y.astype(BF16)

    for chunk in range(3):
        y = nn(low_ref[...], weight[:, D * chunk : D * chunk + D])
        place(y[:, :HALF], 2 * chunk)
        place(y[:, HALF:], 2 * chunk + 1)

    @pl.when(step == pl.num_programs(0) - 1)
    def _():
        save.wait()


def attend_kernel(qkv_ref, segc_ref, segr_ref, *rest):
    mix_ref, probs_ref, bias, scores = rest[-4:]
    for t in range(4):
        same = segc_ref[WINDOWS[t] : WINDOWS[t] + 256, :] == segr_ref[0, :, 128 * t : 128 * t + 128]
        bias[t] = jnp.where(same, 0.0, NEG)
    first, second, _ = lane_masks()

    def operands(p, t):
        at = pl.multiple_of((p // 3) * QKV + (p % 3) * 128, 128)
        window = slice(WINDOWS[t], WINDOWS[t] + 256)
        return at, window

    def scores_of(p, t):
        at, window = operands(p, t)
        q = qkv_ref[128 * t : 128 * t + 128, pl.ds(at, 128)]
        k = qkv_ref[window, pl.ds(at + HALF, 128)]
        s = nt(k, jnp.concatenate([q * first, q * second], axis=0)) + jnp.concatenate([bias[t], bias[t]], axis=1)
        scores[t % 2] = s
        return jnp.max(s, axis=0, keepdims=True)

    def pair(p, peak):
        for t in range(4):
            ahead = scores_of(p, t + 1) if t < 3 else scores_of(jnp.minimum(p + 1, HEADS // 2 - 1), 0)
            at, window = operands(p, t)
            v = qkv_ref[window, pl.ds(at + 2 * HALF, 128)]
            e = jnp.exp(scores[t % 2] - peak)
            probs = (e * (1.0 / jnp.sum(e, axis=0, keepdims=True))).astype(BF16)
            probs_ref[0, p, t] = probs
            out = tn(v, probs)
            out = jnp.concatenate([out[:HEAD, :128], out[HEAD:, 128:]], axis=0)
            mix_ref[128 * t : 128 * t + 128, pl.ds(pl.multiple_of(p * 128, 128), 128)] = out.T.astype(BF16)
            peak = ahead
        return peak

    lax.fori_loop(0, HEADS // 2, pair, scores_of(0, 0))

def expand_kernel(
    tbl, hidden_ref, mix_ref, vec_ref, upb_ref, ua, ub, uc, ud,
    n1_ref, i1_ref, act_ref, slope_ref, mlow_ref, up_ref, up, wide, sems, out_sem,
):
    step = pl.program_id(0)
    save = pltpu.make_async_copy(up, up_ref, out_sem.at[0])

    @pl.when(step == 0)
    def _():
        copies = piece_copies(tbl, (ua, ub, uc, ud), up, sems, 48, ((0, FF // 2, 0), (FF // 2, HALF, FF)))
        for copy in copies:
            copy.start()
        for copy in copies:
            copy.wait()
        save.start()

    normed, inverse = normalize(hidden_ref[...] + nn(mix_ref[...], up[:, FF:]) + vec_ref[2:3, :])
    n1_ref[...] = normed
    i1_ref[...] = inverse
    mlow_ref[...] = (normed * vec_ref[3:4, :] + vec_ref[4:5, :]).astype(BF16)

    def expand(j):
        at = slice(j * D, j * D + D)
        wide[j % 2] = nn(mlow_ref[...], up[:, at]) + upb_ref[:, at]

    def activate(j):
        at = slice(j * D, j * D + D)
        u = wide[j % 2]
        scaled = u * SQRT_HALF
        twice = 1.0 + lax.erf(scaled)
        act_ref[:, at] = ((u * 0.5) * twice).astype(BF16)
        slope_ref[:, at] = (0.5 * twice + (u * INV_ROOT_TAU) * jnp.exp(-(scaled * scaled))).astype(BF16)

    expand(0)
    for j in range(FF // D):
        if j + 1 < FF // D:
            expand(j + 1)
        activate(j)

    @pl.when(step == pl.num_programs(0) - 1)
    def _():
        save.wait()


def contract_kernel(
    tbl, n1_ref, i1_ref, cot_ref, vec_ref, act_ref, slope_ref, up_ref, pick_ref, da, db, dc, dd,
    res_ref, dexp_ref, din_ref, df_ref, ain_ref, vg_ref, gup_ref, slot_ref, down, wide, sems,
):
    step = pl.program_id(0)

    @pl.when(step == 0)
    def _():
        copies = piece_copies(tbl, (da, db, dc, dd), down, sems, FF // CHIPS, ((0, HALF, 0),))
        for copy in copies:
            copy.start()
        for copy in copies:
            copy.wait()
        vg_ref[...] = jnp.zeros_like(vg_ref)
        gup_ref[...] = jnp.zeros_like(gup_ref)
        slot_ref[...] = jnp.zeros_like(slot_ref)

    def vec(i):
        return vec_ref[i : i + 1, :]

    second = n1_ref[...] * vec(3) + vec(4) + nn(act_ref[...], down[...]) + vec(5)
    normed2, inverse2 = normalize(second)
    res_ref[...] = (normed2 * vec(6) + vec(7)).astype(BF16)
    upstream = cot_ref[...].astype(F32)
    vg_ref[0:1, :] += column_sum(upstream * normed2)
    vg_ref[1:2, :] += column_sum(upstream)
    d_second = norm_back(upstream * vec(6), normed2, inverse2)
    down_in = d_second.astype(BF16)
    din_ref[...] = down_in
    vg_ref[2:3, :] += column_sum(down_in.astype(F32))

    def contract(j):
        wide[j % 2] = nt(din_ref[...], down[j * D : j * D + D, :])

    contract(0)
    for j in range(FF // D):
        if j + 1 < FF // D:
            contract(j + 1)
        at = slice(j * D, j * D + D)
        d_exp = (wide[j % 2] * slope_ref[:, at].astype(F32)).astype(BF16)
        dexp_ref[:, at] = d_exp
        gup_ref[:, at] += column_sum(d_exp.astype(F32))
    d_middle = nt(dexp_ref[...], up_ref[...]) + d_second
    normed1 = n1_ref[...]
    vg_ref[3:4, :] += column_sum(d_middle * normed1)
    vg_ref[4:5, :] += column_sum(d_middle)
    d_first = norm_back(d_middle * vec(3), normed1, i1_ref[...])
    df_ref[...] = d_first
    attn_in = d_first.astype(BF16)
    ain_ref[...] = attn_in
    vg_ref[5:6, :] += column_sum(attn_in.astype(F32))
    rest = (d_first - attn_in.astype(F32)).astype(BF16)
    slot_ref[...] += tn(pick_ref[...], attn_in) + tn(pick_ref[...], rest)


def down_grad_kernel(tbl, act_ref, din_ref, own, other, hold, sems):
    step = pl.program_id(0)
    core = tbl[CORE_AT]
    rows = FF // CHIPS
    hold[step] = tn(act_ref[...], din_ref[...]).astype(BF16)

    def copies(j):
        made = []
        for k in range(4):
            chip = 4 * j + k
            for kind, (target, table) in enumerate(((own, OWN_POS), (other, OTHER_POS))):
                half = core if kind == 0 else 1 - core
                src = hold.at[j, pl.ds(k * rows, rows), pl.ds(pl.multiple_of(half * HALF, HALF), HALF)]
                made.append(pltpu.make_async_copy(src, target.at[tbl[table + chip]], sems.at[j, 2 * k + kind]))
        return made

    for copy in copies(step):
        copy.start()

    @pl.when(step == pl.num_programs(0) - 1)
    def _():
        for j in range(4):
            for copy in copies(j):
                copy.wait()


def product_for(step, mlow_ref, dexp_ref, mix_ref, ain_ref, give):
    @pl.when(step < 2)
    def _():
        give(tn(mlow_ref[...], dexp_ref[...]), pl.ds(pl.multiple_of(step * D, D), D), D)

    @pl.when(step == 2)
    def _():
        give(tn(mix_ref[...], ain_ref[...]), pl.ds(2 * D, HALF), HALF)


def up_other_kernel(tbl, mlow_ref, dexp_ref, mix_ref, ain_ref, other, hold, sems):
    step = pl.program_id(0)

    def copies(j, width):
        made = []
        for chip in range(CHIPS):
            src = hold.at[j, pl.ds(48 * chip, 48), pl.ds(0, width)]
            cols = pl.ds(pl.multiple_of(j * D, D), width)
            made.append(pltpu.make_async_copy(src, other.at[tbl[OTHER_POS + chip], :, cols], sems.at[j, chip]))
        return made

    def give(grad, cols, width):
        hold[step, :, :width] = grad.astype(BF16)
        for copy in copies(step, width):
            copy.start()

    product_for(step, mlow_ref, dexp_ref, mix_ref, ain_ref, give)

    @pl.when(step == 2)
    def _():
        for j in range(3):
            for copy in copies(j, D if j < 2 else HALF):
                copy.wait()


def arrivals(tbl, got, came, rows, sems):
    made = []
    for chip in range(CHIPS):
        dst = came.at[pl.ds(rows * chip, rows), :]
        made.append(pltpu.make_async_copy(got.at[tbl[OWN_POS + chip]], dst, sems.at[chip]))
    return made


def leave(tbl, src, chip, keep, away, cols, sem, act):
    at = tbl[OWN_POS + chip]

    @pl.when(at < CHIPS // 2)
    def _():
        act(pltpu.make_async_copy(src, keep.at[at, :, cols], sem))

    @pl.when(at >= CHIPS // 2)
    def _():
        act(pltpu.make_async_copy(src, away.at[at - CHIPS // 2, :, cols], sem))


def start(copy):
    copy.start()


def wait(copy):
    copy.wait()


def up_own_kernel(tbl, mlow_ref, dexp_ref, mix_ref, ain_ref, got, keep, away, hold, came, sems, came_sems):
    step = pl.program_id(0)

    @pl.when(step == 0)
    def _():
        for copy in arrivals(tbl, got, came, 48, came_sems):
            copy.start()

    def each(j, width, act):
        for chip in range(CHIPS):
            src = hold.at[j, pl.ds(48 * chip, 48), pl.ds(0, width)]
            leave(tbl, src, chip, keep, away, pl.ds(pl.multiple_of(j * D, D), width), sems.at[j, chip], act)

    def give(grad, cols, width):
        hold[step, :, :width] = (grad + came[:, cols].astype(F32)).astype(BF16)
        each(step, width, start)

    @pl.when(step == 0)
    def _():
        for copy in arrivals(tbl, got, came, 48, came_sems):
            copy.wait()

    product_for(step, mlow_ref, dexp_ref, mix_ref, ain_ref, give)

    @pl.when(step == 2)
    def _():
        for j in range(3):
            each(j, D if j < 2 else HALF, wait)


def attention_backward_kernel(ain_ref, mix_ref, qkv_ref, probs_ref, w_ref, pick_ref, *rest):
    dqkv_ref, vg_ref, slot_ref, d_mix, delta, d_probs, dk, dv = rest[-8:]
    d_mix[...] = nt(ain_ref[...], w_ref[...]).astype(BF16)
    product = d_mix[...].astype(F32) * mix_ref[...].astype(F32)
    high, low, _ = split_bf16(product)
    head = lax.broadcasted_iota(jnp.int32, (16, D), 0)
    column = lax.broadcasted_iota(jnp.int32, (16, D), 1)
    ones = jnp.where(column // HEAD == head, 1.0, 0.0).astype(BF16)
    dots = nt(ones, high) + nt(ones, low)
    for p in range(HEADS // 2):
        for t in range(4):
            rows = slice(128 * t, 128 * t + 128)
            delta[p, t] = jnp.concatenate([dots[2 * p : 2 * p + 1, rows], dots[2 * p + 1 : 2 * p + 2, rows]], axis=1)
    first, second, choose = lane_masks()

    def offsets(p):
        return pl.multiple_of((p // 3) * QKV + (p % 3) * 128, 128)

    def outs_of(p, t):
        do = d_mix[128 * t : 128 * t + 128, pl.ds(pl.multiple_of(p * 128, 128), 128)]
        return jnp.concatenate([do * first, do * second], axis=0)

    def d_probs_of(p, t):
        v = qkv_ref[WINDOWS[t] : WINDOWS[t] + 256, pl.ds(offsets(p) + 2 * HALF, 128)]
        d_probs[t % 2] = nt(v, outs_of(p, t))

    def pair(p, carry):
        at = offsets(p)
        dk[...] = jnp.zeros_like(dk)
        dv[...] = jnp.zeros_like(dv)
        for t in range(4):
            if t < 3:
                d_probs_of(p, t + 1)
            else:
                d_probs_of(jnp.minimum(p + 1, HEADS // 2 - 1), 0)
            window = slice(WINDOWS[t], WINDOWS[t] + 256)
            q = qkv_ref[128 * t : 128 * t + 128, pl.ds(at, 128)]
            k = qkv_ref[window, pl.ds(at + HALF, 128)]
            queries = jnp.concatenate([q * first, q * second], axis=0)
            probs = probs_ref[0, p, t]
            dv[window, :] += nn(probs, outs_of(p, t))
            scores = (probs.astype(F32) * (d_probs[t % 2] - delta[p, t])).astype(BF16)
            dk[window, :] += nn(scores, queries)
            dq = tn(scores, k) * HEAD**-0.5
            dqkv_ref[128 * t : 128 * t + 128, pl.ds(at, 128)] = jnp.where(choose, dq[:128], dq[128:]).astype(BF16)
        dqkv_ref[:, pl.ds(at + HALF, 128)] = dk[...].astype(BF16)
        dqkv_ref[:, pl.ds(at + 2 * HALF, 128)] = dv[...].astype(BF16)
        return carry

    d_probs_of(0, 0)
    lax.fori_loop(0, HEADS // 2, pair, 0)
    for h in range(2):
        cols = slice(HALF * h, HALF * h + HALF)
        for row, shift in ((0, 0), (1, 2 * HALF)):
            part = dqkv_ref[:, QKV * h + shift : QKV * h + shift + HALF]
            vg_ref[row : row + 1, cols] = column_sum(part.astype(F32))
    slot_ref[...] = tn(pick_ref[...], dqkv_ref[...])


def small_grads(first_ref, second_ref, w_ref, embed_ref, ff_ref, va_ref, vb_ref, up_ref):
    high, low, _ = split_bf16(second_ref[...])
    slots = first_ref[...] + nt(high, w_ref[...]) + nt(low, w_ref[...])
    slot_low = slots.astype(BF16)
    rows = [column_sum(slot_low.astype(F32)), va_ref[0:2, :] + vb_ref[0:2, :], ff_ref[0:6, :], up_ref[0:4, :]]
    rows.append(jnp.zeros((TDIM - 13, D), F32))
    vectors = jnp.concatenate(rows, axis=0).T
    return jnp.concatenate([tn(slot_low, embed_ref[...]), vectors], axis=1).astype(BF16)


def qkv_other_kernel(
    tbl, low_ref, dqkv_ref, first_ref, second_ref, w_ref, embed_ref, ff_ref, va_ref, vb_ref, up_ref,
    small_ref, other, hold, extra, sems, small_sems,
):
    step = pl.program_id(0)
    off = 1 - tbl[CORE_AT]

    def small_copies():
        made = []
        for chip in range(CHIPS):
            src = extra.at[pl.ds(48 * chip, 48), pl.ds(pl.multiple_of(off * TDIM, TDIM), TDIM)]
            dst = other.at[tbl[OTHER_POS + chip], :, pl.ds(QKV, TDIM)]
            made.append(pltpu.make_async_copy(src, dst, small_sems.at[chip]))
        return made

    @pl.when(step == 0)
    def _():
        small = small_grads(first_ref, second_ref, w_ref, embed_ref, ff_ref, va_ref, vb_ref, up_ref)
        small_ref[...] = small
        extra[...] = small
        for copy in small_copies():
            copy.start()

    hold[step] = tn(low_ref[...], dqkv_ref[...]).astype(BF16)

    def copies(j):
        made = []
        for k in range(CHIPS // 2):
            src = hold.at[j, pl.ds(48 * k, 48), :]
            at = tbl[OTHER_POS + j * (CHIPS // 2) + k]
            made.append(pltpu.make_async_copy(src, other.at[at, :, pl.ds(0, QKV)], sems.at[j, k]))
        return made

    for copy in copies(step):
        copy.start()

    @pl.when(step == 1)
    def _():
        for j in range(2):
            for copy in copies(j):
                copy.wait()
        for copy in small_copies():
            copy.wait()


def qkv_own_kernel(tbl, low_ref, dqkv_ref, small_ref, got, keep, away, hold, came, sems, came_sems):
    step = pl.program_id(0)

    @pl.when(step == 0)
    def _():
        for copy in arrivals(tbl, got, came, 48, came_sems):
            copy.start()
        for copy in arrivals(tbl, got, came, 48, came_sems):
            copy.wait()

    rows = pl.ds(pl.multiple_of(step * HALF, HALF), HALF)
    cols = pl.ds(pl.multiple_of(tbl[CORE_AT] * TDIM, TDIM), TDIM)
    hold[step, :, :QKV] = (tn(low_ref[...], dqkv_ref[...]) + came[rows, :QKV].astype(F32)).astype(BF16)
    hold[step, :, QKV:] = (small_ref[rows, cols].astype(F32) + came[rows, QKV:].astype(F32)).astype(BF16)

    def each(j, act):
        for k in range(CHIPS // 2):
            src = hold.at[j, pl.ds(48 * k, 48), :]
            leave(tbl, src, j * (CHIPS // 2) + k, keep, away, pl.ds(0, QKV + TDIM), sems.at[j, k], act)

    each(step, start)

    @pl.when(step == 1)
    def _():
        for j in range(2):
            each(j, wait)


def input_grad_kernel(df_ref, dqkv_ref, w_ref, ig_ref):
    ig_ref[...] = df_ref[...] + nt(dqkv_ref[...], w_ref[...])


def call(kernel, name, grid, in_specs, out_specs, out_shape, scratch, flops, moved, args, prefetch=1, alias=None):
    return pl.pallas_call(
        kernel,
        name=name,
        grid_spec=pltpu.PrefetchScalarGridSpec(
            num_scalar_prefetch=prefetch, grid=grid, in_specs=in_specs, out_specs=out_specs, scratch_shapes=scratch
        ),
        out_shape=out_shape,
        input_output_aliases=alias or {},
        compiler_params=pltpu.CompilerParams(dimension_semantics=("arbitrary",) * len(grid), vmem_limit_bytes=63 << 20),
        cost_estimate=pl.CostEstimate(flops=flops, bytes_accessed=moved, transcendentals=0),
    )(*args)


def rows_spec(rows, cols):
    return pl.BlockSpec((rows, cols), lambda i, *_: (i, 0))


def whole_spec(shape):
    return pl.BlockSpec(shape, lambda i, *_: (0,) * len(shape))


def cols_spec(rows, cols, top):
    return pl.BlockSpec((rows, cols), lambda i, *_: (0, jnp.minimum(i, top)))


def sds(shape, dtype):
    return jax.ShapeDtypeStruct(shape, dtype)


def block_spec(shape, block):
    return pl.BlockSpec(shape, lambda i, *_: (block,) + (0,) * (len(shape) - 1))


def project(tbl, x, pick, embed, pieces):
    rows = x.shape[0]
    slots = pick.shape[1]
    return call(
        project_kernel, "project", (rows // BLOCK,),
        [rows_spec(BLOCK, D), rows_spec(BLOCK, slots), whole_spec((slots, TDIM))] + [ANY] * 4,
        [rows_spec(BLOCK, D), rows_spec(BLOCK, D), rows_spec(BLOCK, 2 * QKV), whole_spec((16, D)), ANY],
        [sds((rows, D), F32), sds((rows, D), BF16), sds((rows, 2 * QKV), BF16), sds((16, D), F32), sds((D, 2 * QKV), BF16)],
        [pltpu.VMEM((D, 2 * QKV + 2 * TDIM), BF16), pltpu.SemaphoreType.DMA((2, 32)), pltpu.SemaphoreType.DMA((1,))],
        6 * rows * D * D, 20 << 20, (tbl, x, pick, embed, *pieces),
    )


def attend(block, qkv, segc, segr, before):
    rows = qkv.shape[0]
    return call(
        attend_kernel, "attend", (1,),
        [block_spec((BLOCK, 2 * QKV), block), block_spec((BLOCK, 1), block), block_spec((1, 1, BLOCK), block)]
        + [ANY] * len(before),
        [block_spec((BLOCK, D), block), block_spec((1, HEADS // 2, 4, 256, 256), block)],
        [sds((rows, D), BF16), sds((rows // BLOCK, HEADS // 2, 4, 256, 256), BF16)],
        [pltpu.VMEM((4, 256, 128), F32), pltpu.VMEM((2, 256, 256), F32)],
        4 * BLOCK * D * D, 20 << 20, (qkv, segc, segr, *before), prefetch=0,
        alias={3 + i: i for i in range(len(before))},
    )


def expand(tbl, hidden, mix, vec, upb, up):
    rows = mix.shape[0]
    tile = 256
    return call(
        expand_kernel, "expand", (rows // tile,),
        [rows_spec(tile, D), rows_spec(tile, D), whole_spec((16, D)), whole_spec((1, FF))] + [ANY] * 4,
        [rows_spec(tile, D), rows_spec(tile, 1), rows_spec(tile, FF), rows_spec(tile, FF), rows_spec(tile, D), ANY],
        [sds((rows, D), F32), sds((rows, 1), F32), sds((rows, FF), BF16), sds((rows, FF), BF16), sds((rows, D), BF16),
         sds((D, FF + D), BF16)],
        [pltpu.VMEM((D, FF + D), BF16), pltpu.VMEM((2, tile, D), F32), pltpu.SemaphoreType.DMA((2, 32)),
         pltpu.SemaphoreType.DMA((1,))],
        2 * rows * D * (FF + D), 20 << 20, (tbl, hidden, mix, vec, upb, *up),
    )


def contract(tbl, n1, i1, cot, vec, act, slope, up, pick, down):
    rows = n1.shape[0]
    tile = 256
    slots = pick.shape[1]
    return call(
        contract_kernel, "contract", (rows // tile,),
        [rows_spec(tile, D), rows_spec(tile, 1), rows_spec(tile, D), whole_spec((16, D)), rows_spec(tile, FF),
         rows_spec(tile, FF), whole_spec((D, FF)), rows_spec(tile, slots)] + [ANY] * 4,
        [rows_spec(tile, D), rows_spec(tile, FF), rows_spec(tile, D), rows_spec(tile, D), rows_spec(tile, D),
         whole_spec((8, D)), whole_spec((1, FF)), whole_spec((slots, D))],
        [sds((rows, D), BF16), sds((rows, FF), BF16), sds((rows, D), BF16), sds((rows, D), F32), sds((rows, D), BF16),
         sds((8, D), F32), sds((1, FF), F32), sds((slots, D), F32)],
        [pltpu.VMEM((FF, D), BF16), pltpu.VMEM((2, tile, D), F32), pltpu.SemaphoreType.DMA((1, 32))],
        6 * rows * D * FF, 20 << 20, (tbl, n1, i1, cot, vec, act, slope, up, pick, *down),
    )


def down_grad(tbl, act, din):
    rows = act.shape[0]
    shape = sds((CHIPS, FF // CHIPS, HALF), BF16)
    return call(
        down_grad_kernel, "down_grad", (4,), [cols_spec(rows, D, 3), whole_spec((rows, D))], [ANY, ANY], [shape, shape],
        [pltpu.VMEM((4, D, D), BF16), pltpu.SemaphoreType.DMA((4, 8))],
        2 * rows * D * FF, 20 << 20, (tbl, act, din),
    )


def up_specs(rows, kind):
    def half(tbl):
        return jnp.where(kind == 0, tbl[CORE_AT], 1 - tbl[CORE_AT])

    return [whole_spec((rows, D)), pl.BlockSpec((rows, D), lambda i, tbl: (0, 2 * half(tbl) + jnp.minimum(i, 1))),
            whole_spec((rows, D)), pl.BlockSpec((rows, HALF), lambda i, tbl: (0, half(tbl)))]


def up_other(tbl, mlow, dexp, mix, ain):
    rows = mlow.shape[0]
    return call(
        up_other_kernel, "up_other", (3,), up_specs(rows, 1), ANY, sds((CHIPS, 48, 2 * D + HALF), BF16),
        [pltpu.VMEM((3, D, D), BF16), pltpu.SemaphoreType.DMA((3, CHIPS))],
        rows * D * (FF + D), 20 << 20, (tbl, mlow, dexp, mix, ain),
    )


def up_own(tbl, mlow, dexp, mix, ain, got):
    rows = mlow.shape[0]
    shape = sds((CHIPS // 2, 48, 2 * D + HALF), BF16)
    return call(
        up_own_kernel, "up_own", (3,), up_specs(rows, 0) + [ANY], [ANY, ANY], [shape, shape],
        [pltpu.VMEM((3, D, D), BF16), pltpu.VMEM((D, 2 * D + HALF), BF16), pltpu.SemaphoreType.DMA((3, CHIPS)),
         pltpu.SemaphoreType.DMA((CHIPS,))],
        rows * D * (FF + D), 20 << 20, (tbl, mlow, dexp, mix, ain, got),
    )


def qkv_specs(rows, kind):
    def half(tbl):
        return jnp.where(kind == 0, tbl[CORE_AT], 1 - tbl[CORE_AT])

    return [pl.BlockSpec((rows, HALF), lambda i, tbl: (0, i)), pl.BlockSpec((rows, QKV), lambda i, tbl: (0, half(tbl)))]


def qkv_other(tbl, low, dqkv, first, second, weight, embed, ff, va, vb, up):
    rows = low.shape[0]
    slots = first.shape[0]
    return call(
        qkv_other_kernel, "qkv_other", (2,),
        qkv_specs(rows, 1) + [whole_spec((slots, D)), whole_spec((slots, 2 * QKV)), whole_spec((D, 2 * QKV)),
                              whole_spec((slots, TDIM)), whole_spec((8, D)), whole_spec((8, D)), whole_spec((8, D)),
                              whole_spec((4, D))],
        [whole_spec((D, 2 * TDIM)), ANY], [sds((D, 2 * TDIM), BF16), sds((CHIPS, 48, QKV + TDIM), BF16)],
        [pltpu.VMEM((2, HALF, QKV), BF16), pltpu.VMEM((D, 2 * TDIM), BF16), pltpu.SemaphoreType.DMA((2, CHIPS // 2)),
         pltpu.SemaphoreType.DMA((CHIPS,))],
        3 * rows * D * D, 20 << 20, (tbl, low, dqkv, first, second, weight, embed, ff, va, vb, up),
    )


def qkv_own(tbl, low, dqkv, small, got):
    rows = low.shape[0]
    shape = sds((CHIPS // 2, 48, QKV + TDIM), BF16)
    return call(
        qkv_own_kernel, "qkv_own", (2,), qkv_specs(rows, 0) + [whole_spec((D, 2 * TDIM)), ANY], [ANY, ANY], [shape, shape],
        [pltpu.VMEM((2, HALF, QKV + TDIM), BF16), pltpu.VMEM((D, QKV + TDIM), BF16),
         pltpu.SemaphoreType.DMA((2, CHIPS // 2)), pltpu.SemaphoreType.DMA((CHIPS,))],
        3 * rows * D * D, 20 << 20, (tbl, low, dqkv, small, got),
    )


def attention_backward(block, ain, mix, qkv, probs, weight, pick, before):
    rows = ain.shape[0]
    slots = pick.shape[1]
    return call(
        attention_backward_kernel, "attention_backward", (1,),
        [block_spec((BLOCK, D), block), block_spec((BLOCK, D), block), block_spec((BLOCK, 2 * QKV), block),
         block_spec((1, HEADS // 2, 4, 256, 256), block), pl.BlockSpec((D, D), lambda i, *_: (0, 4)),
         block_spec((BLOCK, slots), block)] + [ANY] * len(before),
        [block_spec((BLOCK, 2 * QKV), block), whole_spec((8, D)), whole_spec((slots, 2 * QKV))],
        [sds((rows, 2 * QKV), BF16), sds((8, D), F32), sds((slots, 2 * QKV), F32)],
        [pltpu.VMEM((BLOCK, D), BF16), pltpu.VMEM((HEADS // 2, 4, 1, 256), F32), pltpu.VMEM((2, 256, 256), F32),
         pltpu.VMEM((BLOCK, 128), F32), pltpu.VMEM((BLOCK, 128), F32)],
        4 * BLOCK * D * D, 20 << 20, (ain, mix, qkv, probs, weight, pick, *before), prefetch=0,
        alias={6 + i: i for i in range(len(before))},
    )


def input_gradient(df, dqkv, weight):
    rows = df.shape[0]
    tile = 256
    return call(
        input_grad_kernel, "input_grad", (rows // tile,),
        [rows_spec(tile, D), rows_spec(tile, 2 * QKV), whole_spec((D, 2 * QKV))], rows_spec(tile, D), sds((rows, D), F32), [],
        6 * rows * D * D, 20 << 20, (df, dqkv, weight), prefetch=0,
    )


def flip(n, even_bit, odd_bit):
    return [(i, i ^ (odd_bit if i & 1 else even_bit)) for i in range(n)]


def tiled_route(n):
    return {"core": flip(n, 1, 1), "z2": flip(n, 16, 16), "z1": flip(n, 8, 8), "a": flip(n, 2, 4), "b": flip(n, 4, 2)}


def tables(n):
    me = lax.axis_index("fsdp")
    core = me % 2
    chips = jnp.arange(CHIPS, dtype=jnp.int32)
    if n == 32:
        here = me // 2

        def order(kind):
            low, high = jnp.where(kind == 0, 1, 2), jnp.where(kind == 0, 2, 1)
            bits = (chips & 1) * 8 + ((chips >> 1) & 1) * 4 + ((chips >> 2) & 1) * low + (chips >> 3) * high
            return here ^ bits

        def place(kind):
            diff = here ^ chips
            x, y = diff & 1, (diff >> 1) & 1
            low, high = jnp.where(kind == 0, x, y), jnp.where(kind == 0, y, x)
            return (diff >> 3) + ((diff >> 2) & 1) * 2 + low * 4 + high * 8

        parts = [order(core), order(1 - core), place(core), place(1 - core)]
    else:
        parts = [chips] * 4
    return jnp.concatenate(parts + [jnp.full((16,), core, jnp.int32)]).astype(jnp.int32)


def own_half(halves, core):
    return jnp.where(core == 0, halves[0], halves[1]), jnp.where(core == 0, halves[1], halves[0])


def tie(*values):
    return lax.optimization_barrier(values)


def follow(first, *values):
    return lax.optimization_barrier((first,) + values)[1:]


def send_on(value, step, n):
    return lax.ppermute(value, "fsdp", perm=tiled_route(n)[step])


def chip_shards(halves_of_groups, n):
    core = lax.axis_index("fsdp") % 2
    mine, theirs = own_half(
        [jnp.concatenate([halves[h].reshape(-1, HALF) for halves in halves_of_groups], axis=0) for h in range(2)], core
    )
    got = send_on(theirs, "core", n)
    first, second = own_half((mine, got), core)
    shards, at = [], 0
    for halves in halves_of_groups:
        rows, cols = halves[0].shape
        count = rows * cols // HALF
        parts = [item[at : at + count].reshape(rows, cols) for item in (first, second)]
        shards.append(jnp.concatenate(parts, axis=0)[None])
        at += count
    return shards


def whole_gather(halves, core):
    full = [lax.all_gather(half, "fsdp", axis=0, tiled=True) for half in halves]
    full = [item.reshape(CHIPS, -1, item.shape[1]) for item in full]
    own, other = own_half(full, core)
    middle = CHIPS // 2
    return own[:middle], own[middle:], other[:middle], other[middle:]


def widen(held, step, n):
    return jnp.concatenate([held, send_on(held, step, n)], axis=0)


def add(left, right):
    return (left.astype(F32) + right.astype(F32)).astype(BF16)


def halve(keep, got):
    middle = keep.shape[0] // 2
    return add(keep[:middle], got[:middle]), add(keep[middle:], got[middle:])


def finish(keep, got, n):
    core = lax.axis_index("fsdp") % 2
    total = keep[0].astype(F32) + got[0].astype(F32)
    rows = total.shape[0] // 2
    mine, theirs = own_half((total[:rows], total[rows:]), core)
    got = send_on(theirs.astype(BF16), "core", n).astype(F32)
    return own_half((mine, got), core)


def whole_reduce(own, other, core):
    sums = []
    for item in own_half((own, other), core):
        item = item.reshape(-1, item.shape[2])
        sums.append(lax.psum_scatter(item, "fsdp", scatter_dimension=0, tiled=True).astype(F32))
    return sums


def sinusoid(steps):
    half = TDIM // 2
    freqs = jnp.exp(-math.log(10000.0) * jnp.arange(half, dtype=F32) / half)
    angles = steps.astype(F32)[:, None] * freqs[None, :]
    return jnp.concatenate([jnp.cos(angles), jnp.sin(angles)], axis=1)


def body(
    inputs, cotangent, lengths, timesteps, time_weight, time_bias, query_weight, query_bias, key_weight,
    value_weight, value_bias, out_weight, out_bias, mid_gain, mid_shift, up_weight, up_bias, down_weight,
    down_bias, last_gain, last_shift,
):
    n = lax.axis_size("fsdp")
    rows = inputs.shape[0]
    blocks = rows // BLOCK
    tbl = tables(n)
    shard = D // n

    vectors = [query_bias, value_bias, out_bias, mid_gain, mid_shift, down_bias, last_gain, last_shift, time_bias]
    vectors += [up_bias[shard * k : shard * (k + 1)] for k in range(FF // D)]
    lane = lax.broadcasted_iota(jnp.int32, (shard, TDIM), 1)
    columns = jnp.zeros((shard, TDIM), F32)
    for k, item in enumerate(vectors):
        columns = jnp.where(lane == k, item.astype(F32)[:, None], columns)
    columns = columns.astype(BF16)
    small_halves = [time_weight.T, columns]
    attn_halves = [
        jnp.concatenate(
            [w[:, HALF * h : HALF * h + HALF] for w in (query_weight, key_weight, value_weight)] + [small_halves[h]], axis=1
        )
        for h in range(2)
    ]
    up_halves = [
        jnp.concatenate([up_weight[:, FF // 2 * h : FF // 2 * (h + 1)], out_weight[:, HALF * h : HALF * h + HALF]], axis=1)
        for h in range(2)
    ]
    down_halves = [down_weight[:, :HALF], down_weight[:, HALF:]]

    ends = jnp.cumsum(lengths, axis=1)
    position = jnp.arange(BLOCK, dtype=jnp.int32)
    owner = jnp.sum((position[None, :, None] >= ends[:, None, :]).astype(jnp.int32), axis=2)
    pick = (owner[:, :, None] == jnp.arange(SLOTS, dtype=jnp.int32)).astype(BF16)
    pick = (pick[:, :, None, :] * jnp.eye(blocks, dtype=BF16)[:, None, :, None]).reshape(rows, blocks * SLOTS)
    segc = owner.reshape(rows, 1)
    segr = owner.reshape(blocks, 1, BLOCK)
    embed_in = sinusoid(timesteps.reshape(-1)).astype(BF16)
    core = lax.axis_index("fsdp") % 2
    tiled = n == 32

    if tiled:
        a0, u0, d0 = chip_shards((attn_halves, up_halves, down_halves), n)
        a0 = widen(a0, "z2", n)
        a0 = widen(a0, "z1", n)
        (u0,) = follow(a0, u0)
        a0 = widen(a0, "a", n)
        u0 = widen(u0, "z2", n)
        a0, u0 = tie(a0, u0)
        a1 = send_on(a0, "b", n)
        a2 = send_on(a0, "core", n)
        u0 = widen(u0, "z1", n)
        a1, u0, d0 = tie(a1, u0, d0)
        a3 = send_on(a1, "core", n)
        u_got = send_on(u0, "a", n)
        d_got = send_on(d0, "z2", n)
        hidden, low, qkv, vec, weight = project(tbl, inputs, pick, embed_in, (a0, a1, a2, a3))
        qkv, u0, u_got, d0, d_got = tie(qkv, u0, u_got, d0, d_got)
        u0 = jnp.concatenate([u0, u_got], axis=0)
        d0 = jnp.concatenate([d0, d_got], axis=0)
        u1 = send_on(u0, "b", n)
        d_got = send_on(d0, "z1", n)
        u2 = send_on(u0, "core", n)
        parts = attend(0, qkv, segc, segr, ())
        *parts, qkv, u0, u2, d0, d_got = tie(*parts, qkv, u0, u2, d0, d_got)
        d0 = jnp.concatenate([d0, d_got], axis=0)
        d_got = send_on(d0, "a", n)
        mix, probs = attend(1, qkv, segc, segr, parts)
        mix, u1, d0, d_got = tie(mix, u1, d0, d_got)
        u3 = send_on(u1, "core", n)
        d0 = jnp.concatenate([d0, d_got], axis=0)
        d1 = send_on(d0, "b", n)
        d2 = send_on(d0, "core", n)
        up_offset = vec[9:13].reshape(FF // D, n, shard).transpose(1, 0, 2).reshape(1, FF)
        n1, i1, act, slope, mlow, up_full = expand(tbl, hidden, mix, vec, up_offset, (u0, u1, u2, u3))
        act, d1 = tie(act, d1)
        d3 = send_on(d1, "core", n)
        down_pieces = (d0, d1, d2, d3)
    else:
        hidden, low, qkv, vec, weight = project(tbl, inputs, pick, embed_in, whole_gather(attn_halves, core))
        mix, probs = attend(1, qkv, segc, segr, attend(0, qkv, segc, segr, ()))
        up_offset = vec[9:13].reshape(FF // D, n, shard).transpose(1, 0, 2).reshape(1, FF)
        n1, i1, act, slope, mlow, up_full = expand(tbl, hidden, mix, vec, up_offset, whole_gather(up_halves, core))
        down_pieces = whole_gather(down_halves, core)

    res, dexp, din, df, ain, ff_vecs, up_vec, slot_first = contract(
        tbl, n1, i1, cotangent, vec, act, slope, up_full, pick, down_pieces
    )
    up_vec = up_vec.reshape(n, FF // D, shard).transpose(1, 0, 2).reshape(FF // D, D)
    d_own, d_other = down_grad(tbl, act, din)
    mlow, d_own, d_other = tie(mlow, d_own, d_other)
    u_other = up_other(tbl, mlow, dexp, mix, ain)
    if tiled:
        d_got = send_on(d_other, "core", n)
        u_other, d_own, d_got, mlow = tie(u_other, d_own, d_got, mlow)
        u_got = send_on(u_other, "core", n)
        d_keep, d_away = halve(d_own, d_got)
        d_keep, d_away, u_got = tie(d_keep, d_away, u_got)
        d_got = send_on(d_away, "b", n)
        u_keep, u_away = up_own(tbl, mlow, dexp, mix, ain, u_got)
        ain, u_keep, u_away = tie(ain, u_keep, u_away)
        u_got = send_on(u_away, "b", n)
        dqkv, vg0, slot0 = attention_backward(0, ain, mix, qkv, probs, up_full, pick, ())
        dqkv, d_keep, d_got = tie(dqkv, d_keep, d_got)
        d_keep, d_away = halve(d_keep, d_got)
        ain, dqkv, d_keep, d_away = tie(ain, dqkv, d_keep, d_away)
        d_got = send_on(d_away, "a", n)
        dqkv, vg1, slot1 = attention_backward(1, ain, mix, qkv, probs, up_full, pick, (dqkv,))
        dqkv, d_keep, d_got, u_keep, u_got = tie(dqkv, d_keep, d_got, u_keep, u_got)
        u_keep, u_away = halve(u_keep, u_got)
        d_keep, d_away = halve(d_keep, d_got)
        low, dqkv, d_keep, d_away, u_keep, u_away = tie(low, dqkv, d_keep, d_away, u_keep, u_away)
        u_got = send_on(u_away, "a", n)
        d_got = send_on(d_away, "z1", n)
        small, q_other = qkv_other(
            tbl, low, dqkv, slot_first, slot0 + slot1, weight, embed_in, ff_vecs, vg0, vg1, up_vec
        )
        q_other, u_keep, u_got, d_keep, d_got, low = tie(q_other, u_keep, u_got, d_keep, d_got, low)
        q_got = send_on(q_other, "core", n)
        u_keep, u_away = halve(u_keep, u_got)
        d_keep, d_away = halve(d_keep, d_got)
        q_got, u_keep, u_away, d_keep, d_away = tie(q_got, u_keep, u_away, d_keep, d_away)
        u_got = send_on(u_away, "z1", n)
        q_keep, q_away = qkv_own(tbl, low, dqkv, small, q_got)
        df, q_keep, q_away, u_keep, u_got = tie(df, q_keep, q_away, u_keep, u_got)
        q_got = send_on(q_away, "b", n)
        u_keep, u_away = halve(u_keep, u_got)
        df, d_away, u_keep, u_away = tie(df, d_away, u_keep, u_away)
        d_got = send_on(d_away, "z2", n)
        u_got = send_on(u_away, "z2", n)
        input_grad = input_gradient(df, dqkv, weight)
        input_grad, q_keep, q_got = tie(input_grad, q_keep, q_got)
        q_keep, q_away = halve(q_keep, q_got)
        u_keep, u_got, d_keep, d_got = follow(q_away, u_keep, u_got, d_keep, d_got)
        q_got = send_on(q_away, "a", n)
        down_sum = finish(d_keep, d_got, n)
        q_keep, q_away = halve(q_keep, q_got)
        q_got = send_on(q_away, "z1", n)
        up_sum = finish(u_keep, u_got, n)
        q_keep, q_away = halve(q_keep, q_got)
        q_got = send_on(q_away, "z2", n)
        qkv_sum = finish(q_keep, q_got, n)
    else:
        dqkv, vg0, slot0 = attention_backward(0, ain, mix, qkv, probs, up_full, pick, ())
        dqkv, vg1, slot1 = attention_backward(1, ain, mix, qkv, probs, up_full, pick, (dqkv,))
        small, q_other = qkv_other(
            tbl, low, dqkv, slot_first, slot0 + slot1, weight, embed_in, ff_vecs, vg0, vg1, up_vec
        )
        input_grad = input_gradient(df, dqkv, weight)
        down_sum = whole_reduce(d_own, d_other, core)
        zero_u, zero_q = jnp.zeros_like(u_other), jnp.zeros_like(q_other)
        u_own = jnp.concatenate(up_own(tbl, mlow, dexp, mix, ain, zero_u), axis=0)
        q_own = jnp.concatenate(qkv_own(tbl, low, dqkv, small, zero_q), axis=0)
        up_sum = whole_reduce(u_own, u_other, core)
        qkv_sum = whole_reduce(q_own, q_other, core)
    def both(pair, start, stop):
        return jnp.concatenate([half[:, start:stop] for half in pair], axis=1)

    out_query = both(qkv_sum, 0, HALF)
    out_key = both(qkv_sum, HALF, 2 * HALF)
    out_value = both(qkv_sum, 2 * HALF, QKV)
    out_up = both(up_sum, 0, 2 * D)
    out_out = both(up_sum, 2 * D, 2 * D + HALF)
    out_down = both(down_sum, 0, HALF)
    out_time = qkv_sum[0][:, QKV:].T
    v = qkv_sum[1][:, QKV : QKV + 13].T
    v_up = v[9:13].reshape(-1)
    return (
        res, input_grad, out_time, out_query, out_key, out_value, out_out, out_up, out_down,
        v[0], v[1], v[2], v[8], v[6], v[7], v_up, v[5], v[3], v[4],
    )


def solution(mesh):
    row, col, vec = P("fsdp", None), P(None, "fsdp"), P("fsdp")
    in_specs = (
        row, row, row, row, col, vec, row, vec, row, row, vec, row, vec, vec, vec, row, vec, row, vec, vec, vec,
    )
    out_specs = (row, row, col, row, row, row, row, row, row) + (vec,) * 10
    return jax.shard_map(body, mesh=mesh, in_specs=in_specs, out_specs=out_specs, check_vma=False)
```

profile of v0, /device:TPU:0, one launch (start us, length us, event | category | flops | bytes accessed | tf_op | source)
XLA Modules:
  0.0 312.1 jit_solution(13583090389995943122)
XLA Ops:
  9.0 4.0 %collective-permute-start.1 = (bf16[1,48,1280]{2,1,0:T(8,128)(2,1)S(1)}, bf16[1,48,1280]{2,1,0:T(8,128)(2,1)S(1)}, u32[]{:S(2)}, u32[]{:S(2)}) collective-permute-start(bf16[1,48,1280]{2,1,0:T(8,128)(2,1)S(1)} %maximum_bitcast_fusion.2), channel_id=1, source_target_pairs={{0,16},{1,17},{2,18},{3,19},{4,20},{5,21},{6,22},{7,23},{8,24},{9,... | collective-permute-start | bytes 368648 | tf_op jit(solution)/shard_map/ppermute | solution.py:773
  13.0 6.3 %collective-permute-done.1 = bf16[1,48,1280]{2,1,0:T(8,128)(2,1)S(1)} collective-permute-done((bf16[1,48,1280]{2,1,0:T(8,128)(2,1)S(1)}, bf16[1,48,1280]{2,1,0:T(8,128)(2,1)S(1)}, u32[]{:S(2)}, u32[]{:S(2)}) %collective-permute-start.1) | collective-permute-done | bytes 122912 | tf_op jit(solution)/shard_map/ppermute | solution.py:773
  20.3 6.6 %collective-permute-done.2 = bf16[2,48,1280]{2,1,0:T(8,128)(2,1)S(1)} collective-permute-done((bf16[2,48,1280]{2,1,0:T(8,128)(2,1)S(1)}, bf16[2,48,1280]{2,1,0:T(8,128)(2,1)S(1)}, u32[]{:S(2)}, u32[]{:S(2)}) %collective-permute-start.2) | collective-permute-done | bytes 245792 | tf_op jit(solution)/shard_map/ppermute | solution.py:773
  28.2 3.1 collective-permute-start.4
  31.3 8.0 %collective-permute-done.4 = bf16[1,48,1920]{2,1,0:T(8,128)(2,1)S(1)} collective-permute-done((bf16[1,48,1920]{2,1,0:T(8,128)(2,1)S(1)}, bf16[1,48,1920]{2,1,0:T(8,128)(2,1)S(1)}, u32[]{:S(2)}, u32[]{:S(2)}) %collective-permute-start.4) | collective-permute-done | bytes 184352 | tf_op jit(solution)/shard_map/ppermute | solution.py:773
  41.7 9.6 %collective-permute-done.6 = bf16[2,48,1920]{2,1,0:T(8,128)(2,1)} collective-permute-done((bf16[2,48,1920]{2,1,0:T(8,128)(2,1)S(1)}, bf16[2,48,1920]{2,1,0:T(8,128)(2,1)}, u32[]{:S(2)}, u32[]{:S(2)}) %collective-permute-start.6) | collective-permute-done | bytes 368672 | tf_op jit(solution)/shard_map/ppermute | solution.py:773
  58.2 11.6 %project.1 = (f32[1024,768]{1,0:T(8,128)}, bf16[1024,768]{1,0:T(8,128)(2,1)}, bf16[1024,2304]{1,0:T(8,128)(2,1)}, f32[16,768]{1,0:T(8,128)}, bf16[768,2304]{1,0:T(8,128)(2,1)}) custom-call(s32[80]{0:T(128)} %concatenate.81.tbl, bf16[1024,768]{1,0:T(8,128)(2,1)} %x_ref.1, bf16[1024,16]{1,0:T(8,128)(2,1)} %copy.64.pick_ref, ...), custom_call_target="tpu_custom_call" | custom-call | flops 3623878656 | bytes 20971520 | tf_op jit(solution)/shard_map/project/pallas_call | solution.py:538
  70.8 2.0 constant_dynamic-update-slice_fusion.ua
  75.3 2.8 collective-permute-start.12
  79.7 9.3 %attend.2 = (bf16[1024,768]{1,0:T(8,128)(2,1)}, bf16[2,6,4,256,256]{4,3,2,1,0:T(8,128)(2,1)}) custom-call(bf16[1024,2304]{1,0:T(8,128)(2,1)} %get-tuple-element.153.qkv_ref, s32[1024,1]{1,0:T(8,128)} %bitcast.38, s32[2,1,512]{2,1,0:T(1,128)} %reshape.167.segr_ref), custom_call_target="tpu_custom_call" | custom-call | flops 1207959552 | bytes 20971520 | tf_op jit(solution)/shard_map/attend/pallas_call | solution.py:538
  92.3 9.3 %attend.3 = (bf16[1024,768]{1,0:T(8,128)(2,1)}, bf16[2,6,4,256,256]{4,3,2,1,0:T(8,128)(2,1)}) custom-call(bf16[1024,2304]{1,0:T(8,128)(2,1)} %get-tuple-element.153.qkv_ref, s32[1024,1]{1,0:T(8,128)} %bitcast.39, s32[2,1,512]{2,1,0:T(1,128)} %reshape.167.segr_ref, ...), custom_call_target="tpu_custom_call", output_to_operand_aliasing={{0}: (3, {}), {1}: (4, {})} | custom-call | flops 1207959552 | bytes 20971520 | tf_op jit(solution)/shard_map/attend/pallas_call | solution.py:538
  102.5 2.0 constant_dynamic-update-slice_fusion.6.da
  107.0 19.4 %expand.1 = (f32[1024,768]{1,0:T(8,128)}, f32[1024,1]{1,0:T(8,128)}, bf16[1024,3072]{1,0:T(8,128)(2,1)}, bf16[1024,3072]{1,0:T(8,128)(2,1)}, bf16[1024,768]{1,0:T(8,128)(2,1)}, /*index=5*/bf16[768,3840]{1,0:T(8,128)(2,1)}) custom-call(s32[80]{0:T(128)} %concatenate.81.tbl, f32[1024,768]{1,0:T(8,128)} %get-tuple-element.142.hidden_ref, ...), custom_call_target="tpu_custom_call" | custom-call | flops 6039797760 | bytes 20971520 | tf_op jit(solution)/shard_map/expand/pallas_call | solution.py:538
  126.8 2.8 collective-permute-done.18.dd
  129.6 30.9 %contract.1 = (bf16[1024,768]{1,0:T(8,128)(2,1)}, bf16[1024,3072]{1,0:T(8,128)(2,1)}, bf16[1024,768]{1,0:T(8,128)(2,1)}, f32[1024,768]{1,0:T(8,128)}, bf16[1024,...) custom-call(s32[80]{0:T(128)} %concatenate.81.tbl, ...), custom_call_target="tpu_custom_call" | custom-call | flops 14495514624 | bytes 20971520 | tf_op jit(solution)/shard_map/contract/pallas_call | solution.py:538
  160.5 10.2 %down_grad.1 = (bf16[16,192,384]{2,1,0:T(8,128)(2,1)}, bf16[16,192,384]{2,1,0:T(8,128)(2,1)}) custom-call(s32[80]{0:T(128)} %concatenate.81.tbl, bf16[1024,3072]{1,0:T(8,128)(2,1)} %get-tuple-element.169.act_ref, bf16[1024,768]{1,0:T(8,128)(2,1)} %get-tuple-element.178.din_ref), custom_call_target="tpu_custom_call" | custom-call | flops 4831838208 | bytes 20971520 | tf_op jit(solution)/shard_map/down_grad/pallas_call | solution.py:538
  171.1 8.5 %up_other.1 = bf16[16,48,1920]{2,1,0:T(8,128)(2,1)} custom-call(s32[80]{0:T(128)} %concatenate.81.tbl, bf16[1024,768]{1,0:T(8,128)(2,1)} %get-tuple-element.185.mlow_ref, bf16[1024,3072]{1,0:T(8,128)(2,1)} %get-tuple-element.182.dexp_ref, bf16[1024,768]{1,0:T(8,128)(2,1)} %get-tuple-element.159.mix_ref, bf16[1024,768]{1,0:T(8,128)(2,1)} %get-tuple-element.200.ain_ref), custom_call_target="tpu_custom_call" | custom-call | flops 3019898880 | bytes 20971520 | tf_op jit(solution)/shard_map/up_other/pallas_call | solution.py:538
  179.8 4.4 %add_convert_fusion = (bf16[8,192,384]{2,1,0:T(8,128)(2,1)}, bf16[8,192,384]{2,1,0:T(8,128)(2,1)}) fusion(bf16[16,192,384]{2,1,0:T(8,128)(2,1)} %collective-permute-done.19, bf16[16,192,384]{2,1,0:T(8,128)(2,1)} %get-tuple-element.186), kind=kLoop, calls=%fused_computation | loop fusion | flops 4718592 | bytes 7077888 | tf_op jit(solution)/shard_map/convert_element_type | solution.py:806
  186.7 19.9 %up_own.1 = (bf16[8,48,1920]{2,1,0:T(8,128)(2,1)}, bf16[8,48,1920]{2,1,0:T(8,128)(2,1)}) custom-call(s32[80]{0:T(128)} %concatenate.81.tbl, bf16[1024,768]{1,0:T(8,128)(2,1)} %get-tuple-element.185.mlow_ref, bf16[1024,3072]{1,0:T(8,128)(2,1)} %get-tuple-element.182.dexp_ref, bf16[1024,768]{1,0:T(8,128)(2,1)} %get-tuple-element.159.mix_ref, ...), custom_call_target="tpu_custom_call" | custom-call | flops 3019898880 | bytes 20971520 | tf_op jit(solution)/shard_map/up_own/pallas_call | solution.py:538
  207.4 11.3 %attention_backward.2 = (bf16[1024,2304]{1,0:T(8,128)(2,1)}, f32[8,768]{1,0:T(8,128)}, f32[16,2304]{1,0:T(8,128)}) custom-call(bf16[1024,768]{1,0:T(8,128)(2,1)} %get-tuple-element.200.ain_ref, bf16[1024,768]{1,0:T(8,128)(2,1)} %get-tuple-element.159.mix_ref, bf16[1024,2304]{1,0:T(8,128)(2,1)} %get-tuple-element.153.qkv_ref, ...), custom_call_target="tpu_custom_call" | custom-call | flops 1207959552 | bytes 20971520 | tf_op jit(solution)/shard_map/attention_backward/pallas_call | solution.py:538
  218.7 2.9 add_convert_fusion.4
  223.0 11.3 %attention_backward.3 = (bf16[1024,2304]{1,0:T(8,128)(2,1)}, f32[8,768]{1,0:T(8,128)}, f32[16,2304]{1,0:T(8,128)}) custom-call(bf16[1024,768]{1,0:T(8,128)(2,1)} %get-tuple-element.200.ain_ref, bf16[1024,768]{1,0:T(8,128)(2,1)} %get-tuple-element.159.mix_ref, bf16[1024,2304]{1,0:T(8,128)(2,1)} %get-tuple-element.153.qkv_ref, ...), custom_call_target="tpu_custom_call", output_to_operand_aliasing={{0}: (6, {})} | custom-call | flops 1207959552 | bytes 20971520 | tf_op jit(solution)/shard_map/attention_backward/pallas_call | solution.py:538
  235.1 3.1 add_convert_fusion.2
  243.1 10.5 %qkv_other.1 = (bf16[768,256]{1,0:T(8,128)(2,1)}, bf16[16,48,1280]{2,1,0:T(8,128)(2,1)}) custom-call(s32[80]{0:T(128)} %concatenate.81.tbl, bf16[1024,768]{1,0:T(8,128)(2,1)} %get-tuple-element.227.low_ref, bf16[1024,2304]{1,0:T(8,128)(2,1)} %get-tuple-element.213.dqkv_ref, f32[16,768]{1,0:T(8,128)} %get-tuple-element.214.first_ref, ...), custom_call_target="tpu_custom_call" | custom-call | flops 1811939328 | bytes 20971520 | tf_op jit(solution)/shard_map/qkv_other/pallas_call | solution.py:538
  255.6 2.1 add_convert_fusion.8
  259.5 8.2 %qkv_own.1 = (bf16[8,48,1280]{2,1,0:T(8,128)(2,1)}, bf16[8,48,1280]{2,1,0:T(8,128)(2,1)}) custom-call(s32[80]{0:T(128)} %concatenate.81.tbl, bf16[1024,768]{1,0:T(8,128)(2,1)} %get-tuple-element.227.low_ref, bf16[1024,2304]{1,0:T(8,128)(2,1)} %get-tuple-element.213.dqkv_ref, bf16[768,256]{1,0:T(8,128)(2,1)} %get-tuple-element.228.small_ref, ...), custom_call_target="tpu_custom_call" | custom-call | flops 1811939328 | bytes 20971520 | tf_op jit(solution)/shard_map/qkv_own/pallas_call | solution.py:538
  271.5 2.7 collective-permute-start.34
  274.2 9.0 %input_grad.1 = f32[1024,768]{1,0:T(8,128)} custom-call(f32[1024,768]{1,0:T(8,128)} %get-tuple-element.243.df_ref, bf16[1024,2304]{1,0:T(8,128)(2,1)} %get-tuple-element.213.dqkv_ref, bf16[768,2304]{1,0:T(8,128)(2,1)} %get-tuple-element.217.w_ref), custom_call_target="tpu_custom_call" | custom-call | flops 3623878656 | bytes 20971520 | tf_op jit(solution)/shard_map/input_grad/pallas_call | solution.py:538
  286.3 2.1 collective-permute-done.34
  291.8 1.9 collective-permute-done.29
  295.5 5.0 %collective-permute-done.30 = bf16[2,48,1280]{2,1,0:T(8,128)(2,1)S(1)} collective-permute-done((bf16[2,48,1280]{2,1,0:T(8,128)(2,1)S(1)}, bf16[2,48,1280]{2,1,0:T(8,128)(2,1)S(1)}, u32[]{:S(2)}, u32[]{:S(2)}) %collective-permute-start.30) | collective-permute-done | bytes 245792 | tf_op jit(solution)/shard_map/ppermute | solution.py:773
  301.4 4.9 %collective-permute-done.31 = bf16[1,48,1280]{2,1,0:T(8,128)(2,1)S(1)} collective-permute-done((bf16[1,48,1280]{2,1,0:T(8,128)(2,1)S(1)}, bf16[1,48,1280]{2,1,0:T(8,128)(2,1)S(1)}, u32[]{:S(2)}, u32[]{:S(2)}) %collective-permute-start.31) | collective-permute-done | bytes 122912 | tf_op jit(solution)/shard_map/ppermute | solution.py:773
  (205 shorter events, 64.8 us)
Async XLA Ops:
  9.0 10.3 %collective-permute-start.1 = (bf16[1,48,1280]{2,1,0:T(8,128)(2,1)S(1)}, bf16[1,48,1280]{2,1,0:T(8,128)(2,1)S(1)}, u32[]{:S(2)}, u32[]{:S(2)}) collective-permute-start(bf16[1,48,1280]{2,1,0:T(8,128)(2,1)S(1)} %maximum_bitcast_fusion.2), channel_id=1, source_target_pairs={{0,16},{1,17},{2,18},{3,19},{4,20},{5,21},{6,22},{7,23},{8,24},{9,... | collective-permute-start | bytes 368648 | tf_op jit(solution)/shard_map/ppermute | solution.py:773
  19.3 7.6 %collective-permute-start.2 = (bf16[2,48,1280]{2,1,0:T(8,128)(2,1)S(1)}, bf16[2,48,1280]{2,1,0:T(8,128)(2,1)S(1)}, u32[]{:S(2)}, u32[]{:S(2)}) collective-permute-start(bf16[2,48,1280]{2,1,0:T(8,128)(2,1)S(1)} %pad_maximum_fusion.6), channel_id=1, source_target_pairs={{0,8},{1,9},{2,10},{3,11},{4,12},{5,13},{6,14},{7,15},{8,0},{9,1},... | collective-permute-start | bytes 737288 | tf_op jit(solution)/shard_map/ppermute | solution.py:773
  26.9 12.5 %collective-permute-start.3 = (bf16[4,48,1280]{2,1,0:T(8,128)(2,1)S(1)}, bf16[4,48,1280]{2,1,0:T(8,128)(2,1)S(1)}, u32[]{:S(2)}, u32[]{:S(2)}) collective-permute-start(bf16[4,48,1280]{2,1,0:T(8,128)(2,1)S(1)} %pad_maximum_fusion.2), channel_id=1, source_target_pairs={{0,2},{1,5},{2,0},{3,7},{4,6},{5,1},{6,4},{7,3},{8,10},{9,13},{10,... | collective-permute-start | bytes 1474568 | tf_op jit(solution)/shard_map/ppermute | solution.py:773
  28.2 11.1 %collective-permute-start.4 = (bf16[1,48,1920]{2,1,0:T(8,128)(2,1)S(1)}, bf16[1,48,1920]{2,1,0:T(8,128)(2,1)S(1)}, u32[]{:S(2)}, u32[]{:S(2)}) collective-permute-start(bf16[1,48,1920]{2,1,0:T(8,128)(2,1)S(1)} %maximum_bitcast_fusion), channel_id=1, source_target_pairs={{0,16},{1,17},{2,18},{3,19},{4,20},{5,21},{6,22},{7,23},{8,24},{9,... | collective-permute-start | bytes 552968 | tf_op jit(solution)/shard_map/ppermute | solution.py:773
  39.5 14.3 %collective-permute-start.5 = (bf16[8,48,1280]{2,1,0:T(8,128)(2,1)S(1)}, bf16[8,48,1280]{2,1,0:T(8,128)(2,1)}, u32[]{:S(2)}, u32[]{:S(2)}) collective-permute-start(bf16[8,48,1280]{2,1,0:T(8,128)(2,1)S(1)} %pad_maximum_fusion.own_low), channel_id=1, source_target_pairs={{0,4},{1,3},{2,6},{3,1},{4,0},{5,7},{6,2},{7,5},{8,12},{9,11},{10,... | collective-permute-start | bytes 2949128 | tf_op jit(solution)/shard_map/ppermute | solution.py:773
  40.4 10.9 %collective-permute-start.6 = (bf16[2,48,1920]{2,1,0:T(8,128)(2,1)S(1)}, bf16[2,48,1920]{2,1,0:T(8,128)(2,1)}, u32[]{:S(2)}, u32[]{:S(2)}) collective-permute-start(bf16[2,48,1920]{2,1,0:T(8,128)(2,1)S(1)} %pad_maximum_fusion.3), channel_id=1, source_target_pairs={{0,8},{1,9},{2,10},{3,11},{4,12},{5,13},{6,14},{7,15},{8,0},{9,1},... | collective-permute-start | bytes 1105928 | tf_op jit(solution)/shard_map/ppermute | solution.py:773
  41.2 17.0 %collective-permute-start.7 = (bf16[8,48,1280]{2,1,0:T(8,128)(2,1)S(1)}, bf16[8,48,1280]{2,1,0:T(8,128)(2,1)}, u32[]{:S(2)}, u32[]{:S(2)}) collective-permute-start(bf16[8,48,1280]{2,1,0:T(8,128)(2,1)S(1)} %pad_maximum_fusion.own_low), channel_id=1, source_target_pairs={{0,1},{1,0},{2,3},{3,2},{4,5},{5,4},{6,7},{7,6},{8,9},{9,8},{10,11... | collective-permute-start | bytes 2949128 | tf_op jit(solution)/shard_map/ppermute | solution.py:773
  53.8 4.4 %collective-permute-start.8 = (bf16[8,48,1280]{2,1,0:T(8,128)(2,1)}, bf16[8,48,1280]{2,1,0:T(8,128)(2,1)}, u32[]{:S(2)}, u32[]{:S(2)}) collective-permute-start(bf16[8,48,1280]{2,1,0:T(8,128)(2,1)} %collective-permute-done.5.own_high), channel_id=1, source_target_pairs={{0,1},{1,0},{2,3},{3,2},{4,5},{5,4},{6,7},{7,6},{8,9},{9,8},{10,11... | collective-permute-start | bytes 2949128 | tf_op jit(solution)/shard_map/ppermute | solution.py:773
  55.5 14.4 %collective-permute-start.9 = (bf16[4,48,1920]{2,1,0:T(8,128)(2,1)S(1)}, bf16[4,48,1920]{2,1,0:T(8,128)(2,1)}, u32[]{:S(2)}, u32[]{:S(2)}) collective-permute-start(bf16[4,48,1920]{2,1,0:T(8,128)(2,1)S(1)} %pad_maximum_fusion.1), channel_id=1, source_target_pairs={{0,2},{1,5},{2,0},{3,7},{4,6},{5,1},{6,4},{7,3},{8,10},{9,13},{10,... | collective-permute-start | bytes 2211848 | tf_op jit(solution)/shard_map/ppermute | solution.py:773
  57.8 12.1 %collective-permute-start.10 = (bf16[1,192,384]{2,1,0:T(8,128)(2,1)S(1)}, bf16[1,192,384]{2,1,0:T(8,128)(2,1)}, u32[]{:S(2)}, u32[]{:S(2)}) collective-permute-start(bf16[1,192,384]{2,1,0:T(8,128)(2,1)S(1)} %maximum_bitcast_fusion.1), channel_id=1, source_target_pairs={{0,16},{1,17},{2,18},{3,19},{4,20},{5,21},{6,22},{7,23},{8,24},{9,... | collective-permute-start | bytes 442376 | tf_op jit(solution)/shard_map/ppermute | solution.py:773
  72.9 16.1 %collective-permute-start.11 = (bf16[8,48,1920]{2,1,0:T(8,128)(2,1)}, bf16[8,48,1920]{2,1,0:T(8,128)(2,1)}, u32[]{:S(2)}, u32[]{:S(2)}) collective-permute-start(bf16[8,48,1920]{2,1,0:T(8,128)(2,1)} %constant_dynamic-update-slice_fusion.ua), channel_id=1, source_target_pairs={{0,1},{1,0},{2,3},{3,2},{4,5},{5,4},{6,7},{7,6},{8,9},{9,8},{10,11... | collective-permute-start | bytes 4423688 | tf_op jit(solution)/shard_map/ppermute | solution.py:773
  72.9 28.7 %collective-permute-start.13 = (bf16[8,48,1920]{2,1,0:T(8,128)(2,1)}, bf16[8,48,1920]{2,1,0:T(8,128)(2,1)}, u32[]{:S(2)}, u32[]{:S(2)}) collective-permute-start(bf16[8,48,1920]{2,1,0:T(8,128)(2,1)} %constant_dynamic-update-slice_fusion.ua), channel_id=1, source_target_pairs={{0,4},{1,3},{2,6},{3,1},{4,0},{5,7},{6,2},{7,5},{8,12},{9,11},{10,... | collective-permute-start | bytes 4423688 | tf_op jit(solution)/shard_map/ppermute | solution.py:773
  75.3 13.7 %collective-permute-start.12 = (bf16[2,192,384]{2,1,0:T(8,128)(2,1)S(1)}, bf16[2,192,384]{2,1,0:T(8,128)(2,1)S(1)}, u32[]{:S(2)}, u32[]{:S(2)}) collective-permute-start(bf16[2,192,384]{2,1,0:T(8,128)(2,1)S(1)} %constant_dynamic-update-slice_fusion.2), channel_id=1, source_target_pairs={{0,8},{1,9},{2,10},{3,11},{4,12},{5,13},{6,14},{7,15},{8,0},{9,1},... | collective-permute-start | bytes 884744 | tf_op jit(solution)/shard_map/ppermute | solution.py:773
  90.8 10.8 %collective-permute-start.14 = (bf16[4,192,384]{2,1,0:T(8,128)(2,1)S(1)}, bf16[4,192,384]{2,1,0:T(8,128)(2,1)}, u32[]{:S(2)}, u32[]{:S(2)}) collective-permute-start(bf16[4,192,384]{2,1,0:T(8,128)(2,1)S(1)} %constant_dynamic-update-slice_fusion.4), channel_id=1, source_target_pairs={{0,2},{1,5},{2,0},{3,7},{4,6},{5,1},{6,4},{7,3},{8,10},{9,13},{10,... | collective-permute-start | bytes 1769480 | tf_op jit(solution)/shard_map/ppermute | solution.py:773
  101.6 5.4 %collective-permute-start.15 = (bf16[8,48,1920]{2,1,0:T(8,128)(2,1)}, bf16[8,48,1920]{2,1,0:T(8,128)(2,1)}, u32[]{:S(2)}, u32[]{:S(2)}) collective-permute-start(bf16[8,48,1920]{2,1,0:T(8,128)(2,1)} %collective-permute-done.13.ub), channel_id=1, source_target_pairs={{0,1},{1,0},{2,3},{3,2},{4,5},{5,4},{6,7},{7,6},{8,9},{9,8},{10,11... | collective-permute-start | bytes 4423688 | tf_op jit(solution)/shard_map/ppermute | solution.py:773
  104.5 21.9 %collective-permute-start.16 = (bf16[8,192,384]{2,1,0:T(8,128)(2,1)}, bf16[8,192,384]{2,1,0:T(8,128)(2,1)}, u32[]{:S(2)}, u32[]{:S(2)}) collective-permute-start(bf16[8,192,384]{2,1,0:T(8,128)(2,1)} %constant_dynamic-update-slice_fusion.6.da), channel_id=1, source_target_pairs={{0,4},{1,3},{2,6},{3,1},{4,0},{5,7},{6,2},{7,5},{8,12},{9,11},{10,... | collective-permute-start | bytes 3538952 | tf_op jit(solution)/shard_map/ppermute | solution.py:773
  106.8 20.0 %collective-permute-start.17 = (bf16[8,192,384]{2,1,0:T(8,128)(2,1)}, bf16[8,192,384]{2,1,0:T(8,128)(2,1)}, u32[]{:S(2)}, u32[]{:S(2)}) collective-permute-start(bf16[8,192,384]{2,1,0:T(8,128)(2,1)} %constant_dynamic-update-slice_fusion.6.da), channel_id=1, source_target_pairs={{0,1},{1,0},{2,3},{3,2},{4,5},{5,4},{6,7},{7,6},{8,9},{9,8},{10,11... | collective-permute-start | bytes 3538952 | tf_op jit(solution)/shard_map/ppermute | solution.py:773
  170.7 8.9 %collective-permute-start.19 = (bf16[16,192,384]{2,1,0:T(8,128)(2,1)}, bf16[16,192,384]{2,1,0:T(8,128)(2,1)}, u32[]{:S(2)}, u32[]{:S(2)}) collective-permute-start(bf16[16,192,384]{2,1,0:T(8,128)(2,1)} %get-tuple-element.184), channel_id=1, source_target_pairs={{0,1},{1,0},{2,3},{3,2},{4,5},{5,4},{6,7},{7,6},{8,9},{9,8},{10,11... | collective-permute-start | bytes 7077896 | tf_op jit(solution)/shard_map/ppermute | solution.py:773
  179.6 5.8 %collective-permute-start.20 = (bf16[16,48,1920]{2,1,0:T(8,128)(2,1)}, bf16[16,48,1920]{2,1,0:T(8,128)(2,1)}, u32[]{:S(2)}, u32[]{:S(2)}) collective-permute-start(bf16[16,48,1920]{2,1,0:T(8,128)(2,1)} %up_other.1), channel_id=1, source_target_pairs={{0,1},{1,0},{2,3},{3,2},{4,5},{5,4},{6,7},{7,6},{8,9},{9,8},{10,11... | collective-permute-start | bytes 8847368 | tf_op jit(solution)/shard_map/ppermute | solution.py:773
  185.4 33.3 %collective-permute-start.21 = (bf16[8,192,384]{2,1,0:T(8,128)(2,1)}, bf16[8,192,384]{2,1,0:T(8,128)(2,1)}, u32[]{:S(2)}, u32[]{:S(2)}) collective-permute-start(bf16[8,192,384]{2,1,0:T(8,128)(2,1)} %get-tuple-element.196), channel_id=1, source_target_pairs={{0,4},{1,3},{2,6},{3,1},{4,0},{5,7},{6,2},{7,5},{8,12},{9,11},{10,... | collective-permute-start | bytes 3538952 | tf_op jit(solution)/shard_map/ppermute | solution.py:773
  206.6 27.8 %collective-permute-start.23 = (bf16[8,48,1920]{2,1,0:T(8,128)(2,1)}, bf16[8,48,1920]{2,1,0:T(8,128)(2,1)}, u32[]{:S(2)}, u32[]{:S(2)}) collective-permute-start(bf16[8,48,1920]{2,1,0:T(8,128)(2,1)} %get-tuple-element.206), channel_id=1, source_target_pairs={{0,4},{1,3},{2,6},{3,1},{4,0},{5,7},{6,2},{7,5},{8,12},{9,11},{10,... | collective-permute-start | bytes 4423688 | tf_op jit(solution)/shard_map/ppermute | solution.py:773
  221.6 12.7 %collective-permute-start.22 = (bf16[4,192,384]{2,1,0:T(8,128)(2,1)}, bf16[4,192,384]{2,1,0:T(8,128)(2,1)S(1)}, u32[]{:S(2)}, u32[]{:S(2)}) collective-permute-start(bf16[4,192,384]{2,1,0:T(8,128)(2,1)} %get-tuple-element.204), channel_id=1, source_target_pairs={{0,2},{1,5},{2,0},{3,7},{4,6},{5,1},{6,4},{7,3},{8,10},{9,13},{10,... | collective-permute-start | bytes 1769480 | tf_op jit(solution)/shard_map/ppermute | solution.py:773
  239.2 14.4 %collective-permute-start.24 = (bf16[4,48,1920]{2,1,0:T(8,128)(2,1)}, bf16[4,48,1920]{2,1,0:T(8,128)(2,1)}, u32[]{:S(2)}, u32[]{:S(2)}) collective-permute-start(bf16[4,48,1920]{2,1,0:T(8,128)(2,1)} %get-tuple-element.224), channel_id=1, source_target_pairs={{0,2},{1,5},{2,0},{3,7},{4,6},{5,1},{6,4},{7,3},{8,10},{9,13},{10,... | collective-permute-start | bytes 2211848 | tf_op jit(solution)/shard_map/ppermute | solution.py:773
  239.9 13.7 %collective-permute-start.25 = (bf16[2,192,384]{2,1,0:T(8,128)(2,1)}, bf16[2,192,384]{2,1,0:T(8,128)(2,1)}, u32[]{:S(2)}, u32[]{:S(2)}) collective-permute-start(bf16[2,192,384]{2,1,0:T(8,128)(2,1)} %get-tuple-element.226), channel_id=1, source_target_pairs={{0,8},{1,9},{2,10},{3,11},{4,12},{5,13},{6,14},{7,15},{8,0},{9,1},... | collective-permute-start | bytes 884744 | tf_op jit(solution)/shard_map/ppermute | solution.py:773
  258.0 10.9 %collective-permute-start.27 = (bf16[2,48,1920]{2,1,0:T(8,128)(2,1)}, bf16[2,48,1920]{2,1,0:T(8,128)(2,1)S(1)}, u32[]{:S(2)}, u32[]{:S(2)}) collective-permute-start(bf16[2,48,1920]{2,1,0:T(8,128)(2,1)} %get-tuple-element.238), channel_id=1, source_target_pairs={{0,8},{1,9},{2,10},{3,11},{4,12},{5,13},{6,14},{7,15},{8,0},{9,1},... | collective-permute-start | bytes 1105928 | tf_op jit(solution)/shard_map/ppermute | solution.py:773
  268.9 14.4 %collective-permute-start.28 = (bf16[8,48,1280]{2,1,0:T(8,128)(2,1)}, bf16[8,48,1280]{2,1,0:T(8,128)(2,1)}, u32[]{:S(2)}, u32[]{:S(2)}) collective-permute-start(bf16[8,48,1280]{2,1,0:T(8,128)(2,1)} %get-tuple-element.245), channel_id=1, source_target_pairs={{0,4},{1,3},{2,6},{3,1},{4,0},{5,7},{6,2},{7,5},{8,12},{9,11},{10,... | collective-permute-start | bytes 2949128 | tf_op jit(solution)/shard_map/ppermute | solution.py:773
  271.3 17.1 %collective-permute-start.33 = (bf16[1,48,1920]{2,1,0:T(8,128)(2,1)}, bf16[1,48,1920]{2,1,0:T(8,128)(2,1)}, u32[]{:S(2)}, u32[]{:S(2)}) collective-permute-start(bf16[1,48,1920]{2,1,0:T(8,128)(2,1)} %get-tuple-element.250), channel_id=1, source_target_pairs={{0,16},{1,17},{2,18},{3,19},{4,20},{5,21},{6,22},{7,23},{8,24},{9,... | collective-permute-start | bytes 552968 | tf_op jit(solution)/shard_map/ppermute | solution.py:773
  271.5 16.9 %collective-permute-start.34 = (bf16[1,192,384]{2,1,0:T(8,128)(2,1)}, bf16[1,192,384]{2,1,0:T(8,128)(2,1)}, u32[]{:S(2)}, u32[]{:S(2)}) collective-permute-start(bf16[1,192,384]{2,1,0:T(8,128)(2,1)} %get-tuple-element.252), channel_id=1, source_target_pairs={{0,16},{1,17},{2,18},{3,19},{4,20},{5,21},{6,22},{7,23},{8,24},{9,... | collective-permute-start | bytes 442376 | tf_op jit(solution)/shard_map/ppermute | solution.py:773
  284.8 8.9 %collective-permute-start.29 = (bf16[4,48,1280]{2,1,0:T(8,128)(2,1)S(1)}, bf16[4,48,1280]{2,1,0:T(8,128)(2,1)S(1)}, u32[]{:S(2)}, u32[]{:S(2)}) collective-permute-start(bf16[4,48,1280]{2,1,0:T(8,128)(2,1)S(1)} %get-tuple-element.273), channel_id=1, source_target_pairs={{0,2},{1,5},{2,0},{3,7},{4,6},{5,1},{6,4},{7,3},{8,10},{9,13},{10,... | collective-permute-start | bytes 1474568 | tf_op jit(solution)/shard_map/ppermute | solution.py:773
  290.5 4.9 %collective-permute-start.35 = (bf16[24,1920]{1,0:T(8,128)(2,1)S(1)}, bf16[24,1920]{1,0:T(8,128)(2,1)S(1)}, u32[]{:S(2)}, u32[]{:S(2)}) collective-permute-start(bf16[24,1920]{1,0:T(8,128)(2,1)S(1)} %fusion), channel_id=1, source_target_pairs={{0,1},{1,0},{2,3},{3,2},{4,5},{5,4},{6,7},{7,6},{8,9},{9,8},{10,11... | collective-permute-start | bytes 276488 | tf_op jit(solution)/shard_map/ppermute | solution.py:773
  293.9 6.5 %collective-permute-start.30 = (bf16[2,48,1280]{2,1,0:T(8,128)(2,1)S(1)}, bf16[2,48,1280]{2,1,0:T(8,128)(2,1)S(1)}, u32[]{:S(2)}, u32[]{:S(2)}) collective-permute-start(bf16[2,48,1280]{2,1,0:T(8,128)(2,1)S(1)} %get-tuple-element.279), channel_id=1, source_target_pairs={{0,8},{1,9},{2,10},{3,11},{4,12},{5,13},{6,14},{7,15},{8,0},{9,1},... | collective-permute-start | bytes 737288 | tf_op jit(solution)/shard_map/ppermute | solution.py:773
  300.4 5.8 %collective-permute-start.31 = (bf16[1,48,1280]{2,1,0:T(8,128)(2,1)S(1)}, bf16[1,48,1280]{2,1,0:T(8,128)(2,1)S(1)}, u32[]{:S(2)}, u32[]{:S(2)}) collective-permute-start(bf16[1,48,1280]{2,1,0:T(8,128)(2,1)S(1)} %add_convert_fusion.18), channel_id=1, source_target_pairs={{0,16},{1,17},{2,18},{3,19},{4,20},{5,21},{6,22},{7,23},{8,24},{9,... | collective-permute-start | bytes 368648 | tf_op jit(solution)/shard_map/ppermute | solution.py:773
  (22 other events, 148.4 us)
where the time goes:
time: 317 us; the launch traced here: 312 us
  Pallas kernels  169 us (53%)
  waiting for transfers between devices  53 us (17%)
  starting transfers between devices  35.7 us (11%)
  other arithmetic  29.7 us (9%)
  local copies, waits for them, and re-layouts  22.6 us (7%)
    pallas_call x13, Pallas kernels, call(): pl.pallas_call(kernel, name=name, grid_spec=pltpu.PrefetchScalarGridSpec(...  169 us
    ppermute x37, waiting for transfers between devices, send_on(): return lax.ppermute(value, 'fsdp', perm=tiled_route(n)[step])  53 us
    ppermute x37, starting transfers between devices, send_on(): return lax.ppermute(value, 'fsdp', perm=tiled_route(n)[step])  35.7 us
    convert_element_type x10, other arithmetic, add(): return (left.astype(F32) + right.astype(F32)).astype(BF16)  17.9 us
  transfers between devices with their start and end apart: 37, of which 16 were waited for; matrix products, arithmetic and copies ran while one was open for 11% of the time, Pallas kernels for 41%

commit v1 on v0

--- a/solution.py
+++ b/solution.py
@@ -23,6 +23,7 @@
 HIGH = lax.Precision.HIGHEST
 SQRT_HALF = 0.7071067811865476
 INV_ROOT_TAU = 0.3989422804014327
+HALF_LOG = -0.5 / math.log(2.0)
 WINDOWS = (0, 64, 192, 256)
 F32 = jnp.float32
 BF16 = jnp.bfloat16
@@ -91,7 +92,7 @@
 
 def project_kernel(
     tbl, x_ref, pick_ref, embed_ref, own_low, own_high, other_low, other_high,
-    hidden_ref, low_ref, qkv_ref, vec_ref, w_ref, weight, sems, out_sem,
+    hidden_ref, low_ref, qkv_ref, vec_ref, w_ref, weight, offset, factor, sems, out_sem,
 ):
     step = pl.program_id(0)
     save = pltpu.make_async_copy(weight.at[:, pl.ds(0, 2 * QKV)], w_ref, out_sem.at[0])
@@ -106,6 +107,14 @@
             copy.wait()
         save.start()
         vec_ref[...] = weight[:, 2 * QKV + TDIM :].astype(F32).T[:16, :]
+        offset[...] = jnp.zeros_like(offset)
+        factor[...] = jnp.ones_like(factor)
+        for half in range(2):
+            cols = slice(HALF * half, HALF * half + HALF)
+            at = QKV * half
+            offset[:, at : at + HALF] = vec_ref[0:1, cols]
+            offset[:, at + 2 * HALF : at + QKV] = vec_ref[1:2, cols]
+            factor[:, at : at + HALF] = jnp.full((1, HALF), HEAD**-0.5, F32)
 
     slots = nt(embed_ref[...], weight[:, 2 * QKV : 2 * QKV + TDIM]) + vec_ref[8:9, :]
     high, middle, rest = split_bf16(slots)
@@ -115,29 +124,25 @@
     hidden_ref[...] = x_ref[...].astype(F32) + slot
     low_ref[...] = hidden_ref[...].astype(BF16)
 
-    def place(y, run):
-        half, kind = divmod(run, 3)
-        cols = slice(HALF * half, HALF * half + HALF)
-        if kind == 0:
-            y = (y + vec_ref[0:1, cols]).astype(BF16) * jnp.asarray(HEAD**-0.5, BF16)
-        elif kind == 2:
-            y = y + vec_ref[1:2, cols]
-        qkv_ref[:, HALF * run : HALF * run + HALF] = y.astype(BF16)
-
-    for chunk in range(3):
-        y = nn(low_ref[...], weight[:, D * chunk : D * chunk + D])
-        place(y[:, :HALF], 2 * chunk)
-        place(y[:, HALF:], 2 * chunk + 1)
+    def chunk(j, carry):
+        at = pl.ds(pl.multiple_of(j * D, D), D)
+        y = nn(low_ref[...], weight[:, at]) + offset[:, at]
+        qkv_ref[:, at] = (y.astype(BF16).astype(F32) * factor[:, at]).astype(BF16)
+        return carry
+
+    lax.fori_loop(0, 3, chunk, 0)
 
     @pl.when(step == pl.num_programs(0) - 1)
     def _():
         save.wait()
 
 
-def attend_kernel(qkv_ref, segc_ref, segr_ref, *rest):
-    mix_ref, probs_ref, bias, scores = rest[-4:]
+def attend_kernel(block, qkv_ref, pick_ref, segr_ref, *rest):
+    mix_ref, probs_ref, bias, scores, held, sems = rest[-6:]
+    slot = lax.broadcasted_iota(jnp.int32, pick_ref.shape, 1).astype(F32)
+    owner = jnp.sum(pick_ref[...].astype(F32) * slot, axis=1, keepdims=True)
     for t in range(4):
-        same = segc_ref[WINDOWS[t] : WINDOWS[t] + 256, :] == segr_ref[0, :, 128 * t : 128 * t + 128]
+        same = owner[WINDOWS[t] : WINDOWS[t] + 256, :] == segr_ref[0, :, 128 * t : 128 * t + 128]
         bias[t] = jnp.where(same, 0.0, NEG)
     first, second, _ = lane_masks()
 
@@ -154,21 +159,31 @@
         scores[t % 2] = s
         return jnp.max(s, axis=0, keepdims=True)
 
+    def out_copy(p):
+        return pltpu.make_async_copy(held.at[p % 2], probs_ref.at[block, p], sems.at[p % 2])
+
     def pair(p, peak):
+        @pl.when(p >= 2)
+        def _():
+            out_copy(p - 2).wait()
+
         for t in range(4):
             ahead = scores_of(p, t + 1) if t < 3 else scores_of(jnp.minimum(p + 1, HEADS // 2 - 1), 0)
             at, window = operands(p, t)
             v = qkv_ref[window, pl.ds(at + 2 * HALF, 128)]
             e = jnp.exp(scores[t % 2] - peak)
             probs = (e * (1.0 / jnp.sum(e, axis=0, keepdims=True))).astype(BF16)
-            probs_ref[0, p, t] = probs
+            held[p % 2, t] = probs
             out = tn(v, probs)
             out = jnp.concatenate([out[:HEAD, :128], out[HEAD:, 128:]], axis=0)
             mix_ref[128 * t : 128 * t + 128, pl.ds(pl.multiple_of(p * 128, 128), 128)] = out.T.astype(BF16)
             peak = ahead
+        out_copy(p).start()
         return peak
 
     lax.fori_loop(0, HEADS // 2, pair, scores_of(0, 0))
+    out_copy(HEADS // 2 - 2).wait()
+    out_copy(HEADS // 2 - 1).wait()
 
 def expand_kernel(
     tbl, hidden_ref, mix_ref, vec_ref, upb_ref, ua, ub, uc, ud,
@@ -176,15 +191,15 @@
 ):
     step = pl.program_id(0)
     save = pltpu.make_async_copy(up, up_ref, out_sem.at[0])
+    both = piece_copies(tbl, (ua, ub, uc, ud), up, sems, 48, ((FF // 2, HALF, FF), (0, FF // 2, 0)))
+    copies = both[0::2], both[1::2]
 
     @pl.when(step == 0)
     def _():
-        copies = piece_copies(tbl, (ua, ub, uc, ud), up, sems, 48, ((0, FF // 2, 0), (FF // 2, HALF, FF)))
-        for copy in copies:
+        for copy in copies[0] + copies[1]:
             copy.start()
-        for copy in copies:
+        for copy in copies[0]:
             copy.wait()
-        save.start()
 
     normed, inverse = normalize(hidden_ref[...] + nn(mix_ref[...], up[:, FF:]) + vec_ref[2:3, :])
     n1_ref[...] = normed
@@ -201,7 +216,13 @@
         scaled = u * SQRT_HALF
         twice = 1.0 + lax.erf(scaled)
         act_ref[:, at] = ((u * 0.5) * twice).astype(BF16)
-        slope_ref[:, at] = (0.5 * twice + (u * INV_ROOT_TAU) * jnp.exp(-(scaled * scaled))).astype(BF16)
+        slope_ref[:, at] = (0.5 * twice + (u * INV_ROOT_TAU) * jnp.exp2((u * u) * HALF_LOG)).astype(BF16)
+
+    @pl.when(step == 0)
+    def _():
+        for copy in copies[1]:
+            copy.wait()
+        save.start()
 
     expand(0)
     for j in range(FF // D):
@@ -216,9 +237,10 @@
 
 def contract_kernel(
     tbl, n1_ref, i1_ref, cot_ref, vec_ref, act_ref, slope_ref, up_ref, pick_ref, da, db, dc, dd,
-    res_ref, dexp_ref, din_ref, df_ref, ain_ref, vg_ref, gup_ref, slot_ref, down, wide, sems,
+    res_ref, dexp_ref, din_ref, df_ref, ain_ref, vg_ref, gup_ref, slot_ref, down, up, wide, sems, up_sem,
 ):
     step = pl.program_id(0)
+    fetch = pltpu.make_async_copy(up_ref.at[:, pl.ds(0, FF)], up, up_sem.at[0])
 
     @pl.when(step == 0)
     def _():
@@ -227,6 +249,7 @@
             copy.start()
         for copy in copies:
             copy.wait()
+        fetch.start()
         vg_ref[...] = jnp.zeros_like(vg_ref)
         gup_ref[...] = jnp.zeros_like(gup_ref)
         slot_ref[...] = jnp.zeros_like(slot_ref)
@@ -248,6 +271,10 @@
     def contract(j):
         wide[j % 2] = nt(din_ref[...], down[j * D : j * D + D, :])
 
+    @pl.when(step == 0)
+    def _():
+        fetch.wait()
+
     contract(0)
     for j in range(FF // D):
         if j + 1 < FF // D:
@@ -256,7 +283,7 @@
         d_exp = (wide[j % 2] * slope_ref[:, at].astype(F32)).astype(BF16)
         dexp_ref[:, at] = d_exp
         gup_ref[:, at] += column_sum(d_exp.astype(F32))
-    d_middle = nt(dexp_ref[...], up_ref[...]) + d_second
+    d_middle = nt(dexp_ref[...], up[...]) + d_second
     normed1 = n1_ref[...]
     vg_ref[3:4, :] += column_sum(d_middle * normed1)
     vg_ref[4:5, :] += column_sum(d_middle)
@@ -338,54 +365,39 @@
     return made
 
 
-def leave(tbl, src, chip, keep, away, cols, sem, act):
-    at = tbl[OWN_POS + chip]
-
-    @pl.when(at < CHIPS // 2)
-    def _():
-        act(pltpu.make_async_copy(src, keep.at[at, :, cols], sem))
-
-    @pl.when(at >= CHIPS // 2)
-    def _():
-        act(pltpu.make_async_copy(src, away.at[at - CHIPS // 2, :, cols], sem))
-
-
-def start(copy):
-    copy.start()
-
-
-def wait(copy):
-    copy.wait()
-
-
-def up_own_kernel(tbl, mlow_ref, dexp_ref, mix_ref, ain_ref, got, keep, away, hold, came, sems, came_sems):
+def leave(tbl, src, first, count, keep, away, cols):
+    def one(k, carry):
+        at = tbl[OWN_POS + first + k]
+        rows = src[pl.ds(pl.multiple_of(48 * k, 48), 48), :]
+
+        @pl.when(at < CHIPS // 2)
+        def _():
+            keep[at, :, cols] = rows
+
+        @pl.when(at >= CHIPS // 2)
+        def _():
+            away[at - CHIPS // 2, :, cols] = rows
+
+        return carry
+
+    lax.fori_loop(0, count, one, 0)
+
+
+def up_own_kernel(tbl, mlow_ref, dexp_ref, mix_ref, ain_ref, got, keep, away, hold, came, came_sems):
     step = pl.program_id(0)
 
     @pl.when(step == 0)
     def _():
         for copy in arrivals(tbl, got, came, 48, came_sems):
             copy.start()
-
-    def each(j, width, act):
-        for chip in range(CHIPS):
-            src = hold.at[j, pl.ds(48 * chip, 48), pl.ds(0, width)]
-            leave(tbl, src, chip, keep, away, pl.ds(pl.multiple_of(j * D, D), width), sems.at[j, chip], act)
-
-    def give(grad, cols, width):
-        hold[step, :, :width] = (grad + came[:, cols].astype(F32)).astype(BF16)
-        each(step, width, start)
-
-    @pl.when(step == 0)
-    def _():
         for copy in arrivals(tbl, got, came, 48, came_sems):
             copy.wait()
 
+    def give(grad, cols, width):
+        hold[:, :width] = (grad + came[:, cols].astype(F32)).astype(BF16)
+        leave(tbl, hold.at[:, pl.ds(0, width)], 0, CHIPS, keep, away, cols)
+
     product_for(step, mlow_ref, dexp_ref, mix_ref, ain_ref, give)
-
-    @pl.when(step == 2)
-    def _():
-        for j in range(3):
-            each(j, D if j < 2 else HALF, wait)
 
 
 def attention_backward_kernel(ain_ref, mix_ref, qkv_ref, probs_ref, w_ref, pick_ref, *rest):
@@ -447,9 +459,10 @@
     slot_ref[...] = tn(pick_ref[...], dqkv_ref[...])
 
 
-def small_grads(first_ref, second_ref, w_ref, embed_ref, ff_ref, va_ref, vb_ref, up_ref):
-    high, low, _ = split_bf16(second_ref[...])
-    slots = first_ref[...] + nt(high, w_ref[...]) + nt(low, w_ref[...])
+def small_grads(first_ref, sa_ref, sb_ref, w_ref, embed_ref, ff_ref, va_ref, vb_ref, up_ref):
+    high, low, _ = split_bf16(sa_ref[...] + sb_ref[...])
+    both = nt(jnp.concatenate([high, low], axis=0), w_ref[...])
+    slots = first_ref[...] + both[: high.shape[0]] + both[high.shape[0] :]
     slot_low = slots.astype(BF16)
     rows = [column_sum(slot_low.astype(F32)), va_ref[0:2, :] + vb_ref[0:2, :], ff_ref[0:6, :], up_ref[0:4, :]]
     rows.append(jnp.zeros((TDIM - 13, D), F32))
@@ -458,7 +471,7 @@
 
 
 def qkv_other_kernel(
-    tbl, low_ref, dqkv_ref, first_ref, second_ref, w_ref, embed_ref, ff_ref, va_ref, vb_ref, up_ref,
+    tbl, low_ref, dqkv_ref, first_ref, sa_ref, sb_ref, w_ref, embed_ref, ff_ref, va_ref, vb_ref, up_ref,
     small_ref, other, hold, extra, sems, small_sems,
 ):
     step = pl.program_id(0)
@@ -474,7 +487,7 @@
 
     @pl.when(step == 0)
     def _():
-        small = small_grads(first_ref, second_ref, w_ref, embed_ref, ff_ref, va_ref, vb_ref, up_ref)
+        small = small_grads(first_ref, sa_ref, sb_ref, w_ref, embed_ref, ff_ref, va_ref, vb_ref, up_ref)
         small_ref[...] = small
         extra[...] = small
         for copy in small_copies():
@@ -502,7 +515,7 @@
             copy.wait()
 
 
-def qkv_own_kernel(tbl, low_ref, dqkv_ref, small_ref, got, keep, away, hold, came, sems, came_sems):
+def qkv_own_kernel(tbl, low_ref, dqkv_ref, small_ref, got, keep, away, hold, came, came_sems):
     step = pl.program_id(0)
 
     @pl.when(step == 0)
@@ -514,20 +527,9 @@
 
     rows = pl.ds(pl.multiple_of(step * HALF, HALF), HALF)
     cols = pl.ds(pl.multiple_of(tbl[CORE_AT] * TDIM, TDIM), TDIM)
-    hold[step, :, :QKV] = (tn(low_ref[...], dqkv_ref[...]) + came[rows, :QKV].astype(F32)).astype(BF16)
-    hold[step, :, QKV:] = (small_ref[rows, cols].astype(F32) + came[rows, QKV:].astype(F32)).astype(BF16)
-
-    def each(j, act):
-        for k in range(CHIPS // 2):
-            src = hold.at[j, pl.ds(48 * k, 48), :]
-            leave(tbl, src, j * (CHIPS // 2) + k, keep, away, pl.ds(0, QKV + TDIM), sems.at[j, k], act)
-
-    each(step, start)
-
-    @pl.when(step == 1)
-    def _():
-        for j in range(2):
-            each(j, wait)
+    hold[:, :QKV] = (tn(low_ref[...], dqkv_ref[...]) + came[rows, :QKV].astype(F32)).astype(BF16)
+    hold[:, QKV:] = (small_ref[rows, cols].astype(F32) + came[rows, QKV:].astype(F32)).astype(BF16)
+    leave(tbl, hold, step * (CHIPS // 2), CHIPS // 2, keep, away, pl.ds(0, QKV + TDIM))
 
 
 def input_grad_kernel(df_ref, dqkv_ref, w_ref, ig_ref):
@@ -576,21 +578,23 @@
         [rows_spec(BLOCK, D), rows_spec(BLOCK, slots), whole_spec((slots, TDIM))] + [ANY] * 4,
         [rows_spec(BLOCK, D), rows_spec(BLOCK, D), rows_spec(BLOCK, 2 * QKV), whole_spec((16, D)), ANY],
         [sds((rows, D), F32), sds((rows, D), BF16), sds((rows, 2 * QKV), BF16), sds((16, D), F32), sds((D, 2 * QKV), BF16)],
-        [pltpu.VMEM((D, 2 * QKV + 2 * TDIM), BF16), pltpu.SemaphoreType.DMA((2, 32)), pltpu.SemaphoreType.DMA((1,))],
+        [pltpu.VMEM((D, 2 * QKV + 2 * TDIM), BF16), pltpu.VMEM((1, 2 * QKV), F32), pltpu.VMEM((1, 2 * QKV), F32),
+         pltpu.SemaphoreType.DMA((2, 32)), pltpu.SemaphoreType.DMA((1,))],
         6 * rows * D * D, 20 << 20, (tbl, x, pick, embed, *pieces),
     )
 
 
-def attend(block, qkv, segc, segr, before):
+def attend(block, qkv, pick, segr, before):
     rows = qkv.shape[0]
     return call(
-        attend_kernel, "attend", (1,),
-        [block_spec((BLOCK, 2 * QKV), block), block_spec((BLOCK, 1), block), block_spec((1, 1, BLOCK), block)]
-        + [ANY] * len(before),
-        [block_spec((BLOCK, D), block), block_spec((1, HEADS // 2, 4, 256, 256), block)],
+        functools.partial(attend_kernel, block), "attend", (1,),
+        [block_spec((BLOCK, 2 * QKV), block), block_spec((BLOCK, pick.shape[1]), block),
+         block_spec((1, 1, BLOCK), block)] + [ANY] * len(before),
+        [block_spec((BLOCK, D), block), ANY],
         [sds((rows, D), BF16), sds((rows // BLOCK, HEADS // 2, 4, 256, 256), BF16)],
-        [pltpu.VMEM((4, 256, 128), F32), pltpu.VMEM((2, 256, 256), F32)],
-        4 * BLOCK * D * D, 20 << 20, (qkv, segc, segr, *before), prefetch=0,
+        [pltpu.VMEM((4, 256, 128), F32), pltpu.VMEM((2, 256, 256), F32), pltpu.VMEM((2, 4, 256, 256), BF16),
+         pltpu.SemaphoreType.DMA((2,))],
+        4 * BLOCK * D * D, 20 << 20, (qkv, pick, segr, *before), prefetch=0,
         alias={3 + i: i for i in range(len(before))},
     )
 
@@ -617,12 +621,13 @@
     return call(
         contract_kernel, "contract", (rows // tile,),
         [rows_spec(tile, D), rows_spec(tile, 1), rows_spec(tile, D), whole_spec((16, D)), rows_spec(tile, FF),
-         rows_spec(tile, FF), whole_spec((D, FF)), rows_spec(tile, slots)] + [ANY] * 4,
+         rows_spec(tile, FF), ANY, rows_spec(tile, slots)] + [ANY] * 4,
         [rows_spec(tile, D), rows_spec(tile, FF), rows_spec(tile, D), rows_spec(tile, D), rows_spec(tile, D),
          whole_spec((8, D)), whole_spec((1, FF)), whole_spec((slots, D))],
         [sds((rows, D), BF16), sds((rows, FF), BF16), sds((rows, D), BF16), sds((rows, D), F32), sds((rows, D), BF16),
          sds((8, D), F32), sds((1, FF), F32), sds((slots, D), F32)],
-        [pltpu.VMEM((FF, D), BF16), pltpu.VMEM((2, tile, D), F32), pltpu.SemaphoreType.DMA((1, 32))],
+        [pltpu.VMEM((FF, D), BF16), pltpu.VMEM((D, FF), BF16), pltpu.VMEM((2, tile, D), F32), pltpu.SemaphoreType.DMA((1, 32)),
+         pltpu.SemaphoreType.DMA((1,))],
         6 * rows * D * FF, 20 << 20, (tbl, n1, i1, cot, vec, act, slope, up, pick, *down),
     )
 
@@ -658,9 +663,8 @@
     rows = mlow.shape[0]
     shape = sds((CHIPS // 2, 48, 2 * D + HALF), BF16)
     return call(
-        up_own_kernel, "up_own", (3,), up_specs(rows, 0) + [ANY], [ANY, ANY], [shape, shape],
-        [pltpu.VMEM((3, D, D), BF16), pltpu.VMEM((D, 2 * D + HALF), BF16), pltpu.SemaphoreType.DMA((3, CHIPS)),
-         pltpu.SemaphoreType.DMA((CHIPS,))],
+        up_own_kernel, "up_own", (3,), up_specs(rows, 0) + [ANY], [whole_spec(shape.shape)] * 2, [shape, shape],
+        [pltpu.VMEM((D, D), BF16), pltpu.VMEM((D, 2 * D + HALF), BF16), pltpu.SemaphoreType.DMA((CHIPS,))],
         rows * D * (FF + D), 20 << 20, (tbl, mlow, dexp, mix, ain, got),
     )
 
@@ -672,18 +676,18 @@
     return [pl.BlockSpec((rows, HALF), lambda i, tbl: (0, i)), pl.BlockSpec((rows, QKV), lambda i, tbl: (0, half(tbl)))]
 
 
-def qkv_other(tbl, low, dqkv, first, second, weight, embed, ff, va, vb, up):
+def qkv_other(tbl, low, dqkv, first, sa, sb, weight, embed, ff, va, vb, up):
     rows = low.shape[0]
     slots = first.shape[0]
     return call(
         qkv_other_kernel, "qkv_other", (2,),
-        qkv_specs(rows, 1) + [whole_spec((slots, D)), whole_spec((slots, 2 * QKV)), whole_spec((D, 2 * QKV)),
+        qkv_specs(rows, 1) + [whole_spec((slots, D)), whole_spec((slots, 2 * QKV)), whole_spec((slots, 2 * QKV)), whole_spec((D, 2 * QKV)),
                               whole_spec((slots, TDIM)), whole_spec((8, D)), whole_spec((8, D)), whole_spec((8, D)),
                               whole_spec((4, D))],
         [whole_spec((D, 2 * TDIM)), ANY], [sds((D, 2 * TDIM), BF16), sds((CHIPS, 48, QKV + TDIM), BF16)],
         [pltpu.VMEM((2, HALF, QKV), BF16), pltpu.VMEM((D, 2 * TDIM), BF16), pltpu.SemaphoreType.DMA((2, CHIPS // 2)),
          pltpu.SemaphoreType.DMA((CHIPS,))],
-        3 * rows * D * D, 20 << 20, (tbl, low, dqkv, first, second, weight, embed, ff, va, vb, up),
+        3 * rows * D * D, 20 << 20, (tbl, low, dqkv, first, sa, sb, weight, embed, ff, va, vb, up),
     )
 
 
@@ -691,9 +695,9 @@
     rows = low.shape[0]
     shape = sds((CHIPS // 2, 48, QKV + TDIM), BF16)
     return call(
-        qkv_own_kernel, "qkv_own", (2,), qkv_specs(rows, 0) + [whole_spec((D, 2 * TDIM)), ANY], [ANY, ANY], [shape, shape],
-        [pltpu.VMEM((2, HALF, QKV + TDIM), BF16), pltpu.VMEM((D, QKV + TDIM), BF16),
-         pltpu.SemaphoreType.DMA((2, CHIPS // 2)), pltpu.SemaphoreType.DMA((CHIPS,))],
+        qkv_own_kernel, "qkv_own", (2,), qkv_specs(rows, 0) + [whole_spec((D, 2 * TDIM)), ANY],
+        [whole_spec(shape.shape)] * 2, [shape, shape],
+        [pltpu.VMEM((HALF, QKV + TDIM), BF16), pltpu.VMEM((D, QKV + TDIM), BF16), pltpu.SemaphoreType.DMA((CHIPS,))],
         3 * rows * D * D, 20 << 20, (tbl, low, dqkv, small, got),
     )
 
@@ -773,20 +777,43 @@
     return lax.ppermute(value, "fsdp", perm=tiled_route(n)[step])
 
 
-def chip_shards(halves_of_groups, n):
-    core = lax.axis_index("fsdp") % 2
-    mine, theirs = own_half(
-        [jnp.concatenate([halves[h].reshape(-1, HALF) for halves in halves_of_groups], axis=0) for h in range(2)], core
+def halves_kernel(core_ref, q, k, v, o, up, down, time, columns, mine_a, mine_u, mine_d, theirs):
+    core = core_ref[0]
+    rows = q.shape[0]
+
+    def half(ref, which, width):
+        return ref[:, pl.ds(pl.multiple_of(which * width, 128), width)]
+
+    for which, first in ((core, True), (1 - core, False)):
+        tail = jnp.where(which == 0, time[...].astype(F32), columns[...].astype(F32)).astype(BF16)
+        a = [half(q, which, HALF), half(k, which, HALF), half(v, which, HALF), tail]
+        u = [half(up, which, FF // 2), half(o, which, HALF)]
+        d = half(down, which, HALF)
+        if first:
+            mine_a[...] = jnp.concatenate(a, axis=1)
+            mine_u[...] = jnp.concatenate(u, axis=1)
+            mine_d[...] = d
+        else:
+            d = [d[rows * j : rows * j + rows, :] for j in range(d.shape[0] // rows)]
+            theirs[...] = jnp.concatenate(a + u + d, axis=1)
+
+
+def chip_shards(core, q, k, v, o, up, down, time, columns, n):
+    rows = q.shape[0]
+    down_rows = down.shape[0]
+    widths = (QKV + TDIM, FF // 2 + HALF, HALF * down_rows // rows)
+    args = (q, k, v, o, up, down, time, columns)
+    shapes = [sds((rows, widths[0]), BF16), sds((rows, widths[1]), BF16), sds((down_rows, HALF), BF16), sds((rows, sum(widths)), BF16)]
+    mine_a, mine_u, mine_d, theirs = call(
+        halves_kernel, "halves", (1,), [whole_spec(item.shape) for item in args], [whole_spec(item.shape) for item in shapes],
+        shapes, [], 1 << 10, 1 << 20, (core.reshape(1), *args),
     )
     got = send_on(theirs, "core", n)
-    first, second = own_half((mine, got), core)
-    shards, at = [], 0
-    for halves in halves_of_groups:
-        rows, cols = halves[0].shape
-        count = rows * cols // HALF
-        parts = [item[at : at + count].reshape(rows, cols) for item in (first, second)]
-        shards.append(jnp.concatenate(parts, axis=0)[None])
-        at += count
+    got_d = got[:, widths[0] + widths[1] :]
+    got_d = jnp.concatenate([got_d[:, HALF * j : HALF * j + HALF] for j in range(down_rows // rows)], axis=0)
+    shards = []
+    for mine, came in ((mine_a, got[:, : widths[0]]), (mine_u, got[:, widths[0] : widths[0] + widths[1]]), (mine_d, got_d)):
+        shards.append(jnp.concatenate(own_half((mine, came), core), axis=0)[None])
     return shards
 
 
@@ -866,20 +893,25 @@
     ]
     down_halves = [down_weight[:, :HALF], down_weight[:, HALF:]]
 
-    ends = jnp.cumsum(lengths, axis=1)
-    position = jnp.arange(BLOCK, dtype=jnp.int32)
-    owner = jnp.sum((position[None, :, None] >= ends[:, None, :]).astype(jnp.int32), axis=2)
-    pick = (owner[:, :, None] == jnp.arange(SLOTS, dtype=jnp.int32)).astype(BF16)
-    pick = (pick[:, :, None, :] * jnp.eye(blocks, dtype=BF16)[:, None, :, None]).reshape(rows, blocks * SLOTS)
-    segc = owner.reshape(rows, 1)
-    segr = owner.reshape(blocks, 1, BLOCK)
-    embed_in = sinusoid(timesteps.reshape(-1)).astype(BF16)
     core = lax.axis_index("fsdp") % 2
     tiled = n == 32
 
+    def slot_arrays(lengths, timesteps):
+        ends = jnp.cumsum(lengths, axis=1)
+        position = jnp.arange(BLOCK, dtype=jnp.int32)
+        owner = jnp.sum((position[None, :, None] >= ends[:, None, :]).astype(jnp.int32), axis=2)
+        slot_of = (owner + SLOTS * jnp.arange(blocks, dtype=jnp.int32)[:, None]).reshape(rows, 1)
+        pick = (slot_of == lax.broadcasted_iota(jnp.int32, (rows, blocks * SLOTS), 1)).astype(BF16)
+        segr = slot_of.reshape(blocks, 1, BLOCK).astype(F32)
+        embed_in = sinusoid(timesteps.reshape(-1)).astype(BF16)
+        return pick, segr, embed_in
+
     if tiled:
-        a0, u0, d0 = chip_shards((attn_halves, up_halves, down_halves), n)
+        a0, u0, d0 = chip_shards(
+            core, query_weight, key_weight, value_weight, out_weight, up_weight, down_weight, time_weight.T, columns, n
+        )
         a0 = widen(a0, "z2", n)
+        pick, segr, embed_in = slot_arrays(*follow(a0, lengths, timesteps))
         a0 = widen(a0, "z1", n)
         (u0,) = follow(a0, u0)
         a0 = widen(a0, "a", n)
@@ -888,7 +920,7 @@
         a1 = send_on(a0, "b", n)
         a2 = send_on(a0, "core", n)
         u0 = widen(u0, "z1", n)
-        a1, u0, d0 = tie(a1, u0, d0)
+        a1, u0, d0, tbl, pick, segr, embed_in = tie(a1, u0, d0, tbl, pick, segr, embed_in)
         a3 = send_on(a1, "core", n)
         u_got = send_on(u0, "a", n)
         d_got = send_on(d0, "z2", n)
@@ -899,11 +931,11 @@
         u1 = send_on(u0, "b", n)
         d_got = send_on(d0, "z1", n)
         u2 = send_on(u0, "core", n)
-        parts = attend(0, qkv, segc, segr, ())
+        parts = attend(0, qkv, pick, segr, ())
         *parts, qkv, u0, u2, d0, d_got = tie(*parts, qkv, u0, u2, d0, d_got)
         d0 = jnp.concatenate([d0, d_got], axis=0)
         d_got = send_on(d0, "a", n)
-        mix, probs = attend(1, qkv, segc, segr, parts)
+        mix, probs = attend(1, qkv, pick, segr, parts)
         mix, u1, d0, d_got = tie(mix, u1, d0, d_got)
         u3 = send_on(u1, "core", n)
         d0 = jnp.concatenate([d0, d_got], axis=0)
@@ -915,8 +947,9 @@
         d3 = send_on(d1, "core", n)
         down_pieces = (d0, d1, d2, d3)
     else:
+        pick, segr, embed_in = slot_arrays(lengths, timesteps)
         hidden, low, qkv, vec, weight = project(tbl, inputs, pick, embed_in, whole_gather(attn_halves, core))
-        mix, probs = attend(1, qkv, segc, segr, attend(0, qkv, segc, segr, ()))
+        mix, probs = attend(1, qkv, pick, segr, attend(0, qkv, pick, segr, ()))
         up_offset = vec[9:13].reshape(FF // D, n, shard).transpose(1, 0, 2).reshape(1, FF)
         n1, i1, act, slope, mlow, up_full = expand(tbl, hidden, mix, vec, up_offset, whole_gather(up_halves, core))
         down_pieces = whole_gather(down_halves, core)
@@ -930,7 +963,7 @@
     u_other = up_other(tbl, mlow, dexp, mix, ain)
     if tiled:
         d_got = send_on(d_other, "core", n)
-        u_other, d_own, d_got, mlow = tie(u_other, d_own, d_got, mlow)
+        u_other, d_own, d_got, mlow, up_vec = tie(u_other, d_own, d_got, mlow, up_vec)
         u_got = send_on(u_other, "core", n)
         d_keep, d_away = halve(d_own, d_got)
         d_keep, d_away, u_got = tie(d_keep, d_away, u_got)
@@ -951,7 +984,7 @@
         u_got = send_on(u_away, "a", n)
         d_got = send_on(d_away, "z1", n)
         small, q_other = qkv_other(
-            tbl, low, dqkv, slot_first, slot0 + slot1, weight, embed_in, ff_vecs, vg0, vg1, up_vec
+            tbl, low, dqkv, slot_first, slot0, slot1, weight, embed_in, ff_vecs, vg0, vg1, up_vec
         )
         q_other, u_keep, u_got, d_keep, d_got, low = tie(q_other, u_keep, u_got, d_keep, d_got, low)
         q_got = send_on(q_other, "core", n)
@@ -982,7 +1015,7 @@
         dqkv, vg0, slot0 = attention_backward(0, ain, mix, qkv, probs, up_full, pick, ())
         dqkv, vg1, slot1 = attention_backward(1, ain, mix, qkv, probs, up_full, pick, (dqkv,))
         small, q_other = qkv_other(
-            tbl, low, dqkv, slot_first, slot0 + slot1, weight, embed_in, ff_vecs, vg0, vg1, up_vec
+            tbl, low, dqkv, slot_first, slot0, slot1, weight, embed_in, ff_vecs, vg0, vg1, up_vec
         )
         input_grad = input_gradient(df, dqkv, weight)
         down_sum = whole_reduce(d_own, d_other, core)

time: 317 us -> 300 us (0.946); the launches traced: 312 us -> 299 us
  Pallas kernels: 169 us -> 162 us
  local copies, waits for them, and re-layouts: 22.6 us -> 17.1 us
  waiting for transfers between devices: 53 us -> 49.2 us
    pallas_call x13 -> x14, Pallas kernels: 169 us -> 162 us  [call(): pl.pallas_call(kernel, name=name, grid_spec=pltpu.PrefetchScalarGridSpec(...]
    ppermute x37, waiting for transfers between devices: 53 us -> 49.2 us  [send_on(): return lax.ppermute(value, 'fsdp', perm=tiled_route(n)[step])]
    slice x11 -> x1, local copies, waits for them, and re-layouts: 3.28 us -> 0.01 us  [chip_shards(): got_d[:, HALF * j:HALF * j + HALF]]
  transfers between devices with their start and end apart: 37 -> 37, of which waited for: 16 -> 17; matrix products, arithmetic and copies ran while one was open for 11% -> 11% of each run, Pallas kernels for 41% -> 40%
where the time goes in v1:
time: 300 us; the launch traced here: 299 us
  Pallas kernels  162 us (54%)
  waiting for transfers between devices  49.2 us (16%)
  starting transfers between devices  37.3 us (12%)
  other arithmetic  32 us (11%)
  local copies, waits for them, and re-layouts  17.1 us (6%)
    pallas_call x14, Pallas kernels, call(): pl.pallas_call(kernel, name=name, grid_spec=pltpu.PrefetchScalarGridSpec(...  162 us
    ppermute x37, waiting for transfers between devices, send_on(): return lax.ppermute(value, 'fsdp', perm=tiled_route(n)[step])  49.2 us
    ppermute x37, starting transfers between devices, send_on(): return lax.ppermute(value, 'fsdp', perm=tiled_route(n)[step])  37.3 us
    convert_element_type x10, other arithmetic, add(): return (left.astype(F32) + right.astype(F32)).astype(BF16)  17.9 us
  transfers between devices with their start and end apart: 37, of which 17 were waited for; matrix products, arithmetic and copies ran while one was open for 11% of the time, Pallas kernels for 40%

profile of v1, /device:TPU:0, one launch (start us, length us, event | category | flops | bytes accessed | tf_op | source)
XLA Modules:
  0.0 299.3 jit_solution(3732640495359366892)
XLA Ops:
  7.6 4.0 %collective-permute-start.1 = (bf16[1,48,1280]{2,1,0:T(8,128)(2,1)S(1)}, bf16[1,48,1280]{2,1,0:T(8,128)(2,1)S(1)}, u32[]{:S(2)}, u32[]{:S(2)}) collective-permute-start(bf16[1,48,1280]{2,1,0:T(8,128)(2,1)S(1)} %maximum_bitcast_fusion.2), channel_id=1, source_target_pairs={{0,16},{1,17},{2,18},{3,19},{4,20},{5,21},{6,22},{7,23},{8,24},{9,... | collective-permute-start | bytes 368648 | tf_op jit(solution)/shard_map/ppermute | solution.py:777
  13.5 4.4 %collective-permute-done.1 = bf16[1,48,1280]{2,1,0:T(8,128)(2,1)S(1)} collective-permute-done((bf16[1,48,1280]{2,1,0:T(8,128)(2,1)S(1)}, bf16[1,48,1280]{2,1,0:T(8,128)(2,1)S(1)}, u32[]{:S(2)}, u32[]{:S(2)}) %collective-permute-start.1) | collective-permute-done | bytes 122912 | tf_op jit(solution)/shard_map/ppermute | solution.py:777
  19.0 6.5 %collective-permute-done.2 = bf16[2,48,1280]{2,1,0:T(8,128)(2,1)S(1)} collective-permute-done((bf16[2,48,1280]{2,1,0:T(8,128)(2,1)S(1)}, bf16[2,48,1280]{2,1,0:T(8,128)(2,1)S(1)}, u32[]{:S(2)}, u32[]{:S(2)}) %collective-permute-start.2) | collective-permute-done | bytes 245792 | tf_op jit(solution)/shard_map/ppermute | solution.py:777
  27.0 3.0 %collective-permute-start.4 = (bf16[1,48,1920]{2,1,0:T(8,128)(2,1)S(1)}, bf16[1,48,1920]{2,1,0:T(8,128)(2,1)S(1)}, u32[]{:S(2)}, u32[]{:S(2)}) collective-permute-start(bf16[1,48,1920]{2,1,0:T(8,128)(2,1)S(1)} %maximum_bitcast_fusion), channel_id=1, source_target_pairs={{0,16},{1,17},{2,18},{3,19},{4,20},{5,21},{6,22},{7,23},{8,24},{9,... | collective-permute-start | bytes 552968 | tf_op jit(solution)/shard_map/ppermute | solution.py:777
  30.2 7.9 %collective-permute-done.4 = bf16[1,48,1920]{2,1,0:T(8,128)(2,1)S(1)} collective-permute-done((bf16[1,48,1920]{2,1,0:T(8,128)(2,1)S(1)}, bf16[1,48,1920]{2,1,0:T(8,128)(2,1)S(1)}, u32[]{:S(2)}, u32[]{:S(2)}) %collective-permute-start.4) | collective-permute-done | bytes 184352 | tf_op jit(solution)/shard_map/ppermute | solution.py:777
  42.2 7.4 %collective-permute-done.6 = bf16[2,48,1920]{2,1,0:T(8,128)(2,1)S(1)} collective-permute-done((bf16[2,48,1920]{2,1,0:T(8,128)(2,1)S(1)}, bf16[2,48,1920]{2,1,0:T(8,128)(2,1)S(1)}, u32[]{:S(2)}, u32[]{:S(2)}) %collective-permute-start.6) | collective-permute-done | bytes 368672 | tf_op jit(solution)/shard_map/ppermute | solution.py:777
  49.7 2.7 collective-permute-done.5.own_high
  55.1 12.8 %project.1 = (f32[1024,768]{1,0:T(8,128)}, bf16[1024,768]{1,0:T(8,128)(2,1)}, bf16[1024,2304]{1,0:T(8,128)(2,1)}, f32[16,768]{1,0:T(8,128)}, bf16[768,2304]{1,0:T(8,128)(2,1)}) custom-call(s32[80]{0:T(128)} %concatenate.75.tbl, bf16[1024,768]{1,0:T(8,128)(2,1)} %x_ref.1, bf16[1024,16]{1,0:T(8,128)(2,1)} %fusion.pick_ref, ...), custom_call_target="tpu_custom_call" | custom-call | flops 3623878656 | bytes 20971520 | tf_op jit(solution)/shard_map/project/pallas_call | solution.py:540
  68.9 2.0 constant_dynamic-update-slice_fusion.ua
  72.5 3.8 %collective-permute-start.12 = (bf16[2,192,384]{2,1,0:T(8,128)(2,1)S(1)}, bf16[2,192,384]{2,1,0:T(8,128)(2,1)S(1)}, u32[]{:S(2)}, u32[]{:S(2)}) collective-permute-start(bf16[2,192,384]{2,1,0:T(8,128)(2,1)S(1)} %constant_dynamic-update-slice_fusion.2), channel_id=1, source_target_pairs={{0,8},{1,9},{2,10},{3,11},{4,12},{5,13},{6,14},{7,15},{8,0},{9,1},... | collective-permute-start | bytes 884744 | tf_op jit(solution)/shard_map/ppermute | solution.py:777
  76.4 9.1 %attend.2 = (bf16[1024,768]{1,0:T(8,128)(2,1)}, bf16[2,6,4,256,256]{4,3,2,1,0:T(8,128)(2,1)}) custom-call(bf16[1024,2304]{1,0:T(8,128)(2,1)} %get-tuple-element.174.qkv_ref, bf16[1024,16]{1,0:T(8,128)(2,1)} %fusion.pick_ref, f32[2,1,512]{2,1,0:T(1,128)} %add_convert_fusion.20.segr_ref), custom_call_target="tpu_custom_call" | custom-call | flops 1207959552 | bytes 20971520 | tf_op jit(solution)/shard_map/attend/pallas_call | solution.py:540
  88.7 9.1 %attend.3 = (bf16[1024,768]{1,0:T(8,128)(2,1)}, bf16[2,6,4,256,256]{4,3,2,1,0:T(8,128)(2,1)}) custom-call(bf16[1024,2304]{1,0:T(8,128)(2,1)} %get-tuple-element.174.qkv_ref, bf16[1024,16]{1,0:T(8,128)(2,1)} %fusion.pick_ref, f32[2,1,512]{2,1,0:T(1,128)} %add_convert_fusion.20.segr_ref, ...), custom_call_target="tpu_custom_call", output_to_operand_aliasing={{0}: (3, {}), {1}: (4, {})} | custom-call | flops 1207959552 | bytes 20971520 | tf_op jit(solution)/shard_map/attend/pallas_call | solution.py:540
  103.3 18.6 %expand.1 = (f32[1024,768]{1,0:T(8,128)}, f32[1024,1]{1,0:T(8,128)}, bf16[1024,3072]{1,0:T(8,128)(2,1)}, bf16[1024,3072]{1,0:T(8,128)(2,1)}, bf16[1024,768]{1,0:T(8,128)(2,1)}, /*index=5*/bf16[768,3840]{1,0:T(8,128)(2,1)}) custom-call(s32[80]{0:T(128)} %concatenate.75.tbl, f32[1024,768]{1,0:T(8,128)} %get-tuple-element.162.hidden_ref, ...), custom_call_target="tpu_custom_call" | custom-call | flops 6039797760 | bytes 20971520 | tf_op jit(solution)/shard_map/expand/pallas_call | solution.py:540
  122.5 2.8 collective-permute-done.18.dd
  125.3 30.1 %contract.1 = (bf16[1024,768]{1,0:T(8,128)(2,1)}, bf16[1024,3072]{1,0:T(8,128)(2,1)}, bf16[1024,768]{1,0:T(8,128)(2,1)}, f32[1024,768]{1,0:T(8,128)}, bf16[1024,...) custom-call(s32[80]{0:T(128)} %concatenate.75.tbl, ...), custom_call_target="tpu_custom_call" | custom-call | flops 14495514624 | bytes 20971520 | tf_op jit(solution)/shard_map/contract/pallas_call | solution.py:540
  155.4 10.3 %down_grad.1 = (bf16[16,192,384]{2,1,0:T(8,128)(2,1)}, bf16[16,192,384]{2,1,0:T(8,128)(2,1)}) custom-call(s32[80]{0:T(128)} %concatenate.75.tbl, bf16[1024,3072]{1,0:T(8,128)(2,1)} %get-tuple-element.190.act_ref, bf16[1024,768]{1,0:T(8,128)(2,1)} %get-tuple-element.199.din_ref), custom_call_target="tpu_custom_call" | custom-call | flops 4831838208 | bytes 20971520 | tf_op jit(solution)/shard_map/down_grad/pallas_call | solution.py:540
  168.2 8.5 %up_other.1 = bf16[16,48,1920]{2,1,0:T(8,128)(2,1)} custom-call(s32[80]{0:T(128)} %concatenate.75.tbl, bf16[1024,768]{1,0:T(8,128)(2,1)} %get-tuple-element.207.mlow_ref, bf16[1024,3072]{1,0:T(8,128)(2,1)} %get-tuple-element.203.dexp_ref, bf16[1024,768]{1,0:T(8,128)(2,1)} %get-tuple-element.180.mix_ref, bf16[1024,768]{1,0:T(8,128)(2,1)} %get-tuple-element.222.ain_ref), custom_call_target="tpu_custom_call" | custom-call | flops 3019898880 | bytes 20971520 | tf_op jit(solution)/shard_map/up_other/pallas_call | solution.py:540
  176.8 4.4 %add_convert_fusion = (bf16[8,192,384]{2,1,0:T(8,128)(2,1)}, bf16[8,192,384]{2,1,0:T(8,128)(2,1)}) fusion(bf16[16,192,384]{2,1,0:T(8,128)(2,1)} %collective-permute-done.19, bf16[16,192,384]{2,1,0:T(8,128)(2,1)} %get-tuple-element.208), kind=kLoop, calls=%fused_computation | loop fusion | flops 4718592 | bytes 7077888 | tf_op jit(solution)/shard_map/convert_element_type | solution.py:833
  183.6 12.0 %up_own.1 = (bf16[8,48,1920]{2,1,0:T(8,128)(2,1)}, bf16[8,48,1920]{2,1,0:T(8,128)(2,1)}) custom-call(s32[80]{0:T(128)} %concatenate.75.tbl, bf16[1024,768]{1,0:T(8,128)(2,1)} %get-tuple-element.207.mlow_ref, bf16[1024,3072]{1,0:T(8,128)(2,1)} %get-tuple-element.203.dexp_ref, bf16[1024,768]{1,0:T(8,128)(2,1)} %get-tuple-element.180.mix_ref, ...), custom_call_target="tpu_custom_call" | custom-call | flops 3019898880 | bytes 20971520 | tf_op jit(solution)/shard_map/up_own/pallas_call | solution.py:540
  196.5 11.4 %attention_backward.2 = (bf16[1024,2304]{1,0:T(8,128)(2,1)}, f32[8,768]{1,0:T(8,128)}, f32[16,2304]{1,0:T(8,128)}) custom-call(bf16[1024,768]{1,0:T(8,128)(2,1)} %get-tuple-element.222.ain_ref, bf16[1024,768]{1,0:T(8,128)(2,1)} %get-tuple-element.180.mix_ref, bf16[1024,2304]{1,0:T(8,128)(2,1)} %get-tuple-element.174.qkv_ref, ...), custom_call_target="tpu_custom_call" | custom-call | flops 1207959552 | bytes 20971520 | tf_op jit(solution)/shard_map/attention_backward/pallas_call | solution.py:540
  207.9 2.9 add_convert_fusion.4
  212.1 11.4 %attention_backward.3 = (bf16[1024,2304]{1,0:T(8,128)(2,1)}, f32[8,768]{1,0:T(8,128)}, f32[16,2304]{1,0:T(8,128)}) custom-call(bf16[1024,768]{1,0:T(8,128)(2,1)} %get-tuple-element.222.ain_ref, bf16[1024,768]{1,0:T(8,128)(2,1)} %get-tuple-element.180.mix_ref, bf16[1024,2304]{1,0:T(8,128)(2,1)} %get-tuple-element.174.qkv_ref, ...), custom_call_target="tpu_custom_call", output_to_operand_aliasing={{0}: (6, {})} | custom-call | flops 1207959552 | bytes 20971520 | tf_op jit(solution)/shard_map/attention_backward/pallas_call | solution.py:540
  224.3 3.1 %add_convert_fusion.2 = (bf16[4,48,1920]{2,1,0:T(8,128)(2,1)}, bf16[4,48,1920]{2,1,0:T(8,128)(2,1)S(1)}) fusion(bf16[8,48,1920]{2,1,0:T(8,128)(2,1)} %collective-permute-done.23, bf16[8,48,1920]{2,1,0:T(8,128)(2,1)} %get-tuple-element.232), kind=kLoop, calls=%fused_computation.2 | loop fusion | flops 2949120 | bytes 4423680 | tf_op jit(solution)/shard_map/convert_element_type | solution.py:833
  229.1 2.3 collective-permute-start.25
  231.5 9.7 %qkv_other.1 = (bf16[768,256]{1,0:T(8,128)(2,1)}, bf16[16,48,1280]{2,1,0:T(8,128)(2,1)}) custom-call(s32[80]{0:T(128)} %concatenate.75.tbl, bf16[1024,768]{1,0:T(8,128)(2,1)} %get-tuple-element.249.low_ref, bf16[1024,2304]{1,0:T(8,128)(2,1)} %get-tuple-element.235.dqkv_ref, f32[16,768]{1,0:T(8,128)} %get-tuple-element.236.first_ref, ...), custom_call_target="tpu_custom_call" | custom-call | flops 1811939328 | bytes 20971520 | tf_op jit(solution)/shard_map/qkv_other/pallas_call | solution.py:540
  243.2 2.1 add_convert_fusion.8
  246.9 8.6 %qkv_own.1 = (bf16[8,48,1280]{2,1,0:T(8,128)(2,1)}, bf16[8,48,1280]{2,1,0:T(8,128)(2,1)}) custom-call(s32[80]{0:T(128)} %concatenate.75.tbl, bf16[1024,768]{1,0:T(8,128)(2,1)} %get-tuple-element.249.low_ref, bf16[1024,2304]{1,0:T(8,128)(2,1)} %get-tuple-element.235.dqkv_ref, bf16[768,256]{1,0:T(8,128)(2,1)} %get-tuple-element.250.small_ref, ...), custom_call_target="tpu_custom_call" | custom-call | flops 1811939328 | bytes 20971520 | tf_op jit(solution)/shard_map/qkv_own/pallas_call | solution.py:540
  259.1 2.6 collective-permute-start.34
  261.8 9.1 %input_grad.1 = f32[1024,768]{1,0:T(8,128)} custom-call(f32[1024,768]{1,0:T(8,128)} %get-tuple-element.265.df_ref, bf16[1024,2304]{1,0:T(8,128)(2,1)} %get-tuple-element.235.dqkv_ref, bf16[768,2304]{1,0:T(8,128)(2,1)} %get-tuple-element.239.w_ref), custom_call_target="tpu_custom_call" | custom-call | flops 3623878656 | bytes 20971520 | tf_op jit(solution)/shard_map/input_grad/pallas_call | solution.py:540
  273.8 2.1 collective-permute-done.34
  282.9 5.0 %collective-permute-done.30 = bf16[2,48,1280]{2,1,0:T(8,128)(2,1)S(1)} collective-permute-done((bf16[2,48,1280]{2,1,0:T(8,128)(2,1)S(1)}, bf16[2,48,1280]{2,1,0:T(8,128)(2,1)S(1)}, u32[]{:S(2)}, u32[]{:S(2)}) %collective-permute-start.30) | collective-permute-done | bytes 245792 | tf_op jit(solution)/shard_map/ppermute | solution.py:777
  289.2 4.6 %collective-permute-done.31 = bf16[1,48,1280]{2,1,0:T(8,128)(2,1)S(1)} collective-permute-done((bf16[1,48,1280]{2,1,0:T(8,128)(2,1)S(1)}, bf16[1,48,1280]{2,1,0:T(8,128)(2,1)S(1)}, u32[]{:S(2)}, u32[]{:S(2)}) %collective-permute-start.31) | collective-permute-done | bytes 122912 | tf_op jit(solution)/shard_map/ppermute | solution.py:777
  (180 shorter events, 63.5 us)
Async XLA Ops:
  7.6 10.3 %collective-permute-start.1 = (bf16[1,48,1280]{2,1,0:T(8,128)(2,1)S(1)}, bf16[1,48,1280]{2,1,0:T(8,128)(2,1)S(1)}, u32[]{:S(2)}, u32[]{:S(2)}) collective-permute-start(bf16[1,48,1280]{2,1,0:T(8,128)(2,1)S(1)} %maximum_bitcast_fusion.2), channel_id=1, source_target_pairs={{0,16},{1,17},{2,18},{3,19},{4,20},{5,21},{6,22},{7,23},{8,24},{9,... | collective-permute-start | bytes 368648 | tf_op jit(solution)/shard_map/ppermute | solution.py:777
  18.0 7.6 %collective-permute-start.2 = (bf16[2,48,1280]{2,1,0:T(8,128)(2,1)S(1)}, bf16[2,48,1280]{2,1,0:T(8,128)(2,1)S(1)}, u32[]{:S(2)}, u32[]{:S(2)}) collective-permute-start(bf16[2,48,1280]{2,1,0:T(8,128)(2,1)S(1)} %pad_maximum_fusion.6), channel_id=1, source_target_pairs={{0,8},{1,9},{2,10},{3,11},{4,12},{5,13},{6,14},{7,15},{8,0},{9,1},... | collective-permute-start | bytes 737288 | tf_op jit(solution)/shard_map/ppermute | solution.py:777
  25.6 12.6 %collective-permute-start.3 = (bf16[4,48,1280]{2,1,0:T(8,128)(2,1)S(1)}, bf16[4,48,1280]{2,1,0:T(8,128)(2,1)S(1)}, u32[]{:S(2)}, u32[]{:S(2)}) collective-permute-start(bf16[4,48,1280]{2,1,0:T(8,128)(2,1)S(1)} %pad_maximum_fusion.2), channel_id=1, source_target_pairs={{0,2},{1,5},{2,0},{3,7},{4,6},{5,1},{6,4},{7,3},{8,10},{9,13},{10,... | collective-permute-start | bytes 1474568 | tf_op jit(solution)/shard_map/ppermute | solution.py:777
  27.0 11.0 %collective-permute-start.4 = (bf16[1,48,1920]{2,1,0:T(8,128)(2,1)S(1)}, bf16[1,48,1920]{2,1,0:T(8,128)(2,1)S(1)}, u32[]{:S(2)}, u32[]{:S(2)}) collective-permute-start(bf16[1,48,1920]{2,1,0:T(8,128)(2,1)S(1)} %maximum_bitcast_fusion), channel_id=1, source_target_pairs={{0,16},{1,17},{2,18},{3,19},{4,20},{5,21},{6,22},{7,23},{8,24},{9,... | collective-permute-start | bytes 552968 | tf_op jit(solution)/shard_map/ppermute | solution.py:777
  38.3 14.2 %collective-permute-start.5 = (bf16[8,48,1280]{2,1,0:T(8,128)(2,1)S(1)}, bf16[8,48,1280]{2,1,0:T(8,128)(2,1)S(1)}, u32[]{:S(2)}, u32[]{:S(2)}) collective-permute-start(bf16[8,48,1280]{2,1,0:T(8,128)(2,1)S(1)} %pad_maximum_fusion.own_low), channel_id=1, source_target_pairs={{0,4},{1,3},{2,6},{3,1},{4,0},{5,7},{6,2},{7,5},{8,12},{9,11},{10,... | collective-permute-start | bytes 2949128 | tf_op jit(solution)/shard_map/ppermute | solution.py:777
  38.9 10.7 %collective-permute-start.6 = (bf16[2,48,1920]{2,1,0:T(8,128)(2,1)S(1)}, bf16[2,48,1920]{2,1,0:T(8,128)(2,1)S(1)}, u32[]{:S(2)}, u32[]{:S(2)}) collective-permute-start(bf16[2,48,1920]{2,1,0:T(8,128)(2,1)S(1)} %pad_maximum_fusion.3), channel_id=1, source_target_pairs={{0,8},{1,9},{2,10},{3,11},{4,12},{5,13},{6,14},{7,15},{8,0},{9,1},... | collective-permute-start | bytes 1105928 | tf_op jit(solution)/shard_map/ppermute | solution.py:777
  41.8 12.2 %collective-permute-start.7 = (bf16[8,48,1280]{2,1,0:T(8,128)(2,1)S(1)}, bf16[8,48,1280]{2,1,0:T(8,128)(2,1)S(1)}, u32[]{:S(2)}, u32[]{:S(2)}) collective-permute-start(bf16[8,48,1280]{2,1,0:T(8,128)(2,1)S(1)} %pad_maximum_fusion.own_low), channel_id=1, source_target_pairs={{0,1},{1,0},{2,3},{3,2},{4,5},{5,4},{6,7},{7,6},{8,9},{9,8},{10,11... | collective-permute-start | bytes 2949128 | tf_op jit(solution)/shard_map/ppermute | solution.py:777
  52.4 15.5 %collective-permute-start.9 = (bf16[4,48,1920]{2,1,0:T(8,128)(2,1)S(1)}, bf16[4,48,1920]{2,1,0:T(8,128)(2,1)}, u32[]{:S(2)}, u32[]{:S(2)}) collective-permute-start(bf16[4,48,1920]{2,1,0:T(8,128)(2,1)S(1)} %pad_maximum_fusion.1), channel_id=1, source_target_pairs={{0,2},{1,5},{2,0},{3,7},{4,6},{5,1},{6,4},{7,3},{8,10},{9,13},{10,... | collective-permute-start | bytes 2211848 | tf_op jit(solution)/shard_map/ppermute | solution.py:777
  54.0 13.9 %collective-permute-start.10 = (bf16[1,192,384]{2,1,0:T(8,128)(2,1)S(1)}, bf16[1,192,384]{2,1,0:T(8,128)(2,1)}, u32[]{:S(2)}, u32[]{:S(2)}) collective-permute-start(bf16[1,192,384]{2,1,0:T(8,128)(2,1)S(1)} %maximum_bitcast_fusion.1), channel_id=1, source_target_pairs={{0,16},{1,17},{2,18},{3,19},{4,20},{5,21},{6,22},{7,23},{8,24},{9,... | collective-permute-start | bytes 442376 | tf_op jit(solution)/shard_map/ppermute | solution.py:777
  70.9 14.5 %collective-permute-start.11 = (bf16[8,48,1920]{2,1,0:T(8,128)(2,1)}, bf16[8,48,1920]{2,1,0:T(8,128)(2,1)}, u32[]{:S(2)}, u32[]{:S(2)}) collective-permute-start(bf16[8,48,1920]{2,1,0:T(8,128)(2,1)} %constant_dynamic-update-slice_fusion.ua), channel_id=1, source_target_pairs={{0,1},{1,0},{2,3},{3,2},{4,5},{5,4},{6,7},{7,6},{8,9},{9,8},{10,11... | collective-permute-start | bytes 4423688 | tf_op jit(solution)/shard_map/ppermute | solution.py:777
  71.0 26.8 %collective-permute-start.13 = (bf16[8,48,1920]{2,1,0:T(8,128)(2,1)}, bf16[8,48,1920]{2,1,0:T(8,128)(2,1)}, u32[]{:S(2)}, u32[]{:S(2)}) collective-permute-start(bf16[8,48,1920]{2,1,0:T(8,128)(2,1)} %constant_dynamic-update-slice_fusion.ua), channel_id=1, source_target_pairs={{0,4},{1,3},{2,6},{3,1},{4,0},{5,7},{6,2},{7,5},{8,12},{9,11},{10,... | collective-permute-start | bytes 4423688 | tf_op jit(solution)/shard_map/ppermute | solution.py:777
  72.5 12.9 %collective-permute-start.12 = (bf16[2,192,384]{2,1,0:T(8,128)(2,1)S(1)}, bf16[2,192,384]{2,1,0:T(8,128)(2,1)S(1)}, u32[]{:S(2)}, u32[]{:S(2)}) collective-permute-start(bf16[2,192,384]{2,1,0:T(8,128)(2,1)S(1)} %constant_dynamic-update-slice_fusion.2), channel_id=1, source_target_pairs={{0,8},{1,9},{2,10},{3,11},{4,12},{5,13},{6,14},{7,15},{8,0},{9,1},... | collective-permute-start | bytes 884744 | tf_op jit(solution)/shard_map/ppermute | solution.py:777
  87.2 10.6 %collective-permute-start.14 = (bf16[4,192,384]{2,1,0:T(8,128)(2,1)S(1)}, bf16[4,192,384]{2,1,0:T(8,128)(2,1)}, u32[]{:S(2)}, u32[]{:S(2)}) collective-permute-start(bf16[4,192,384]{2,1,0:T(8,128)(2,1)S(1)} %constant_dynamic-update-slice_fusion.4), channel_id=1, source_target_pairs={{0,2},{1,5},{2,0},{3,7},{4,6},{5,1},{6,4},{7,3},{8,10},{9,13},{10,... | collective-permute-start | bytes 1769480 | tf_op jit(solution)/shard_map/ppermute | solution.py:777
  97.8 5.5 %collective-permute-start.15 = (bf16[8,48,1920]{2,1,0:T(8,128)(2,1)}, bf16[8,48,1920]{2,1,0:T(8,128)(2,1)}, u32[]{:S(2)}, u32[]{:S(2)}) collective-permute-start(bf16[8,48,1920]{2,1,0:T(8,128)(2,1)} %collective-permute-done.13.ub), channel_id=1, source_target_pairs={{0,1},{1,0},{2,3},{3,2},{4,5},{5,4},{6,7},{7,6},{8,9},{9,8},{10,11... | collective-permute-start | bytes 4423688 | tf_op jit(solution)/shard_map/ppermute | solution.py:777
  100.7 21.2 %collective-permute-start.16 = (bf16[8,192,384]{2,1,0:T(8,128)(2,1)}, bf16[8,192,384]{2,1,0:T(8,128)(2,1)}, u32[]{:S(2)}, u32[]{:S(2)}) collective-permute-start(bf16[8,192,384]{2,1,0:T(8,128)(2,1)} %constant_dynamic-update-slice_fusion.6.da), channel_id=1, source_target_pairs={{0,4},{1,3},{2,6},{3,1},{4,0},{5,7},{6,2},{7,5},{8,12},{9,11},{10,... | collective-permute-start | bytes 3538952 | tf_op jit(solution)/shard_map/ppermute | solution.py:777
  103.2 19.2 %collective-permute-start.17 = (bf16[8,192,384]{2,1,0:T(8,128)(2,1)}, bf16[8,192,384]{2,1,0:T(8,128)(2,1)}, u32[]{:S(2)}, u32[]{:S(2)}) collective-permute-start(bf16[8,192,384]{2,1,0:T(8,128)(2,1)} %constant_dynamic-update-slice_fusion.6.da), channel_id=1, source_target_pairs={{0,1},{1,0},{2,3},{3,2},{4,5},{5,4},{6,7},{7,6},{8,9},{9,8},{10,11... | collective-permute-start | bytes 3538952 | tf_op jit(solution)/shard_map/ppermute | solution.py:777
  165.7 10.9 %collective-permute-start.19 = (bf16[16,192,384]{2,1,0:T(8,128)(2,1)}, bf16[16,192,384]{2,1,0:T(8,128)(2,1)}, u32[]{:S(2)}, u32[]{:S(2)}) collective-permute-start(bf16[16,192,384]{2,1,0:T(8,128)(2,1)} %get-tuple-element.205), channel_id=1, source_target_pairs={{0,1},{1,0},{2,3},{3,2},{4,5},{5,4},{6,7},{7,6},{8,9},{9,8},{10,11... | collective-permute-start | bytes 7077896 | tf_op jit(solution)/shard_map/ppermute | solution.py:777
  176.6 5.8 %collective-permute-start.20 = (bf16[16,48,1920]{2,1,0:T(8,128)(2,1)}, bf16[16,48,1920]{2,1,0:T(8,128)(2,1)}, u32[]{:S(2)}, u32[]{:S(2)}) collective-permute-start(bf16[16,48,1920]{2,1,0:T(8,128)(2,1)} %up_other.1), channel_id=1, source_target_pairs={{0,1},{1,0},{2,3},{3,2},{4,5},{5,4},{6,7},{7,6},{8,9},{9,8},{10,11... | collective-permute-start | bytes 8847368 | tf_op jit(solution)/shard_map/ppermute | solution.py:777
  182.4 25.5 %collective-permute-start.21 = (bf16[8,192,384]{2,1,0:T(8,128)(2,1)}, bf16[8,192,384]{2,1,0:T(8,128)(2,1)}, u32[]{:S(2)}, u32[]{:S(2)}) collective-permute-start(bf16[8,192,384]{2,1,0:T(8,128)(2,1)} %get-tuple-element.218), channel_id=1, source_target_pairs={{0,4},{1,3},{2,6},{3,1},{4,0},{5,7},{6,2},{7,5},{8,12},{9,11},{10,... | collective-permute-start | bytes 3538952 | tf_op jit(solution)/shard_map/ppermute | solution.py:777
  195.6 27.9 %collective-permute-start.23 = (bf16[8,48,1920]{2,1,0:T(8,128)(2,1)}, bf16[8,48,1920]{2,1,0:T(8,128)(2,1)}, u32[]{:S(2)}, u32[]{:S(2)}) collective-permute-start(bf16[8,48,1920]{2,1,0:T(8,128)(2,1)} %get-tuple-element.228), channel_id=1, source_target_pairs={{0,4},{1,3},{2,6},{3,1},{4,0},{5,7},{6,2},{7,5},{8,12},{9,11},{10,... | collective-permute-start | bytes 4423688 | tf_op jit(solution)/shard_map/ppermute | solution.py:777
  210.8 12.6 %collective-permute-start.22 = (bf16[4,192,384]{2,1,0:T(8,128)(2,1)}, bf16[4,192,384]{2,1,0:T(8,128)(2,1)S(1)}, u32[]{:S(2)}, u32[]{:S(2)}) collective-permute-start(bf16[4,192,384]{2,1,0:T(8,128)(2,1)} %get-tuple-element.226), channel_id=1, source_target_pairs={{0,2},{1,5},{2,0},{3,7},{4,6},{5,1},{6,4},{7,3},{8,10},{9,13},{10,... | collective-permute-start | bytes 1769480 | tf_op jit(solution)/shard_map/ppermute | solution.py:777
  228.4 12.8 %collective-permute-start.24 = (bf16[4,48,1920]{2,1,0:T(8,128)(2,1)}, bf16[4,48,1920]{2,1,0:T(8,128)(2,1)}, u32[]{:S(2)}, u32[]{:S(2)}) collective-permute-start(bf16[4,48,1920]{2,1,0:T(8,128)(2,1)} %get-tuple-element.246), channel_id=1, source_target_pairs={{0,2},{1,5},{2,0},{3,7},{4,6},{5,1},{6,4},{7,3},{8,10},{9,13},{10,... | collective-permute-start | bytes 2211848 | tf_op jit(solution)/shard_map/ppermute | solution.py:777
  229.1 12.0 %collective-permute-start.25 = (bf16[2,192,384]{2,1,0:T(8,128)(2,1)}, bf16[2,192,384]{2,1,0:T(8,128)(2,1)}, u32[]{:S(2)}, u32[]{:S(2)}) collective-permute-start(bf16[2,192,384]{2,1,0:T(8,128)(2,1)} %get-tuple-element.248), channel_id=1, source_target_pairs={{0,8},{1,9},{2,10},{3,11},{4,12},{5,13},{6,14},{7,15},{8,0},{9,1},... | collective-permute-start | bytes 884744 | tf_op jit(solution)/shard_map/ppermute | solution.py:777
  241.2 4.4 %collective-permute-start.26 = (bf16[16,48,1280]{2,1,0:T(8,128)(2,1)}, bf16[16,48,1280]{2,1,0:T(8,128)(2,1)}, u32[]{:S(2)}, u32[]{:S(2)}) collective-permute-start(bf16[16,48,1280]{2,1,0:T(8,128)(2,1)} %get-tuple-element.251), channel_id=1, source_target_pairs={{0,1},{1,0},{2,3},{3,2},{4,5},{5,4},{6,7},{7,6},{8,9},{9,8},{10,11... | collective-permute-start | bytes 5898248 | tf_op jit(solution)/shard_map/ppermute | solution.py:777
  245.5 11.0 %collective-permute-start.27 = (bf16[2,48,1920]{2,1,0:T(8,128)(2,1)}, bf16[2,48,1920]{2,1,0:T(8,128)(2,1)S(1)}, u32[]{:S(2)}, u32[]{:S(2)}) collective-permute-start(bf16[2,48,1920]{2,1,0:T(8,128)(2,1)} %get-tuple-element.260), channel_id=1, source_target_pairs={{0,8},{1,9},{2,10},{3,11},{4,12},{5,13},{6,14},{7,15},{8,0},{9,1},... | collective-permute-start | bytes 1105928 | tf_op jit(solution)/shard_map/ppermute | solution.py:777
  256.5 14.4 %collective-permute-start.28 = (bf16[8,48,1280]{2,1,0:T(8,128)(2,1)}, bf16[8,48,1280]{2,1,0:T(8,128)(2,1)}, u32[]{:S(2)}, u32[]{:S(2)}) collective-permute-start(bf16[8,48,1280]{2,1,0:T(8,128)(2,1)} %get-tuple-element.267), channel_id=1, source_target_pairs={{0,4},{1,3},{2,6},{3,1},{4,0},{5,7},{6,2},{7,5},{8,12},{9,11},{10,... | collective-permute-start | bytes 2949128 | tf_op jit(solution)/shard_map/ppermute | solution.py:777
  258.9 17.1 %collective-permute-start.33 = (bf16[1,48,1920]{2,1,0:T(8,128)(2,1)}, bf16[1,48,1920]{2,1,0:T(8,128)(2,1)}, u32[]{:S(2)}, u32[]{:S(2)}) collective-permute-start(bf16[1,48,1920]{2,1,0:T(8,128)(2,1)} %get-tuple-element.272), channel_id=1, source_target_pairs={{0,16},{1,17},{2,18},{3,19},{4,20},{5,21},{6,22},{7,23},{8,24},{9,... | collective-permute-start | bytes 552968 | tf_op jit(solution)/shard_map/ppermute | solution.py:777
  259.1 16.8 %collective-permute-start.34 = (bf16[1,192,384]{2,1,0:T(8,128)(2,1)}, bf16[1,192,384]{2,1,0:T(8,128)(2,1)}, u32[]{:S(2)}, u32[]{:S(2)}) collective-permute-start(bf16[1,192,384]{2,1,0:T(8,128)(2,1)} %get-tuple-element.274), channel_id=1, source_target_pairs={{0,16},{1,17},{2,18},{3,19},{4,20},{5,21},{6,22},{7,23},{8,24},{9,... | collective-permute-start | bytes 442376 | tf_op jit(solution)/shard_map/ppermute | solution.py:777
  272.4 8.9 %collective-permute-start.29 = (bf16[4,48,1280]{2,1,0:T(8,128)(2,1)S(1)}, bf16[4,48,1280]{2,1,0:T(8,128)(2,1)S(1)}, u32[]{:S(2)}, u32[]{:S(2)}) collective-permute-start(bf16[4,48,1280]{2,1,0:T(8,128)(2,1)S(1)} %get-tuple-element.295), channel_id=1, source_target_pairs={{0,2},{1,5},{2,0},{3,7},{4,6},{5,1},{6,4},{7,3},{8,10},{9,13},{10,... | collective-permute-start | bytes 1474568 | tf_op jit(solution)/shard_map/ppermute | solution.py:777
  278.0 4.8 %collective-permute-start.35 = (bf16[24,1920]{1,0:T(8,128)(2,1)S(1)}, bf16[24,1920]{1,0:T(8,128)(2,1)S(1)}, u32[]{:S(2)}, u32[]{:S(2)}) collective-permute-start(bf16[24,1920]{1,0:T(8,128)(2,1)S(1)} %fusion.1), channel_id=1, source_target_pairs={{0,1},{1,0},{2,3},{3,2},{4,5},{5,4},{6,7},{7,6},{8,9},{9,8},{10,11... | collective-permute-start | bytes 276488 | tf_op jit(solution)/shard_map/ppermute | solution.py:777
  281.4 6.4 %collective-permute-start.30 = (bf16[2,48,1280]{2,1,0:T(8,128)(2,1)S(1)}, bf16[2,48,1280]{2,1,0:T(8,128)(2,1)S(1)}, u32[]{:S(2)}, u32[]{:S(2)}) collective-permute-start(bf16[2,48,1280]{2,1,0:T(8,128)(2,1)S(1)} %get-tuple-element.301), channel_id=1, source_target_pairs={{0,8},{1,9},{2,10},{3,11},{4,12},{5,13},{6,14},{7,15},{8,0},{9,1},... | collective-permute-start | bytes 737288 | tf_op jit(solution)/shard_map/ppermute | solution.py:777
  287.9 5.8 %collective-permute-start.31 = (bf16[1,48,1280]{2,1,0:T(8,128)(2,1)S(1)}, bf16[1,48,1280]{2,1,0:T(8,128)(2,1)S(1)}, u32[]{:S(2)}, u32[]{:S(2)}) collective-permute-start(bf16[1,48,1280]{2,1,0:T(8,128)(2,1)S(1)} %add_convert_fusion.18), channel_id=1, source_target_pairs={{0,16},{1,17},{2,18},{3,19},{4,20},{5,21},{6,22},{7,23},{8,24},{9,... | collective-permute-start | bytes 368648 | tf_op jit(solution)/shard_map/ppermute | solution.py:777
  (21 other events, 154.7 us)

commit v2 on v1

--- a/solution.py
+++ b/solution.py
@@ -43,6 +43,11 @@
     return lax.dot_general(left, right, (((0,), (0,)), ((), ())), preferred_element_type=F32)
 
 
+def in_halves(product, left, right):
+    middle = left.shape[0] // 2
+    return jnp.concatenate([product(left[:middle], right), product(left[middle:], right)], axis=0)
+
+
 def mean(values):
     return jnp.sum(values, axis=-1, keepdims=True) * (1.0 / D)
 
@@ -124,13 +129,10 @@
     hidden_ref[...] = x_ref[...].astype(F32) + slot
     low_ref[...] = hidden_ref[...].astype(BF16)
 
-    def chunk(j, carry):
-        at = pl.ds(pl.multiple_of(j * D, D), D)
+    for j in range(3):
+        at = slice(j * D, j * D + D)
         y = nn(low_ref[...], weight[:, at]) + offset[:, at]
         qkv_ref[:, at] = (y.astype(BF16).astype(F32) * factor[:, at]).astype(BF16)
-        return carry
-
-    lax.fori_loop(0, 3, chunk, 0)
 
     @pl.when(step == pl.num_programs(0) - 1)
     def _():
@@ -155,7 +157,8 @@
         at, window = operands(p, t)
         q = qkv_ref[128 * t : 128 * t + 128, pl.ds(at, 128)]
         k = qkv_ref[window, pl.ds(at + HALF, 128)]
-        s = nt(k, jnp.concatenate([q * first, q * second], axis=0)) + jnp.concatenate([bias[t], bias[t]], axis=1)
+        both = jnp.concatenate([q * first, q * second], axis=0)
+        s = in_halves(nt, k, both) + jnp.concatenate([bias[t], bias[t]], axis=1)
         scores[t % 2] = s
         return jnp.max(s, axis=0, keepdims=True)
 
@@ -174,8 +177,8 @@
             e = jnp.exp(scores[t % 2] - peak)
             probs = (e * (1.0 / jnp.sum(e, axis=0, keepdims=True))).astype(BF16)
             held[p % 2, t] = probs
-            out = tn(v, probs)
-            out = jnp.concatenate([out[:HEAD, :128], out[HEAD:, 128:]], axis=0)
+            turned = v.T
+            out = jnp.concatenate([nn(turned[:HEAD], probs[:, :128]), nn(turned[HEAD:], probs[:, 128:])], axis=0)
             mix_ref[128 * t : 128 * t + 128, pl.ds(pl.multiple_of(p * 128, 128), 128)] = out.T.astype(BF16)
             peak = ahead
         out_copy(p).start()
@@ -322,17 +325,29 @@
                 copy.wait()
 
 
-def product_for(step, mlow_ref, dexp_ref, mix_ref, ain_ref, give):
+def product_for(step, half, mlow_ref, dexp_ref, mix_all, ain_all, mix, ain, sems, give):
+    fetches = [
+        pltpu.make_async_copy(mix_all, mix, sems.at[0]),
+        pltpu.make_async_copy(ain_all.at[:, pl.ds(pl.multiple_of(half * HALF, HALF), HALF)], ain, sems.at[1]),
+    ]
+
+    @pl.when(step == 0)
+    def _():
+        for fetch in fetches:
+            fetch.start()
+
     @pl.when(step < 2)
     def _():
         give(tn(mlow_ref[...], dexp_ref[...]), pl.ds(pl.multiple_of(step * D, D), D), D)
 
     @pl.when(step == 2)
     def _():
-        give(tn(mix_ref[...], ain_ref[...]), pl.ds(2 * D, HALF), HALF)
-
-
-def up_other_kernel(tbl, mlow_ref, dexp_ref, mix_ref, ain_ref, other, hold, sems):
+        for fetch in fetches:
+            fetch.wait()
+        give(tn(mix[...], ain[...]), pl.ds(2 * D, HALF), HALF)
+
+
+def up_other_kernel(tbl, mlow_ref, dexp_ref, mix_all, ain_all, other, hold, mix, ain, sems, fetch_sems):
     step = pl.program_id(0)
 
     def copies(j, width):
@@ -348,7 +363,7 @@
         for copy in copies(step, width):
             copy.start()
 
-    product_for(step, mlow_ref, dexp_ref, mix_ref, ain_ref, give)
+    product_for(step, 1 - tbl[CORE_AT], mlow_ref, dexp_ref, mix_all, ain_all, mix, ain, fetch_sems, give)
 
     @pl.when(step == 2)
     def _():
@@ -383,7 +398,7 @@
     lax.fori_loop(0, count, one, 0)
 
 
-def up_own_kernel(tbl, mlow_ref, dexp_ref, mix_ref, ain_ref, got, keep, away, hold, came, came_sems):
+def up_own_kernel(tbl, mlow_ref, dexp_ref, mix_all, ain_all, got, keep, away, hold, came, mix, ain, came_sems, fetch_sems):
     step = pl.program_id(0)
 
     @pl.when(step == 0)
@@ -397,11 +412,17 @@
         hold[:, :width] = (grad + came[:, cols].astype(F32)).astype(BF16)
         leave(tbl, hold.at[:, pl.ds(0, width)], 0, CHIPS, keep, away, cols)
 
-    product_for(step, mlow_ref, dexp_ref, mix_ref, ain_ref, give)
-
-
-def attention_backward_kernel(ain_ref, mix_ref, qkv_ref, probs_ref, w_ref, pick_ref, *rest):
-    dqkv_ref, vg_ref, slot_ref, d_mix, delta, d_probs, dk, dv = rest[-8:]
+    product_for(step, tbl[CORE_AT], mlow_ref, dexp_ref, mix_all, ain_all, mix, ain, fetch_sems, give)
+
+
+def attention_backward_kernel(block, ain_ref, mix_ref, qkv_all, probs_all, w_ref, pick_ref, *rest):
+    dqkv_ref, slot_ref, d_mix, delta, d_probs, dk, dv, qkv_ref, probs_ref, sems = rest[-10:]
+    fetches = [
+        pltpu.make_async_copy(qkv_all.at[pl.ds(block * BLOCK, BLOCK), :], qkv_ref, sems.at[0]),
+        pltpu.make_async_copy(probs_all.at[block], probs_ref, sems.at[1]),
+    ]
+    for fetch in fetches:
+        fetch.start()
     d_mix[...] = nt(ain_ref[...], w_ref[...]).astype(BF16)
     product = d_mix[...].astype(F32) * mix_ref[...].astype(F32)
     high, low, _ = split_bf16(product)
@@ -424,7 +445,7 @@
 
     def d_probs_of(p, t):
         v = qkv_ref[WINDOWS[t] : WINDOWS[t] + 256, pl.ds(offsets(p) + 2 * HALF, 128)]
-        d_probs[t % 2] = nt(v, outs_of(p, t))
+        d_probs[t % 2] = in_halves(nt, v, outs_of(p, t))
 
     def pair(p, carry):
         at = offsets(p)
@@ -439,40 +460,41 @@
             q = qkv_ref[128 * t : 128 * t + 128, pl.ds(at, 128)]
             k = qkv_ref[window, pl.ds(at + HALF, 128)]
             queries = jnp.concatenate([q * first, q * second], axis=0)
-            probs = probs_ref[0, p, t]
-            dv[window, :] += nn(probs, outs_of(p, t))
+            probs = probs_ref[p, t]
+            dv[window, :] += in_halves(nn, probs, outs_of(p, t))
             scores = (probs.astype(F32) * (d_probs[t % 2] - delta[p, t])).astype(BF16)
-            dk[window, :] += nn(scores, queries)
-            dq = tn(scores, k) * HEAD**-0.5
-            dqkv_ref[128 * t : 128 * t + 128, pl.ds(at, 128)] = jnp.where(choose, dq[:128], dq[128:]).astype(BF16)
+            dk[window, :] += in_halves(nn, scores, queries)
+            dq = jnp.where(choose, tn(scores[:, :128], k), tn(scores[:, 128:], k)) * HEAD**-0.5
+            dqkv_ref[128 * t : 128 * t + 128, pl.ds(at, 128)] = dq.astype(BF16)
         dqkv_ref[:, pl.ds(at + HALF, 128)] = dk[...].astype(BF16)
         dqkv_ref[:, pl.ds(at + 2 * HALF, 128)] = dv[...].astype(BF16)
         return carry
 
+    for fetch in fetches:
+        fetch.wait()
     d_probs_of(0, 0)
     lax.fori_loop(0, HEADS // 2, pair, 0)
-    for h in range(2):
-        cols = slice(HALF * h, HALF * h + HALF)
-        for row, shift in ((0, 0), (1, 2 * HALF)):
-            part = dqkv_ref[:, QKV * h + shift : QKV * h + shift + HALF]
-            vg_ref[row : row + 1, cols] = column_sum(part.astype(F32))
     slot_ref[...] = tn(pick_ref[...], dqkv_ref[...])
 
 
-def small_grads(first_ref, sa_ref, sb_ref, w_ref, embed_ref, ff_ref, va_ref, vb_ref, up_ref):
-    high, low, _ = split_bf16(sa_ref[...] + sb_ref[...])
+def small_grads(first_ref, sa_ref, sb_ref, w_ref, embed_ref, ff_ref, up_ref):
+    second = sa_ref[...] + sb_ref[...]
+    high, low, _ = split_bf16(second)
+    biases = column_sum(second)
+    query = jnp.concatenate([biases[:, :HALF], biases[:, QKV : QKV + HALF]], axis=1)
+    value = jnp.concatenate([biases[:, 2 * HALF : QKV], biases[:, QKV + 2 * HALF :]], axis=1)
     both = nt(jnp.concatenate([high, low], axis=0), w_ref[...])
     slots = first_ref[...] + both[: high.shape[0]] + both[high.shape[0] :]
     slot_low = slots.astype(BF16)
-    rows = [column_sum(slot_low.astype(F32)), va_ref[0:2, :] + vb_ref[0:2, :], ff_ref[0:6, :], up_ref[0:4, :]]
+    rows = [column_sum(slot_low.astype(F32)), query, value, ff_ref[0:6, :], up_ref[0:4, :]]
     rows.append(jnp.zeros((TDIM - 13, D), F32))
     vectors = jnp.concatenate(rows, axis=0).T
     return jnp.concatenate([tn(slot_low, embed_ref[...]), vectors], axis=1).astype(BF16)
 
 
 def qkv_other_kernel(
-    tbl, low_ref, dqkv_ref, first_ref, sa_ref, sb_ref, w_ref, embed_ref, ff_ref, va_ref, vb_ref, up_ref,
-    small_ref, other, hold, extra, sems, small_sems,
+    tbl, low_ref, dqkv_ref, first_ref, sa_ref, sb_ref, w_all, embed_ref, ff_ref, up_ref,
+    small_ref, other, hold, extra, w_ref, sems, small_sems, w_sem,
 ):
     step = pl.program_id(0)
     off = 1 - tbl[CORE_AT]
@@ -485,9 +507,16 @@
             made.append(pltpu.make_async_copy(src, dst, small_sems.at[chip]))
         return made
 
+    fetch = pltpu.make_async_copy(w_all, w_ref, w_sem.at[0])
+
     @pl.when(step == 0)
     def _():
-        small = small_grads(first_ref, sa_ref, sb_ref, w_ref, embed_ref, ff_ref, va_ref, vb_ref, up_ref)
+        fetch.start()
+
+    @pl.when(step == 1)
+    def _():
+        fetch.wait()
+        small = small_grads(first_ref, sa_ref, sb_ref, w_ref, embed_ref, ff_ref, up_ref)
         small_ref[...] = small
         extra[...] = small
         for copy in small_copies():
@@ -647,14 +676,15 @@
         return jnp.where(kind == 0, tbl[CORE_AT], 1 - tbl[CORE_AT])
 
     return [whole_spec((rows, D)), pl.BlockSpec((rows, D), lambda i, tbl: (0, 2 * half(tbl) + jnp.minimum(i, 1))),
-            whole_spec((rows, D)), pl.BlockSpec((rows, HALF), lambda i, tbl: (0, half(tbl)))]
+            ANY, ANY]
 
 
 def up_other(tbl, mlow, dexp, mix, ain):
     rows = mlow.shape[0]
     return call(
         up_other_kernel, "up_other", (3,), up_specs(rows, 1), ANY, sds((CHIPS, 48, 2 * D + HALF), BF16),
-        [pltpu.VMEM((3, D, D), BF16), pltpu.SemaphoreType.DMA((3, CHIPS))],
+        [pltpu.VMEM((3, D, D), BF16), pltpu.VMEM((rows, D), BF16), pltpu.VMEM((rows, HALF), BF16),
+         pltpu.SemaphoreType.DMA((3, CHIPS)), pltpu.SemaphoreType.DMA((2,))],
         rows * D * (FF + D), 20 << 20, (tbl, mlow, dexp, mix, ain),
     )
 
@@ -664,7 +694,8 @@
     shape = sds((CHIPS // 2, 48, 2 * D + HALF), BF16)
     return call(
         up_own_kernel, "up_own", (3,), up_specs(rows, 0) + [ANY], [whole_spec(shape.shape)] * 2, [shape, shape],
-        [pltpu.VMEM((D, D), BF16), pltpu.VMEM((D, 2 * D + HALF), BF16), pltpu.SemaphoreType.DMA((CHIPS,))],
+        [pltpu.VMEM((D, D), BF16), pltpu.VMEM((D, 2 * D + HALF), BF16), pltpu.VMEM((rows, D), BF16),
+         pltpu.VMEM((rows, HALF), BF16), pltpu.SemaphoreType.DMA((CHIPS,)), pltpu.SemaphoreType.DMA((2,))],
         rows * D * (FF + D), 20 << 20, (tbl, mlow, dexp, mix, ain, got),
     )
 
@@ -676,18 +707,17 @@
     return [pl.BlockSpec((rows, HALF), lambda i, tbl: (0, i)), pl.BlockSpec((rows, QKV), lambda i, tbl: (0, half(tbl)))]
 
 
-def qkv_other(tbl, low, dqkv, first, sa, sb, weight, embed, ff, va, vb, up):
+def qkv_other(tbl, low, dqkv, first, sa, sb, weight, embed, ff, up):
     rows = low.shape[0]
     slots = first.shape[0]
     return call(
         qkv_other_kernel, "qkv_other", (2,),
-        qkv_specs(rows, 1) + [whole_spec((slots, D)), whole_spec((slots, 2 * QKV)), whole_spec((slots, 2 * QKV)), whole_spec((D, 2 * QKV)),
-                              whole_spec((slots, TDIM)), whole_spec((8, D)), whole_spec((8, D)), whole_spec((8, D)),
-                              whole_spec((4, D))],
+        qkv_specs(rows, 1) + [whole_spec((slots, D)), whole_spec((slots, 2 * QKV)), whole_spec((slots, 2 * QKV)), ANY,
+                              whole_spec((slots, TDIM)), whole_spec((8, D)), whole_spec((4, D))],
         [whole_spec((D, 2 * TDIM)), ANY], [sds((D, 2 * TDIM), BF16), sds((CHIPS, 48, QKV + TDIM), BF16)],
-        [pltpu.VMEM((2, HALF, QKV), BF16), pltpu.VMEM((D, 2 * TDIM), BF16), pltpu.SemaphoreType.DMA((2, CHIPS // 2)),
-         pltpu.SemaphoreType.DMA((CHIPS,))],
-        3 * rows * D * D, 20 << 20, (tbl, low, dqkv, first, sa, sb, weight, embed, ff, va, vb, up),
+        [pltpu.VMEM((2, HALF, QKV), BF16), pltpu.VMEM((D, 2 * TDIM), BF16), pltpu.VMEM((D, 2 * QKV), BF16),
+         pltpu.SemaphoreType.DMA((2, CHIPS // 2)), pltpu.SemaphoreType.DMA((CHIPS,)), pltpu.SemaphoreType.DMA((1,))],
+        3 * rows * D * D, 20 << 20, (tbl, low, dqkv, first, sa, sb, weight, embed, ff, up),
     )
 
 
@@ -706,14 +736,14 @@
     rows = ain.shape[0]
     slots = pick.shape[1]
     return call(
-        attention_backward_kernel, "attention_backward", (1,),
-        [block_spec((BLOCK, D), block), block_spec((BLOCK, D), block), block_spec((BLOCK, 2 * QKV), block),
-         block_spec((1, HEADS // 2, 4, 256, 256), block), pl.BlockSpec((D, D), lambda i, *_: (0, 4)),
+        functools.partial(attention_backward_kernel, block), "attention_backward", (1,),
+        [block_spec((BLOCK, D), block), block_spec((BLOCK, D), block), ANY, ANY, pl.BlockSpec((D, D), lambda i, *_: (0, 4)),
          block_spec((BLOCK, slots), block)] + [ANY] * len(before),
-        [block_spec((BLOCK, 2 * QKV), block), whole_spec((8, D)), whole_spec((slots, 2 * QKV))],
-        [sds((rows, 2 * QKV), BF16), sds((8, D), F32), sds((slots, 2 * QKV), F32)],
+        [block_spec((BLOCK, 2 * QKV), block), whole_spec((slots, 2 * QKV))],
+        [sds((rows, 2 * QKV), BF16), sds((slots, 2 * QKV), F32)],
         [pltpu.VMEM((BLOCK, D), BF16), pltpu.VMEM((HEADS // 2, 4, 1, 256), F32), pltpu.VMEM((2, 256, 256), F32),
-         pltpu.VMEM((BLOCK, 128), F32), pltpu.VMEM((BLOCK, 128), F32)],
+         pltpu.VMEM((BLOCK, 128), F32), pltpu.VMEM((BLOCK, 128), F32), pltpu.VMEM((BLOCK, 2 * QKV), BF16),
+         pltpu.VMEM((HEADS // 2, 4, 256, 256), BF16), pltpu.SemaphoreType.DMA((2,))],
         4 * BLOCK * D * D, 20 << 20, (ain, mix, qkv, probs, weight, pick, *before), prefetch=0,
         alias={6 + i: i for i in range(len(before))},
     )
@@ -971,12 +1001,12 @@
         u_keep, u_away = up_own(tbl, mlow, dexp, mix, ain, u_got)
         ain, u_keep, u_away = tie(ain, u_keep, u_away)
         u_got = send_on(u_away, "b", n)
-        dqkv, vg0, slot0 = attention_backward(0, ain, mix, qkv, probs, up_full, pick, ())
+        dqkv, slot0 = attention_backward(0, ain, mix, qkv, probs, up_full, pick, ())
         dqkv, d_keep, d_got = tie(dqkv, d_keep, d_got)
         d_keep, d_away = halve(d_keep, d_got)
         ain, dqkv, d_keep, d_away = tie(ain, dqkv, d_keep, d_away)
         d_got = send_on(d_away, "a", n)
-        dqkv, vg1, slot1 = attention_backward(1, ain, mix, qkv, probs, up_full, pick, (dqkv,))
+        dqkv, slot1 = attention_backward(1, ain, mix, qkv, probs, up_full, pick, (dqkv,))
         dqkv, d_keep, d_got, u_keep, u_got = tie(dqkv, d_keep, d_got, u_keep, u_got)
         u_keep, u_away = halve(u_keep, u_got)
         d_keep, d_away = halve(d_keep, d_got)
@@ -984,7 +1014,7 @@
         u_got = send_on(u_away, "a", n)
         d_got = send_on(d_away, "z1", n)
         small, q_other = qkv_other(
-            tbl, low, dqkv, slot_first, slot0, slot1, weight, embed_in, ff_vecs, vg0, vg1, up_vec
+            tbl, low, dqkv, slot_first, slot0, slot1, weight, embed_in, ff_vecs, up_vec
         )
         q_other, u_keep, u_got, d_keep, d_got, low = tie(q_other, u_keep, u_got, d_keep, d_got, low)
         q_got = send_on(q_other, "core", n)
@@ -1012,10 +1042,10 @@
         q_got = send_on(q_away, "z2", n)
         qkv_sum = finish(q_keep, q_got, n)
     else:
-        dqkv, vg0, slot0 = attention_backward(0, ain, mix, qkv, probs, up_full, pick, ())
-        dqkv, vg1, slot1 = attention_backward(1, ain, mix, qkv, probs, up_full, pick, (dqkv,))
+        dqkv, slot0 = attention_backward(0, ain, mix, qkv, probs, up_full, pick, ())
+        dqkv, slot1 = attention_backward(1, ain, mix, qkv, probs, up_full, pick, (dqkv,))
         small, q_other = qkv_other(
-            tbl, low, dqkv, slot_first, slot0, slot1, weight, embed_in, ff_vecs, vg0, vg1, up_vec
+            tbl, low, dqkv, slot_first, slot0, slot1, weight, embed_in, ff_vecs, up_vec
         )
         input_grad = input_gradient(df, dqkv, weight)
         down_sum = whole_reduce(d_own, d_other, core)

time: 300 us -> 297 us (0.990)
  Pallas kernels: 162 us -> 158 us
    pallas_call x14, Pallas kernels: 162 us -> 158 us  [call(): pl.pallas_call(kernel, name=name, grid_spec=pltpu.PrefetchScalarGridSpec(...]
  transfers between devices with their start and end apart: 37 -> 37, of which waited for: 17 -> 17; matrix products, arithmetic and copies ran while one was open for 11% -> 11% of each run, Pallas kernels for 40% -> 39%
where the time goes in v2:
time: 297 us; the launch traced here: 296 us
  Pallas kernels  158 us (53%)
  waiting for transfers between devices  49.2 us (17%)
  starting transfers between devices  38.1 us (13%)
  other arithmetic  32 us (11%)
  local copies, waits for them, and re-layouts  17.1 us (6%)
    pallas_call x14, Pallas kernels, call(): pl.pallas_call(kernel, name=name, grid_spec=pltpu.PrefetchScalarGridSpec(...  158 us
    ppermute x37, waiting for transfers between devices, send_on(): return lax.ppermute(value, 'fsdp', perm=tiled_route(n)[step])  49.2 us
    ppermute x37, starting transfers between devices, send_on(): return lax.ppermute(value, 'fsdp', perm=tiled_route(n)[step])  38.1 us
    convert_element_type x10, other arithmetic, add(): return (left.astype(F32) + right.astype(F32)).astype(BF16)  17.9 us
  transfers between devices with their start and end apart: 37, of which 17 were waited for; matrix products, arithmetic and copies ran while one was open for 11% of the time, Pallas kernels for 39%

profile of v2, /device:TPU:0, one launch (start us, length us, event | category | flops | bytes accessed | tf_op | source)
XLA Modules:
  0.0 295.9 jit_solution(11410680769198170387)
XLA Ops:
  7.6 4.0 %collective-permute-start.1 = (bf16[1,48,1280]{2,1,0:T(8,128)(2,1)S(1)}, bf16[1,48,1280]{2,1,0:T(8,128)(2,1)S(1)}, u32[]{:S(2)}, u32[]{:S(2)}) collective-permute-start(bf16[1,48,1280]{2,1,0:T(8,128)(2,1)S(1)} %maximum_bitcast_fusion.2), channel_id=1, source_target_pairs={{0,16},{1,17},{2,18},{3,19},{4,20},{5,21},{6,22},{7,23},{8,24},{9,... | collective-permute-start | bytes 368648 | tf_op jit(solution)/shard_map/ppermute | solution.py:807
  13.5 4.4 %collective-permute-done.1 = bf16[1,48,1280]{2,1,0:T(8,128)(2,1)S(1)} collective-permute-done((bf16[1,48,1280]{2,1,0:T(8,128)(2,1)S(1)}, bf16[1,48,1280]{2,1,0:T(8,128)(2,1)S(1)}, u32[]{:S(2)}, u32[]{:S(2)}) %collective-permute-start.1) | collective-permute-done | bytes 122912 | tf_op jit(solution)/shard_map/ppermute | solution.py:807
  19.0 6.5 %collective-permute-done.2 = bf16[2,48,1280]{2,1,0:T(8,128)(2,1)S(1)} collective-permute-done((bf16[2,48,1280]{2,1,0:T(8,128)(2,1)S(1)}, bf16[2,48,1280]{2,1,0:T(8,128)(2,1)S(1)}, u32[]{:S(2)}, u32[]{:S(2)}) %collective-permute-start.2) | collective-permute-done | bytes 245792 | tf_op jit(solution)/shard_map/ppermute | solution.py:807
  27.0 3.0 %collective-permute-start.4 = (bf16[1,48,1920]{2,1,0:T(8,128)(2,1)S(1)}, bf16[1,48,1920]{2,1,0:T(8,128)(2,1)S(1)}, u32[]{:S(2)}, u32[]{:S(2)}) collective-permute-start(bf16[1,48,1920]{2,1,0:T(8,128)(2,1)S(1)} %maximum_bitcast_fusion), channel_id=1, source_target_pairs={{0,16},{1,17},{2,18},{3,19},{4,20},{5,21},{6,22},{7,23},{8,24},{9,... | collective-permute-start | bytes 552968 | tf_op jit(solution)/shard_map/ppermute | solution.py:807
  30.2 7.9 %collective-permute-done.4 = bf16[1,48,1920]{2,1,0:T(8,128)(2,1)S(1)} collective-permute-done((bf16[1,48,1920]{2,1,0:T(8,128)(2,1)S(1)}, bf16[1,48,1920]{2,1,0:T(8,128)(2,1)S(1)}, u32[]{:S(2)}, u32[]{:S(2)}) %collective-permute-start.4) | collective-permute-done | bytes 184352 | tf_op jit(solution)/shard_map/ppermute | solution.py:807
  42.2 7.4 %collective-permute-done.6 = bf16[2,48,1920]{2,1,0:T(8,128)(2,1)S(1)} collective-permute-done((bf16[2,48,1920]{2,1,0:T(8,128)(2,1)S(1)}, bf16[2,48,1920]{2,1,0:T(8,128)(2,1)S(1)}, u32[]{:S(2)}, u32[]{:S(2)}) %collective-permute-start.6) | collective-permute-done | bytes 368672 | tf_op jit(solution)/shard_map/ppermute | solution.py:807
  49.7 2.7 collective-permute-done.5.own_high
  55.1 11.7 %project.1 = (f32[1024,768]{1,0:T(8,128)}, bf16[1024,768]{1,0:T(8,128)(2,1)}, bf16[1024,2304]{1,0:T(8,128)(2,1)}, f32[16,768]{1,0:T(8,128)}, bf16[768,2304]{1,0:T(8,128)(2,1)}) custom-call(s32[80]{0:T(128)} %concatenate.75.tbl, bf16[1024,768]{1,0:T(8,128)(2,1)} %x_ref.1, bf16[1024,16]{1,0:T(8,128)(2,1)} %fusion.pick_ref, ...), custom_call_target="tpu_custom_call" | custom-call | flops 3623878656 | bytes 20971520 | tf_op jit(solution)/shard_map/project/pallas_call | solution.py:569
  67.8 2.0 constant_dynamic-update-slice_fusion.ua
  71.5 3.8 %collective-permute-start.12 = (bf16[2,192,384]{2,1,0:T(8,128)(2,1)S(1)}, bf16[2,192,384]{2,1,0:T(8,128)(2,1)S(1)}, u32[]{:S(2)}, u32[]{:S(2)}) collective-permute-start(bf16[2,192,384]{2,1,0:T(8,128)(2,1)S(1)} %constant_dynamic-update-slice_fusion.2), channel_id=1, source_target_pairs={{0,8},{1,9},{2,10},{3,11},{4,12},{5,13},{6,14},{7,15},{8,0},{9,1},... | collective-permute-start | bytes 884744 | tf_op jit(solution)/shard_map/ppermute | solution.py:807
  75.3 8.8 %attend.2 = (bf16[1024,768]{1,0:T(8,128)(2,1)}, bf16[2,6,4,256,256]{4,3,2,1,0:T(8,128)(2,1)}) custom-call(bf16[1024,2304]{1,0:T(8,128)(2,1)} %get-tuple-element.172.qkv_ref.qkv_all, bf16[1024,16]{1,0:T(8,128)(2,1)} %fusion.pick_ref, f32[2,1,512]{2,1,0:T(1,128)} %add_convert_fusion.20.segr_ref), custom_call_target="tpu_custom_call" | custom-call | flops 1207959552 | bytes 20971520 | tf_op jit(solution)/shard_map/attend/pallas_call | solution.py:569
  87.3 8.9 %attend.3 = (bf16[1024,768]{1,0:T(8,128)(2,1)}, bf16[2,6,4,256,256]{4,3,2,1,0:T(8,128)(2,1)}) custom-call(bf16[1024,2304]{1,0:T(8,128)(2,1)} %get-tuple-element.172.qkv_ref.qkv_all, bf16[1024,16]{1,0:T(8,128)(2,1)} %fusion.pick_ref, f32[2,1,512]{2,1,0:T(1,128)} %add_convert_fusion.20.segr_ref, ...), custom_call_target="tpu_custom_call", output_to_operand_aliasing={{0}: (3, {}), {1}: (4, {})} | custom-call | flops 1207959552 | bytes 20971520 | tf_op jit(solution)/shard_map/attend/pallas_call | solution.py:569
  102.0 18.6 %expand.1 = (f32[1024,768]{1,0:T(8,128)}, f32[1024,1]{1,0:T(8,128)}, bf16[1024,3072]{1,0:T(8,128)(2,1)}, bf16[1024,3072]{1,0:T(8,128)(2,1)}, bf16[1024,768]{1,0:T(8,128)(2,1)}, /*index=5*/bf16[768,3840]{1,0:T(8,128)(2,1)}) custom-call(s32[80]{0:T(128)} %concatenate.75.tbl, f32[1024,768]{1,0:T(8,128)} %get-tuple-element.160.hidden_ref, ...), custom_call_target="tpu_custom_call" | custom-call | flops 6039797760 | bytes 20971520 | tf_op jit(solution)/shard_map/expand/pallas_call | solution.py:569
  121.2 2.8 collective-permute-done.18.dd
  124.0 30.1 %contract.1 = (bf16[1024,768]{1,0:T(8,128)(2,1)}, bf16[1024,3072]{1,0:T(8,128)(2,1)}, bf16[1024,768]{1,0:T(8,128)(2,1)}, f32[1024,768]{1,0:T(8,128)}, bf16[1024,...) custom-call(s32[80]{0:T(128)} %concatenate.75.tbl, ...), custom_call_target="tpu_custom_call" | custom-call | flops 14495514624 | bytes 20971520 | tf_op jit(solution)/shard_map/contract/pallas_call | solution.py:569
  154.0 10.3 %down_grad.1 = (bf16[16,192,384]{2,1,0:T(8,128)(2,1)}, bf16[16,192,384]{2,1,0:T(8,128)(2,1)}) custom-call(s32[80]{0:T(128)} %concatenate.75.tbl, bf16[1024,3072]{1,0:T(8,128)(2,1)} %get-tuple-element.188.act_ref, bf16[1024,768]{1,0:T(8,128)(2,1)} %get-tuple-element.197.din_ref), custom_call_target="tpu_custom_call" | custom-call | flops 4831838208 | bytes 20971520 | tf_op jit(solution)/shard_map/down_grad/pallas_call | solution.py:569
  166.8 7.8 %up_other.1 = bf16[16,48,1920]{2,1,0:T(8,128)(2,1)} custom-call(s32[80]{0:T(128)} %concatenate.75.tbl, bf16[1024,768]{1,0:T(8,128)(2,1)} %get-tuple-element.205.mlow_ref, bf16[1024,3072]{1,0:T(8,128)(2,1)} %get-tuple-element.201.dexp_ref, bf16[1024,768]{1,0:T(8,128)(2,1)} %get-tuple-element.178.mix_ref.mix_all, ...), custom_call_target="tpu_custom_call" | custom-call | flops 3019898880 | bytes 20971520 | tf_op jit(solution)/shard_map/up_other/pallas_call | solution.py:569
  174.9 4.4 %add_convert_fusion = (bf16[8,192,384]{2,1,0:T(8,128)(2,1)}, bf16[8,192,384]{2,1,0:T(8,128)(2,1)}) fusion(bf16[16,192,384]{2,1,0:T(8,128)(2,1)} %collective-permute-done.19, bf16[16,192,384]{2,1,0:T(8,128)(2,1)} %get-tuple-element.206), kind=kLoop, calls=%fused_computation | loop fusion | flops 4718592 | bytes 7077888 | tf_op jit(solution)/shard_map/convert_element_type | solution.py:863
  181.3 11.3 %up_own.1 = (bf16[8,48,1920]{2,1,0:T(8,128)(2,1)}, bf16[8,48,1920]{2,1,0:T(8,128)(2,1)}) custom-call(s32[80]{0:T(128)} %concatenate.75.tbl, bf16[1024,768]{1,0:T(8,128)(2,1)} %get-tuple-element.205.mlow_ref, bf16[1024,3072]{1,0:T(8,128)(2,1)} %get-tuple-element.201.dexp_ref, bf16[1024,768]{1,0:T(8,128)(2,1)} %get-tuple-element.178.mix_ref.mix_all, ...), custom_call_target="tpu_custom_call" | custom-call | flops 3019898880 | bytes 20971520 | tf_op jit(solution)/shard_map/up_own/pallas_call | solution.py:569
  193.9 10.9 %attention_backward.2 = (bf16[1024,2304]{1,0:T(8,128)(2,1)}, f32[16,2304]{1,0:T(8,128)}) custom-call(bf16[1024,768]{1,0:T(8,128)(2,1)} %get-tuple-element.220.ain_all.ain_ref, bf16[1024,768]{1,0:T(8,128)(2,1)} %get-tuple-element.178.mix_ref.mix_all, bf16[1024,2304]{1,0:T(8,128)(2,1)} %get-tuple-element.172.qkv_ref.qkv_all, ...), custom_call_target="tpu_custom_call" | custom-call | flops 1207959552 | bytes 20971520 | tf_op jit(solution)/shard_map/attention_backward/pallas_call | solution.py:569
  204.8 2.9 add_convert_fusion.4
  208.7 10.9 %attention_backward.3 = (bf16[1024,2304]{1,0:T(8,128)(2,1)}, f32[16,2304]{1,0:T(8,128)}) custom-call(bf16[1024,768]{1,0:T(8,128)(2,1)} %get-tuple-element.220.ain_all.ain_ref, bf16[1024,768]{1,0:T(8,128)(2,1)} %get-tuple-element.178.mix_ref.mix_all, bf16[1024,2304]{1,0:T(8,128)(2,1)} %get-tuple-element.172.qkv_ref.qkv_all, ...), custom_call_target="tpu_custom_call", output_to_operand_aliasing={{0}: (6, {})} | custom-call | flops 1207959552 | bytes 20971520 | tf_op jit(solution)/shard_map/attention_backward/pallas_call | solution.py:569
  220.4 3.1 %add_convert_fusion.2 = (bf16[4,48,1920]{2,1,0:T(8,128)(2,1)}, bf16[4,48,1920]{2,1,0:T(8,128)(2,1)S(1)}) fusion(bf16[8,48,1920]{2,1,0:T(8,128)(2,1)} %collective-permute-done.23, bf16[8,48,1920]{2,1,0:T(8,128)(2,1)} %get-tuple-element.230), kind=kLoop, calls=%fused_computation.2 | loop fusion | flops 2949120 | bytes 4423680 | tf_op jit(solution)/shard_map/convert_element_type | solution.py:863
  225.6 2.6 collective-permute-start.25
  228.1 9.3 %qkv_other.1 = (bf16[768,256]{1,0:T(8,128)(2,1)}, bf16[16,48,1280]{2,1,0:T(8,128)(2,1)}) custom-call(s32[80]{0:T(128)} %concatenate.75.tbl, bf16[1024,768]{1,0:T(8,128)(2,1)} %get-tuple-element.245.low_ref, bf16[1024,2304]{1,0:T(8,128)(2,1)} %get-tuple-element.233.dqkv_ref, f32[16,768]{1,0:T(8,128)} %get-tuple-element.234.first_ref, ...), custom_call_target="tpu_custom_call" | custom-call | flops 1811939328 | bytes 20971520 | tf_op jit(solution)/shard_map/qkv_other/pallas_call | solution.py:569
  239.5 2.1 add_convert_fusion.8
  243.6 8.6 %qkv_own.1 = (bf16[8,48,1280]{2,1,0:T(8,128)(2,1)}, bf16[8,48,1280]{2,1,0:T(8,128)(2,1)}) custom-call(s32[80]{0:T(128)} %concatenate.75.tbl, bf16[1024,768]{1,0:T(8,128)(2,1)} %get-tuple-element.245.low_ref, bf16[1024,2304]{1,0:T(8,128)(2,1)} %get-tuple-element.233.dqkv_ref, bf16[768,256]{1,0:T(8,128)(2,1)} %get-tuple-element.246.small_ref, ...), custom_call_target="tpu_custom_call" | custom-call | flops 1811939328 | bytes 20971520 | tf_op jit(solution)/shard_map/qkv_own/pallas_call | solution.py:569
  255.5 2.6 collective-permute-start.34
  258.1 9.0 %input_grad.1 = f32[1024,768]{1,0:T(8,128)} custom-call(f32[1024,768]{1,0:T(8,128)} %get-tuple-element.261.df_ref, bf16[1024,2304]{1,0:T(8,128)(2,1)} %get-tuple-element.233.dqkv_ref, bf16[768,2304]{1,0:T(8,128)(2,1)} %get-tuple-element.237.w_all.w_ref), custom_call_target="tpu_custom_call" | custom-call | flops 3623878656 | bytes 20971520 | tf_op jit(solution)/shard_map/input_grad/pallas_call | solution.py:569
  270.1 2.1 collective-permute-done.34
  279.5 5.0 %collective-permute-done.30 = bf16[2,48,1280]{2,1,0:T(8,128)(2,1)S(1)} collective-permute-done((bf16[2,48,1280]{2,1,0:T(8,128)(2,1)S(1)}, bf16[2,48,1280]{2,1,0:T(8,128)(2,1)S(1)}, u32[]{:S(2)}, u32[]{:S(2)}) %collective-permute-start.30) | collective-permute-done | bytes 245792 | tf_op jit(solution)/shard_map/ppermute | solution.py:807
  285.5 4.9 %collective-permute-done.31 = bf16[1,48,1280]{2,1,0:T(8,128)(2,1)S(1)} collective-permute-done((bf16[1,48,1280]{2,1,0:T(8,128)(2,1)S(1)}, bf16[1,48,1280]{2,1,0:T(8,128)(2,1)S(1)}, u32[]{:S(2)}, u32[]{:S(2)}) %collective-permute-start.31) | collective-permute-done | bytes 122912 | tf_op jit(solution)/shard_map/ppermute | solution.py:807
  (180 shorter events, 63.9 us)
Async XLA Ops:
  7.6 10.3 %collective-permute-start.1 = (bf16[1,48,1280]{2,1,0:T(8,128)(2,1)S(1)}, bf16[1,48,1280]{2,1,0:T(8,128)(2,1)S(1)}, u32[]{:S(2)}, u32[]{:S(2)}) collective-permute-start(bf16[1,48,1280]{2,1,0:T(8,128)(2,1)S(1)} %maximum_bitcast_fusion.2), channel_id=1, source_target_pairs={{0,16},{1,17},{2,18},{3,19},{4,20},{5,21},{6,22},{7,23},{8,24},{9,... | collective-permute-start | bytes 368648 | tf_op jit(solution)/shard_map/ppermute | solution.py:807
  18.0 7.6 %collective-permute-start.2 = (bf16[2,48,1280]{2,1,0:T(8,128)(2,1)S(1)}, bf16[2,48,1280]{2,1,0:T(8,128)(2,1)S(1)}, u32[]{:S(2)}, u32[]{:S(2)}) collective-permute-start(bf16[2,48,1280]{2,1,0:T(8,128)(2,1)S(1)} %pad_maximum_fusion.6), channel_id=1, source_target_pairs={{0,8},{1,9},{2,10},{3,11},{4,12},{5,13},{6,14},{7,15},{8,0},{9,1},... | collective-permute-start | bytes 737288 | tf_op jit(solution)/shard_map/ppermute | solution.py:807
  25.6 12.6 %collective-permute-start.3 = (bf16[4,48,1280]{2,1,0:T(8,128)(2,1)S(1)}, bf16[4,48,1280]{2,1,0:T(8,128)(2,1)S(1)}, u32[]{:S(2)}, u32[]{:S(2)}) collective-permute-start(bf16[4,48,1280]{2,1,0:T(8,128)(2,1)S(1)} %pad_maximum_fusion.2), channel_id=1, source_target_pairs={{0,2},{1,5},{2,0},{3,7},{4,6},{5,1},{6,4},{7,3},{8,10},{9,13},{10,... | collective-permute-start | bytes 1474568 | tf_op jit(solution)/shard_map/ppermute | solution.py:807
  27.0 11.0 %collective-permute-start.4 = (bf16[1,48,1920]{2,1,0:T(8,128)(2,1)S(1)}, bf16[1,48,1920]{2,1,0:T(8,128)(2,1)S(1)}, u32[]{:S(2)}, u32[]{:S(2)}) collective-permute-start(bf16[1,48,1920]{2,1,0:T(8,128)(2,1)S(1)} %maximum_bitcast_fusion), channel_id=1, source_target_pairs={{0,16},{1,17},{2,18},{3,19},{4,20},{5,21},{6,22},{7,23},{8,24},{9,... | collective-permute-start | bytes 552968 | tf_op jit(solution)/shard_map/ppermute | solution.py:807
  38.3 14.2 %collective-permute-start.5 = (bf16[8,48,1280]{2,1,0:T(8,128)(2,1)S(1)}, bf16[8,48,1280]{2,1,0:T(8,128)(2,1)S(1)}, u32[]{:S(2)}, u32[]{:S(2)}) collective-permute-start(bf16[8,48,1280]{2,1,0:T(8,128)(2,1)S(1)} %pad_maximum_fusion.own_low), channel_id=1, source_target_pairs={{0,4},{1,3},{2,6},{3,1},{4,0},{5,7},{6,2},{7,5},{8,12},{9,11},{10,... | collective-permute-start | bytes 2949128 | tf_op jit(solution)/shard_map/ppermute | solution.py:807
  38.9 10.7 %collective-permute-start.6 = (bf16[2,48,1920]{2,1,0:T(8,128)(2,1)S(1)}, bf16[2,48,1920]{2,1,0:T(8,128)(2,1)S(1)}, u32[]{:S(2)}, u32[]{:S(2)}) collective-permute-start(bf16[2,48,1920]{2,1,0:T(8,128)(2,1)S(1)} %pad_maximum_fusion.3), channel_id=1, source_target_pairs={{0,8},{1,9},{2,10},{3,11},{4,12},{5,13},{6,14},{7,15},{8,0},{9,1},... | collective-permute-start | bytes 1105928 | tf_op jit(solution)/shard_map/ppermute | solution.py:807
  41.8 12.2 %collective-permute-start.7 = (bf16[8,48,1280]{2,1,0:T(8,128)(2,1)S(1)}, bf16[8,48,1280]{2,1,0:T(8,128)(2,1)S(1)}, u32[]{:S(2)}, u32[]{:S(2)}) collective-permute-start(bf16[8,48,1280]{2,1,0:T(8,128)(2,1)S(1)} %pad_maximum_fusion.own_low), channel_id=1, source_target_pairs={{0,1},{1,0},{2,3},{3,2},{4,5},{5,4},{6,7},{7,6},{8,9},{9,8},{10,11... | collective-permute-start | bytes 2949128 | tf_op jit(solution)/shard_map/ppermute | solution.py:807
  52.4 14.5 %collective-permute-start.9 = (bf16[4,48,1920]{2,1,0:T(8,128)(2,1)S(1)}, bf16[4,48,1920]{2,1,0:T(8,128)(2,1)}, u32[]{:S(2)}, u32[]{:S(2)}) collective-permute-start(bf16[4,48,1920]{2,1,0:T(8,128)(2,1)S(1)} %pad_maximum_fusion.1), channel_id=1, source_target_pairs={{0,2},{1,5},{2,0},{3,7},{4,6},{5,1},{6,4},{7,3},{8,10},{9,13},{10,... | collective-permute-start | bytes 2211848 | tf_op jit(solution)/shard_map/ppermute | solution.py:807
  54.0 12.9 %collective-permute-start.10 = (bf16[1,192,384]{2,1,0:T(8,128)(2,1)S(1)}, bf16[1,192,384]{2,1,0:T(8,128)(2,1)}, u32[]{:S(2)}, u32[]{:S(2)}) collective-permute-start(bf16[1,192,384]{2,1,0:T(8,128)(2,1)S(1)} %maximum_bitcast_fusion.1), channel_id=1, source_target_pairs={{0,16},{1,17},{2,18},{3,19},{4,20},{5,21},{6,22},{7,23},{8,24},{9,... | collective-permute-start | bytes 442376 | tf_op jit(solution)/shard_map/ppermute | solution.py:807
  69.9 14.3 %collective-permute-start.11 = (bf16[8,48,1920]{2,1,0:T(8,128)(2,1)}, bf16[8,48,1920]{2,1,0:T(8,128)(2,1)}, u32[]{:S(2)}, u32[]{:S(2)}) collective-permute-start(bf16[8,48,1920]{2,1,0:T(8,128)(2,1)} %constant_dynamic-update-slice_fusion.ua), channel_id=1, source_target_pairs={{0,1},{1,0},{2,3},{3,2},{4,5},{5,4},{6,7},{7,6},{8,9},{9,8},{10,11... | collective-permute-start | bytes 4423688 | tf_op jit(solution)/shard_map/ppermute | solution.py:807
  70.0 26.2 %collective-permute-start.13 = (bf16[8,48,1920]{2,1,0:T(8,128)(2,1)}, bf16[8,48,1920]{2,1,0:T(8,128)(2,1)}, u32[]{:S(2)}, u32[]{:S(2)}) collective-permute-start(bf16[8,48,1920]{2,1,0:T(8,128)(2,1)} %constant_dynamic-update-slice_fusion.ua), channel_id=1, source_target_pairs={{0,4},{1,3},{2,6},{3,1},{4,0},{5,7},{6,2},{7,5},{8,12},{9,11},{10,... | collective-permute-start | bytes 4423688 | tf_op jit(solution)/shard_map/ppermute | solution.py:807
  71.5 12.6 %collective-permute-start.12 = (bf16[2,192,384]{2,1,0:T(8,128)(2,1)S(1)}, bf16[2,192,384]{2,1,0:T(8,128)(2,1)S(1)}, u32[]{:S(2)}, u32[]{:S(2)}) collective-permute-start(bf16[2,192,384]{2,1,0:T(8,128)(2,1)S(1)} %constant_dynamic-update-slice_fusion.2), channel_id=1, source_target_pairs={{0,8},{1,9},{2,10},{3,11},{4,12},{5,13},{6,14},{7,15},{8,0},{9,1},... | collective-permute-start | bytes 884744 | tf_op jit(solution)/shard_map/ppermute | solution.py:807
  85.9 10.3 %collective-permute-start.14 = (bf16[4,192,384]{2,1,0:T(8,128)(2,1)S(1)}, bf16[4,192,384]{2,1,0:T(8,128)(2,1)}, u32[]{:S(2)}, u32[]{:S(2)}) collective-permute-start(bf16[4,192,384]{2,1,0:T(8,128)(2,1)S(1)} %constant_dynamic-update-slice_fusion.4), channel_id=1, source_target_pairs={{0,2},{1,5},{2,0},{3,7},{4,6},{5,1},{6,4},{7,3},{8,10},{9,13},{10,... | collective-permute-start | bytes 1769480 | tf_op jit(solution)/shard_map/ppermute | solution.py:807
  96.2 5.8 %collective-permute-start.15 = (bf16[8,48,1920]{2,1,0:T(8,128)(2,1)}, bf16[8,48,1920]{2,1,0:T(8,128)(2,1)}, u32[]{:S(2)}, u32[]{:S(2)}) collective-permute-start(bf16[8,48,1920]{2,1,0:T(8,128)(2,1)} %collective-permute-done.13.ub), channel_id=1, source_target_pairs={{0,1},{1,0},{2,3},{3,2},{4,5},{5,4},{6,7},{7,6},{8,9},{9,8},{10,11... | collective-permute-start | bytes 4423688 | tf_op jit(solution)/shard_map/ppermute | solution.py:807
  99.2 21.5 %collective-permute-start.16 = (bf16[8,192,384]{2,1,0:T(8,128)(2,1)}, bf16[8,192,384]{2,1,0:T(8,128)(2,1)}, u32[]{:S(2)}, u32[]{:S(2)}) collective-permute-start(bf16[8,192,384]{2,1,0:T(8,128)(2,1)} %constant_dynamic-update-slice_fusion.6.da), channel_id=1, source_target_pairs={{0,4},{1,3},{2,6},{3,1},{4,0},{5,7},{6,2},{7,5},{8,12},{9,11},{10,... | collective-permute-start | bytes 3538952 | tf_op jit(solution)/shard_map/ppermute | solution.py:807
  101.9 19.2 %collective-permute-start.17 = (bf16[8,192,384]{2,1,0:T(8,128)(2,1)}, bf16[8,192,384]{2,1,0:T(8,128)(2,1)}, u32[]{:S(2)}, u32[]{:S(2)}) collective-permute-start(bf16[8,192,384]{2,1,0:T(8,128)(2,1)} %constant_dynamic-update-slice_fusion.6.da), channel_id=1, source_target_pairs={{0,1},{1,0},{2,3},{3,2},{4,5},{5,4},{6,7},{7,6},{8,9},{9,8},{10,11... | collective-permute-start | bytes 3538952 | tf_op jit(solution)/shard_map/ppermute | solution.py:807
  164.4 10.3 %collective-permute-start.19 = (bf16[16,192,384]{2,1,0:T(8,128)(2,1)}, bf16[16,192,384]{2,1,0:T(8,128)(2,1)}, u32[]{:S(2)}, u32[]{:S(2)}) collective-permute-start(bf16[16,192,384]{2,1,0:T(8,128)(2,1)} %get-tuple-element.203), channel_id=1, source_target_pairs={{0,1},{1,0},{2,3},{3,2},{4,5},{5,4},{6,7},{7,6},{8,9},{9,8},{10,11... | collective-permute-start | bytes 7077896 | tf_op jit(solution)/shard_map/ppermute | solution.py:807
  174.7 5.8 %collective-permute-start.20 = (bf16[16,48,1920]{2,1,0:T(8,128)(2,1)}, bf16[16,48,1920]{2,1,0:T(8,128)(2,1)}, u32[]{:S(2)}, u32[]{:S(2)}) collective-permute-start(bf16[16,48,1920]{2,1,0:T(8,128)(2,1)} %up_other.1), channel_id=1, source_target_pairs={{0,1},{1,0},{2,3},{3,2},{4,5},{5,4},{6,7},{7,6},{8,9},{9,8},{10,11... | collective-permute-start | bytes 8847368 | tf_op jit(solution)/shard_map/ppermute | solution.py:807
  180.4 24.3 %collective-permute-start.21 = (bf16[8,192,384]{2,1,0:T(8,128)(2,1)}, bf16[8,192,384]{2,1,0:T(8,128)(2,1)}, u32[]{:S(2)}, u32[]{:S(2)}) collective-permute-start(bf16[8,192,384]{2,1,0:T(8,128)(2,1)} %get-tuple-element.216), channel_id=1, source_target_pairs={{0,4},{1,3},{2,6},{3,1},{4,0},{5,7},{6,2},{7,5},{8,12},{9,11},{10,... | collective-permute-start | bytes 3538952 | tf_op jit(solution)/shard_map/ppermute | solution.py:807
  192.6 26.9 %collective-permute-start.23 = (bf16[8,48,1920]{2,1,0:T(8,128)(2,1)}, bf16[8,48,1920]{2,1,0:T(8,128)(2,1)}, u32[]{:S(2)}, u32[]{:S(2)}) collective-permute-start(bf16[8,48,1920]{2,1,0:T(8,128)(2,1)} %get-tuple-element.226), channel_id=1, source_target_pairs={{0,4},{1,3},{2,6},{3,1},{4,0},{5,7},{6,2},{7,5},{8,12},{9,11},{10,... | collective-permute-start | bytes 4423688 | tf_op jit(solution)/shard_map/ppermute | solution.py:807
  207.7 11.9 %collective-permute-start.22 = (bf16[4,192,384]{2,1,0:T(8,128)(2,1)}, bf16[4,192,384]{2,1,0:T(8,128)(2,1)S(1)}, u32[]{:S(2)}, u32[]{:S(2)}) collective-permute-start(bf16[4,192,384]{2,1,0:T(8,128)(2,1)} %get-tuple-element.224), channel_id=1, source_target_pairs={{0,2},{1,5},{2,0},{3,7},{4,6},{5,1},{6,4},{7,3},{8,10},{9,13},{10,... | collective-permute-start | bytes 1769480 | tf_op jit(solution)/shard_map/ppermute | solution.py:807
  224.5 13.0 %collective-permute-start.24 = (bf16[4,48,1920]{2,1,0:T(8,128)(2,1)}, bf16[4,48,1920]{2,1,0:T(8,128)(2,1)}, u32[]{:S(2)}, u32[]{:S(2)}) collective-permute-start(bf16[4,48,1920]{2,1,0:T(8,128)(2,1)} %get-tuple-element.242), channel_id=1, source_target_pairs={{0,2},{1,5},{2,0},{3,7},{4,6},{5,1},{6,4},{7,3},{8,10},{9,13},{10,... | collective-permute-start | bytes 2211848 | tf_op jit(solution)/shard_map/ppermute | solution.py:807
  225.6 11.9 %collective-permute-start.25 = (bf16[2,192,384]{2,1,0:T(8,128)(2,1)}, bf16[2,192,384]{2,1,0:T(8,128)(2,1)}, u32[]{:S(2)}, u32[]{:S(2)}) collective-permute-start(bf16[2,192,384]{2,1,0:T(8,128)(2,1)} %get-tuple-element.244), channel_id=1, source_target_pairs={{0,8},{1,9},{2,10},{3,11},{4,12},{5,13},{6,14},{7,15},{8,0},{9,1},... | collective-permute-start | bytes 884744 | tf_op jit(solution)/shard_map/ppermute | solution.py:807
  237.5 4.4 %collective-permute-start.26 = (bf16[16,48,1280]{2,1,0:T(8,128)(2,1)}, bf16[16,48,1280]{2,1,0:T(8,128)(2,1)}, u32[]{:S(2)}, u32[]{:S(2)}) collective-permute-start(bf16[16,48,1280]{2,1,0:T(8,128)(2,1)} %get-tuple-element.247), channel_id=1, source_target_pairs={{0,1},{1,0},{2,3},{3,2},{4,5},{5,4},{6,7},{7,6},{8,9},{9,8},{10,11... | collective-permute-start | bytes 5898248 | tf_op jit(solution)/shard_map/ppermute | solution.py:807
  241.8 11.0 %collective-permute-start.27 = (bf16[2,48,1920]{2,1,0:T(8,128)(2,1)}, bf16[2,48,1920]{2,1,0:T(8,128)(2,1)S(1)}, u32[]{:S(2)}, u32[]{:S(2)}) collective-permute-start(bf16[2,48,1920]{2,1,0:T(8,128)(2,1)} %get-tuple-element.256), channel_id=1, source_target_pairs={{0,8},{1,9},{2,10},{3,11},{4,12},{5,13},{6,14},{7,15},{8,0},{9,1},... | collective-permute-start | bytes 1105928 | tf_op jit(solution)/shard_map/ppermute | solution.py:807
  252.8 14.4 %collective-permute-start.28 = (bf16[8,48,1280]{2,1,0:T(8,128)(2,1)}, bf16[8,48,1280]{2,1,0:T(8,128)(2,1)}, u32[]{:S(2)}, u32[]{:S(2)}) collective-permute-start(bf16[8,48,1280]{2,1,0:T(8,128)(2,1)} %get-tuple-element.263), channel_id=1, source_target_pairs={{0,4},{1,3},{2,6},{3,1},{4,0},{5,7},{6,2},{7,5},{8,12},{9,11},{10,... | collective-permute-start | bytes 2949128 | tf_op jit(solution)/shard_map/ppermute | solution.py:807
  255.2 17.0 %collective-permute-start.33 = (bf16[1,48,1920]{2,1,0:T(8,128)(2,1)}, bf16[1,48,1920]{2,1,0:T(8,128)(2,1)}, u32[]{:S(2)}, u32[]{:S(2)}) collective-permute-start(bf16[1,48,1920]{2,1,0:T(8,128)(2,1)} %get-tuple-element.268), channel_id=1, source_target_pairs={{0,16},{1,17},{2,18},{3,19},{4,20},{5,21},{6,22},{7,23},{8,24},{9,... | collective-permute-start | bytes 552968 | tf_op jit(solution)/shard_map/ppermute | solution.py:807
  255.5 16.7 %collective-permute-start.34 = (bf16[1,192,384]{2,1,0:T(8,128)(2,1)}, bf16[1,192,384]{2,1,0:T(8,128)(2,1)}, u32[]{:S(2)}, u32[]{:S(2)}) collective-permute-start(bf16[1,192,384]{2,1,0:T(8,128)(2,1)} %get-tuple-element.270), channel_id=1, source_target_pairs={{0,16},{1,17},{2,18},{3,19},{4,20},{5,21},{6,22},{7,23},{8,24},{9,... | collective-permute-start | bytes 442376 | tf_op jit(solution)/shard_map/ppermute | solution.py:807
  268.7 8.9 %collective-permute-start.29 = (bf16[4,48,1280]{2,1,0:T(8,128)(2,1)S(1)}, bf16[4,48,1280]{2,1,0:T(8,128)(2,1)S(1)}, u32[]{:S(2)}, u32[]{:S(2)}) collective-permute-start(bf16[4,48,1280]{2,1,0:T(8,128)(2,1)S(1)} %get-tuple-element.291), channel_id=1, source_target_pairs={{0,2},{1,5},{2,0},{3,7},{4,6},{5,1},{6,4},{7,3},{8,10},{9,13},{10,... | collective-permute-start | bytes 1474568 | tf_op jit(solution)/shard_map/ppermute | solution.py:807
  274.3 5.2 %collective-permute-start.35 = (bf16[24,1920]{1,0:T(8,128)(2,1)S(1)}, bf16[24,1920]{1,0:T(8,128)(2,1)S(1)}, u32[]{:S(2)}, u32[]{:S(2)}) collective-permute-start(bf16[24,1920]{1,0:T(8,128)(2,1)S(1)} %fusion.1), channel_id=1, source_target_pairs={{0,1},{1,0},{2,3},{3,2},{4,5},{5,4},{6,7},{7,6},{8,9},{9,8},{10,11... | collective-permute-start | bytes 276488 | tf_op jit(solution)/shard_map/ppermute | solution.py:807
  277.7 6.7 %collective-permute-start.30 = (bf16[2,48,1280]{2,1,0:T(8,128)(2,1)S(1)}, bf16[2,48,1280]{2,1,0:T(8,128)(2,1)S(1)}, u32[]{:S(2)}, u32[]{:S(2)}) collective-permute-start(bf16[2,48,1280]{2,1,0:T(8,128)(2,1)S(1)} %get-tuple-element.297), channel_id=1, source_target_pairs={{0,8},{1,9},{2,10},{3,11},{4,12},{5,13},{6,14},{7,15},{8,0},{9,1},... | collective-permute-start | bytes 737288 | tf_op jit(solution)/shard_map/ppermute | solution.py:807
  284.5 5.8 %collective-permute-start.31 = (bf16[1,48,1280]{2,1,0:T(8,128)(2,1)S(1)}, bf16[1,48,1280]{2,1,0:T(8,128)(2,1)S(1)}, u32[]{:S(2)}, u32[]{:S(2)}) collective-permute-start(bf16[1,48,1280]{2,1,0:T(8,128)(2,1)S(1)} %add_convert_fusion.18), channel_id=1, source_target_pairs={{0,16},{1,17},{2,18},{3,19},{4,20},{5,21},{6,22},{7,23},{8,24},{9,... | collective-permute-start | bytes 368648 | tf_op jit(solution)/shard_map/ppermute | solution.py:807
  (21 other events, 154.3 us)

commit v3 on v2

--- a/solution.py
+++ b/solution.py
@@ -95,9 +95,17 @@
     return high, rest.astype(BF16), rest
 
 
+def with_slots(x_ref, pick_ref, slots):
+    high, middle, rest = split_bf16(slots)
+    low = (rest - middle.astype(F32)).astype(BF16)
+    picks = pick_ref[...]
+    slot = nn(jnp.concatenate([picks, picks, picks], axis=1), jnp.concatenate([high, middle, low], axis=0))
+    return x_ref[...].astype(F32) + slot
+
+
 def project_kernel(
     tbl, x_ref, pick_ref, embed_ref, own_low, own_high, other_low, other_high,
-    hidden_ref, low_ref, qkv_ref, vec_ref, w_ref, weight, offset, factor, sems, out_sem,
+    low_ref, qkv_ref, vec_ref, slots_ref, w_ref, weight, offset, factor, sems, out_sem,
 ):
     step = pl.program_id(0)
     save = pltpu.make_async_copy(weight.at[:, pl.ds(0, 2 * QKV)], w_ref, out_sem.at[0])
@@ -122,12 +130,8 @@
             factor[:, at : at + HALF] = jnp.full((1, HALF), HEAD**-0.5, F32)
 
     slots = nt(embed_ref[...], weight[:, 2 * QKV : 2 * QKV + TDIM]) + vec_ref[8:9, :]
-    high, middle, rest = split_bf16(slots)
-    low = (rest - middle.astype(F32)).astype(BF16)
-    picks = pick_ref[...]
-    slot = nn(jnp.concatenate([picks, picks, picks], axis=1), jnp.concatenate([high, middle, low], axis=0))
-    hidden_ref[...] = x_ref[...].astype(F32) + slot
-    low_ref[...] = hidden_ref[...].astype(BF16)
+    slots_ref[...] = slots
+    low_ref[...] = with_slots(x_ref, pick_ref, slots).astype(BF16)
 
     for j in range(3):
         at = slice(j * D, j * D + D)
@@ -189,7 +193,7 @@
     out_copy(HEADS // 2 - 1).wait()
 
 def expand_kernel(
-    tbl, hidden_ref, mix_ref, vec_ref, upb_ref, ua, ub, uc, ud,
+    tbl, x_ref, pick_ref, slots_ref, mix_ref, vec_ref, upb_ref, ua, ub, uc, ud,
     n1_ref, i1_ref, act_ref, slope_ref, mlow_ref, up_ref, up, wide, sems, out_sem,
 ):
     step = pl.program_id(0)
@@ -204,7 +208,7 @@
         for copy in copies[0]:
             copy.wait()
 
-    normed, inverse = normalize(hidden_ref[...] + nn(mix_ref[...], up[:, FF:]) + vec_ref[2:3, :])
+    normed, inverse = normalize(with_slots(x_ref, pick_ref, slots_ref[...]) + nn(mix_ref[...], up[:, FF:]) + vec_ref[2:3, :])
     n1_ref[...] = normed
     i1_ref[...] = inverse
     mlow_ref[...] = (normed * vec_ref[3:4, :] + vec_ref[4:5, :]).astype(BF16)
@@ -605,8 +609,8 @@
     return call(
         project_kernel, "project", (rows // BLOCK,),
         [rows_spec(BLOCK, D), rows_spec(BLOCK, slots), whole_spec((slots, TDIM))] + [ANY] * 4,
-        [rows_spec(BLOCK, D), rows_spec(BLOCK, D), rows_spec(BLOCK, 2 * QKV), whole_spec((16, D)), ANY],
-        [sds((rows, D), F32), sds((rows, D), BF16), sds((rows, 2 * QKV), BF16), sds((16, D), F32), sds((D, 2 * QKV), BF16)],
+        [rows_spec(BLOCK, D), rows_spec(BLOCK, 2 * QKV), whole_spec((16, D)), whole_spec((slots, D)), ANY],
+        [sds((rows, D), BF16), sds((rows, 2 * QKV), BF16), sds((16, D), F32), sds((slots, D), F32), sds((D, 2 * QKV), BF16)],
         [pltpu.VMEM((D, 2 * QKV + 2 * TDIM), BF16), pltpu.VMEM((1, 2 * QKV), F32), pltpu.VMEM((1, 2 * QKV), F32),
          pltpu.SemaphoreType.DMA((2, 32)), pltpu.SemaphoreType.DMA((1,))],
         6 * rows * D * D, 20 << 20, (tbl, x, pick, embed, *pieces),
@@ -628,18 +632,19 @@
     )
 
 
-def expand(tbl, hidden, mix, vec, upb, up):
+def expand(tbl, x, pick, slots, mix, vec, upb, up):
     rows = mix.shape[0]
     tile = 256
     return call(
         expand_kernel, "expand", (rows // tile,),
-        [rows_spec(tile, D), rows_spec(tile, D), whole_spec((16, D)), whole_spec((1, FF))] + [ANY] * 4,
+        [rows_spec(tile, D), rows_spec(tile, pick.shape[1]), whole_spec(slots.shape), rows_spec(tile, D), whole_spec((16, D)),
+         whole_spec((1, FF))] + [ANY] * 4,
         [rows_spec(tile, D), rows_spec(tile, 1), rows_spec(tile, FF), rows_spec(tile, FF), rows_spec(tile, D), ANY],
         [sds((rows, D), F32), sds((rows, 1), F32), sds((rows, FF), BF16), sds((rows, FF), BF16), sds((rows, D), BF16),
          sds((D, FF + D), BF16)],
         [pltpu.VMEM((D, FF + D), BF16), pltpu.VMEM((2, tile, D), F32), pltpu.SemaphoreType.DMA((2, 32)),
          pltpu.SemaphoreType.DMA((1,))],
-        2 * rows * D * (FF + D), 20 << 20, (tbl, hidden, mix, vec, upb, *up),
+        2 * rows * D * (FF + D), 20 << 20, (tbl, x, pick, slots, mix, vec, upb, *up),
     )
 
 
@@ -954,7 +959,7 @@
         a3 = send_on(a1, "core", n)
         u_got = send_on(u0, "a", n)
         d_got = send_on(d0, "z2", n)
-        hidden, low, qkv, vec, weight = project(tbl, inputs, pick, embed_in, (a0, a1, a2, a3))
+        low, qkv, vec, slots, weight = project(tbl, inputs, pick, embed_in, (a0, a1, a2, a3))
         qkv, u0, u_got, d0, d_got = tie(qkv, u0, u_got, d0, d_got)
         u0 = jnp.concatenate([u0, u_got], axis=0)
         d0 = jnp.concatenate([d0, d_got], axis=0)
@@ -972,16 +977,16 @@
         d1 = send_on(d0, "b", n)
         d2 = send_on(d0, "core", n)
         up_offset = vec[9:13].reshape(FF // D, n, shard).transpose(1, 0, 2).reshape(1, FF)
-        n1, i1, act, slope, mlow, up_full = expand(tbl, hidden, mix, vec, up_offset, (u0, u1, u2, u3))
+        n1, i1, act, slope, mlow, up_full = expand(tbl, inputs, pick, slots, mix, vec, up_offset, (u0, u1, u2, u3))
         act, d1 = tie(act, d1)
         d3 = send_on(d1, "core", n)
         down_pieces = (d0, d1, d2, d3)
     else:
         pick, segr, embed_in = slot_arrays(lengths, timesteps)
-        hidden, low, qkv, vec, weight = project(tbl, inputs, pick, embed_in, whole_gather(attn_halves, core))
+        low, qkv, vec, slots, weight = project(tbl, inputs, pick, embed_in, whole_gather(attn_halves, core))
         mix, probs = attend(1, qkv, pick, segr, attend(0, qkv, pick, segr, ()))
         up_offset = vec[9:13].reshape(FF // D, n, shard).transpose(1, 0, 2).reshape(1, FF)
-        n1, i1, act, slope, mlow, up_full = expand(tbl, hidden, mix, vec, up_offset, whole_gather(up_halves, core))
+        n1, i1, act, slope, mlow, up_full = expand(tbl, inputs, pick, slots, mix, vec, up_offset, whole_gather(up_halves, core))
         down_pieces = whole_gather(down_halves, core)
 
     res, dexp, din, df, ain, ff_vecs, up_vec, slot_first = contract(

time: 297 us -> 297 us (level)
  transfers between devices with their start and end apart: 37 -> 37, of which waited for: 17 -> 16; matrix products, arithmetic and copies ran while one was open for 11% -> 11% of each run, Pallas kernels for 39% -> 39%
where the time goes in v3:
time: 297 us; the launch traced here: 295 us
  Pallas kernels  158 us (53%)
  waiting for transfers between devices  49 us (16%)
  starting transfers between devices  38.3 us (13%)
  other arithmetic  32 us (11%)
  local copies, waits for them, and re-layouts  17.1 us (6%)
    pallas_call x14, Pallas kernels, call(): pl.pallas_call(kernel, name=name, grid_spec=pltpu.PrefetchScalarGridSpec(...  158 us
    ppermute x37, waiting for transfers between devices, send_on(): return lax.ppermute(value, 'fsdp', perm=tiled_route(n)[step])  49 us
    ppermute x37, starting transfers between devices, send_on(): return lax.ppermute(value, 'fsdp', perm=tiled_route(n)[step])  38.3 us
    convert_element_type x10, other arithmetic, add(): return (left.astype(F32) + right.astype(F32)).astype(BF16)  17.9 us
  transfers between devices with their start and end apart: 37, of which 16 were waited for; matrix products, arithmetic and copies ran while one was open for 11% of the time, Pallas kernels for 39%

profile of v3, /device:TPU:0, one launch (start us, length us, event | category | flops | bytes accessed | tf_op | source)
XLA Modules:
  0.0 295.2 jit_solution(18397799602345490128)
XLA Ops:
  7.6 4.0 %collective-permute-start.1 = (bf16[1,48,1280]{2,1,0:T(8,128)(2,1)S(1)}, bf16[1,48,1280]{2,1,0:T(8,128)(2,1)S(1)}, u32[]{:S(2)}, u32[]{:S(2)}) collective-permute-start(bf16[1,48,1280]{2,1,0:T(8,128)(2,1)S(1)} %maximum_bitcast_fusion.2), channel_id=1, source_target_pairs={{0,16},{1,17},{2,18},{3,19},{4,20},{5,21},{6,22},{7,23},{8,24},{9,... | collective-permute-start | bytes 368648 | tf_op jit(solution)/shard_map/ppermute | solution.py:812
  13.5 4.4 %collective-permute-done.1 = bf16[1,48,1280]{2,1,0:T(8,128)(2,1)S(1)} collective-permute-done((bf16[1,48,1280]{2,1,0:T(8,128)(2,1)S(1)}, bf16[1,48,1280]{2,1,0:T(8,128)(2,1)S(1)}, u32[]{:S(2)}, u32[]{:S(2)}) %collective-permute-start.1) | collective-permute-done | bytes 122912 | tf_op jit(solution)/shard_map/ppermute | solution.py:812
  19.0 6.5 %collective-permute-done.2 = bf16[2,48,1280]{2,1,0:T(8,128)(2,1)S(1)} collective-permute-done((bf16[2,48,1280]{2,1,0:T(8,128)(2,1)S(1)}, bf16[2,48,1280]{2,1,0:T(8,128)(2,1)S(1)}, u32[]{:S(2)}, u32[]{:S(2)}) %collective-permute-start.2) | collective-permute-done | bytes 245792 | tf_op jit(solution)/shard_map/ppermute | solution.py:812
  27.0 3.0 %collective-permute-start.4 = (bf16[1,48,1920]{2,1,0:T(8,128)(2,1)S(1)}, bf16[1,48,1920]{2,1,0:T(8,128)(2,1)S(1)}, u32[]{:S(2)}, u32[]{:S(2)}) collective-permute-start(bf16[1,48,1920]{2,1,0:T(8,128)(2,1)S(1)} %maximum_bitcast_fusion), channel_id=1, source_target_pairs={{0,16},{1,17},{2,18},{3,19},{4,20},{5,21},{6,22},{7,23},{8,24},{9,... | collective-permute-start | bytes 552968 | tf_op jit(solution)/shard_map/ppermute | solution.py:812
  30.2 7.9 %collective-permute-done.4 = bf16[1,48,1920]{2,1,0:T(8,128)(2,1)S(1)} collective-permute-done((bf16[1,48,1920]{2,1,0:T(8,128)(2,1)S(1)}, bf16[1,48,1920]{2,1,0:T(8,128)(2,1)S(1)}, u32[]{:S(2)}, u32[]{:S(2)}) %collective-permute-start.4) | collective-permute-done | bytes 184352 | tf_op jit(solution)/shard_map/ppermute | solution.py:812
  42.2 7.4 %collective-permute-done.6 = bf16[2,48,1920]{2,1,0:T(8,128)(2,1)S(1)} collective-permute-done((bf16[2,48,1920]{2,1,0:T(8,128)(2,1)S(1)}, bf16[2,48,1920]{2,1,0:T(8,128)(2,1)S(1)}, u32[]{:S(2)}, u32[]{:S(2)}) %collective-permute-start.6) | collective-permute-done | bytes 368672 | tf_op jit(solution)/shard_map/ppermute | solution.py:812
  49.7 2.7 collective-permute-done.5.own_high
  55.1 11.2 %project.1 = (bf16[1024,768]{1,0:T(8,128)(2,1)}, bf16[1024,2304]{1,0:T(8,128)(2,1)}, f32[16,768]{1,0:T(8,128)}, f32[16,768]{1,0:T(8,128)}, bf16[768,2304]{1,0:T(8,128)(2,1)}) custom-call(s32[80]{0:T(128)} %concatenate.75.tbl, bf16[1024,768]{1,0:T(8,128)(2,1)} %x_ref.3, bf16[1024,16]{1,0:T(8,128)(2,1)} %fusion.pick_ref, ...), custom_call_target="tpu_custom_call" | custom-call | flops 3623878656 | bytes 20971520 | tf_op jit(solution)/shard_map/project/pallas_call | solution.py:573
  67.3 2.0 constant_dynamic-update-slice_fusion.ua
  71.0 3.9 %collective-permute-start.12 = (bf16[2,192,384]{2,1,0:T(8,128)(2,1)S(1)}, bf16[2,192,384]{2,1,0:T(8,128)(2,1)S(1)}, u32[]{:S(2)}, u32[]{:S(2)}) collective-permute-start(bf16[2,192,384]{2,1,0:T(8,128)(2,1)S(1)} %constant_dynamic-update-slice_fusion.2), channel_id=1, source_target_pairs={{0,8},{1,9},{2,10},{3,11},{4,12},{5,13},{6,14},{7,15},{8,0},{9,1},... | collective-permute-start | bytes 884744 | tf_op jit(solution)/shard_map/ppermute | solution.py:812
  74.8 8.8 %attend.2 = (bf16[1024,768]{1,0:T(8,128)(2,1)}, bf16[2,6,4,256,256]{4,3,2,1,0:T(8,128)(2,1)}) custom-call(bf16[1024,2304]{1,0:T(8,128)(2,1)} %get-tuple-element.172.qkv_ref.qkv_all, bf16[1024,16]{1,0:T(8,128)(2,1)} %fusion.pick_ref, f32[2,1,512]{2,1,0:T(1,128)} %add_convert_fusion.20.segr_ref), custom_call_target="tpu_custom_call" | custom-call | flops 1207959552 | bytes 20971520 | tf_op jit(solution)/shard_map/attend/pallas_call | solution.py:573
  86.9 8.8 %attend.3 = (bf16[1024,768]{1,0:T(8,128)(2,1)}, bf16[2,6,4,256,256]{4,3,2,1,0:T(8,128)(2,1)}) custom-call(bf16[1024,2304]{1,0:T(8,128)(2,1)} %get-tuple-element.172.qkv_ref.qkv_all, bf16[1024,16]{1,0:T(8,128)(2,1)} %fusion.pick_ref, f32[2,1,512]{2,1,0:T(1,128)} %add_convert_fusion.20.segr_ref, ...), custom_call_target="tpu_custom_call", output_to_operand_aliasing={{0}: (3, {}), {1}: (4, {})} | custom-call | flops 1207959552 | bytes 20971520 | tf_op jit(solution)/shard_map/attend/pallas_call | solution.py:573
  101.6 18.4 %expand.1 = (f32[1024,768]{1,0:T(8,128)}, f32[1024,1]{1,0:T(8,128)}, bf16[1024,3072]{1,0:T(8,128)(2,1)}, bf16[1024,3072]{1,0:T(8,128)(2,1)}, bf16[1024,768]{1,0:T(8,128)(2,1)}, /*index=5*/bf16[768,3840]{1,0:T(8,128)(2,1)}) custom-call(s32[80]{0:T(128)} %concatenate.75.tbl, bf16[1024,768]{1,0:T(8,128)(2,1)} %x_ref.3, bf16[1024,16]{1,0:T(8,128)(2,1)} %fusion.pick_ref, ...), custom_call_target="tpu_custom_call" | custom-call | flops 6039797760 | bytes 20971520 | tf_op jit(solution)/shard_map/expand/pallas_call | solution.py:573
  120.5 2.8 collective-permute-done.18.dd
  123.3 30.1 %contract.1 = (bf16[1024,768]{1,0:T(8,128)(2,1)}, bf16[1024,3072]{1,0:T(8,128)(2,1)}, bf16[1024,768]{1,0:T(8,128)(2,1)}, f32[1024,768]{1,0:T(8,128)}, bf16[1024,...) custom-call(s32[80]{0:T(128)} %concatenate.75.tbl, ...), custom_call_target="tpu_custom_call" | custom-call | flops 14495514624 | bytes 20971520 | tf_op jit(solution)/shard_map/contract/pallas_call | solution.py:573
  153.4 10.3 %down_grad.1 = (bf16[16,192,384]{2,1,0:T(8,128)(2,1)}, bf16[16,192,384]{2,1,0:T(8,128)(2,1)}) custom-call(s32[80]{0:T(128)} %concatenate.75.tbl, bf16[1024,3072]{1,0:T(8,128)(2,1)} %get-tuple-element.188.act_ref, bf16[1024,768]{1,0:T(8,128)(2,1)} %get-tuple-element.197.din_ref), custom_call_target="tpu_custom_call" | custom-call | flops 4831838208 | bytes 20971520 | tf_op jit(solution)/shard_map/down_grad/pallas_call | solution.py:573
  166.1 7.8 %up_other.1 = bf16[16,48,1920]{2,1,0:T(8,128)(2,1)} custom-call(s32[80]{0:T(128)} %concatenate.75.tbl, bf16[1024,768]{1,0:T(8,128)(2,1)} %get-tuple-element.205.mlow_ref, bf16[1024,3072]{1,0:T(8,128)(2,1)} %get-tuple-element.201.dexp_ref, bf16[1024,768]{1,0:T(8,128)(2,1)} %get-tuple-element.178.mix_ref.mix_all, ...), custom_call_target="tpu_custom_call" | custom-call | flops 3019898880 | bytes 20971520 | tf_op jit(solution)/shard_map/up_other/pallas_call | solution.py:573
  174.2 4.4 %add_convert_fusion = (bf16[8,192,384]{2,1,0:T(8,128)(2,1)}, bf16[8,192,384]{2,1,0:T(8,128)(2,1)}) fusion(bf16[16,192,384]{2,1,0:T(8,128)(2,1)} %collective-permute-done.19, bf16[16,192,384]{2,1,0:T(8,128)(2,1)} %get-tuple-element.206), kind=kLoop, calls=%fused_computation | loop fusion | flops 4718592 | bytes 7077888 | tf_op jit(solution)/shard_map/convert_element_type | solution.py:868
  180.6 11.3 %up_own.1 = (bf16[8,48,1920]{2,1,0:T(8,128)(2,1)}, bf16[8,48,1920]{2,1,0:T(8,128)(2,1)}) custom-call(s32[80]{0:T(128)} %concatenate.75.tbl, bf16[1024,768]{1,0:T(8,128)(2,1)} %get-tuple-element.205.mlow_ref, bf16[1024,3072]{1,0:T(8,128)(2,1)} %get-tuple-element.201.dexp_ref, bf16[1024,768]{1,0:T(8,128)(2,1)} %get-tuple-element.178.mix_ref.mix_all, ...), custom_call_target="tpu_custom_call" | custom-call | flops 3019898880 | bytes 20971520 | tf_op jit(solution)/shard_map/up_own/pallas_call | solution.py:573
  193.2 10.9 %attention_backward.2 = (bf16[1024,2304]{1,0:T(8,128)(2,1)}, f32[16,2304]{1,0:T(8,128)}) custom-call(bf16[1024,768]{1,0:T(8,128)(2,1)} %get-tuple-element.220.ain_all.ain_ref, bf16[1024,768]{1,0:T(8,128)(2,1)} %get-tuple-element.178.mix_ref.mix_all, bf16[1024,2304]{1,0:T(8,128)(2,1)} %get-tuple-element.172.qkv_ref.qkv_all, ...), custom_call_target="tpu_custom_call" | custom-call | flops 1207959552 | bytes 20971520 | tf_op jit(solution)/shard_map/attention_backward/pallas_call | solution.py:573
  204.1 2.9 add_convert_fusion.4
  207.9 10.9 %attention_backward.3 = (bf16[1024,2304]{1,0:T(8,128)(2,1)}, f32[16,2304]{1,0:T(8,128)}) custom-call(bf16[1024,768]{1,0:T(8,128)(2,1)} %get-tuple-element.220.ain_all.ain_ref, bf16[1024,768]{1,0:T(8,128)(2,1)} %get-tuple-element.178.mix_ref.mix_all, bf16[1024,2304]{1,0:T(8,128)(2,1)} %get-tuple-element.172.qkv_ref.qkv_all, ...), custom_call_target="tpu_custom_call", output_to_operand_aliasing={{0}: (6, {})} | custom-call | flops 1207959552 | bytes 20971520 | tf_op jit(solution)/shard_map/attention_backward/pallas_call | solution.py:573
  219.7 3.1 %add_convert_fusion.2 = (bf16[4,48,1920]{2,1,0:T(8,128)(2,1)}, bf16[4,48,1920]{2,1,0:T(8,128)(2,1)S(1)}) fusion(bf16[8,48,1920]{2,1,0:T(8,128)(2,1)} %collective-permute-done.23, bf16[8,48,1920]{2,1,0:T(8,128)(2,1)} %get-tuple-element.230), kind=kLoop, calls=%fused_computation.2 | loop fusion | flops 2949120 | bytes 4423680 | tf_op jit(solution)/shard_map/convert_element_type | solution.py:868
  224.8 2.6 collective-permute-start.25
  227.4 9.3 %qkv_other.1 = (bf16[768,256]{1,0:T(8,128)(2,1)}, bf16[16,48,1280]{2,1,0:T(8,128)(2,1)}) custom-call(s32[80]{0:T(128)} %concatenate.75.tbl, bf16[1024,768]{1,0:T(8,128)(2,1)} %get-tuple-element.245.low_ref, bf16[1024,2304]{1,0:T(8,128)(2,1)} %get-tuple-element.233.dqkv_ref, f32[16,768]{1,0:T(8,128)} %get-tuple-element.234.first_ref, ...), custom_call_target="tpu_custom_call" | custom-call | flops 1811939328 | bytes 20971520 | tf_op jit(solution)/shard_map/qkv_other/pallas_call | solution.py:573
  238.8 2.1 add_convert_fusion.8
  242.9 8.7 %qkv_own.1 = (bf16[8,48,1280]{2,1,0:T(8,128)(2,1)}, bf16[8,48,1280]{2,1,0:T(8,128)(2,1)}) custom-call(s32[80]{0:T(128)} %concatenate.75.tbl, bf16[1024,768]{1,0:T(8,128)(2,1)} %get-tuple-element.245.low_ref, bf16[1024,2304]{1,0:T(8,128)(2,1)} %get-tuple-element.233.dqkv_ref, bf16[768,256]{1,0:T(8,128)(2,1)} %get-tuple-element.246.small_ref, ...), custom_call_target="tpu_custom_call" | custom-call | flops 1811939328 | bytes 20971520 | tf_op jit(solution)/shard_map/qkv_own/pallas_call | solution.py:573
  254.8 2.6 collective-permute-start.34
  257.4 9.0 %input_grad.1 = f32[1024,768]{1,0:T(8,128)} custom-call(f32[1024,768]{1,0:T(8,128)} %get-tuple-element.261.df_ref, bf16[1024,2304]{1,0:T(8,128)(2,1)} %get-tuple-element.233.dqkv_ref, bf16[768,2304]{1,0:T(8,128)(2,1)} %get-tuple-element.237.w_all.w_ref), custom_call_target="tpu_custom_call" | custom-call | flops 3623878656 | bytes 20971520 | tf_op jit(solution)/shard_map/input_grad/pallas_call | solution.py:573
  269.4 2.2 collective-permute-done.34
  278.8 5.0 %collective-permute-done.30 = bf16[2,48,1280]{2,1,0:T(8,128)(2,1)S(1)} collective-permute-done((bf16[2,48,1280]{2,1,0:T(8,128)(2,1)S(1)}, bf16[2,48,1280]{2,1,0:T(8,128)(2,1)S(1)}, u32[]{:S(2)}, u32[]{:S(2)}) %collective-permute-start.30) | collective-permute-done | bytes 245792 | tf_op jit(solution)/shard_map/ppermute | solution.py:812
  284.8 4.9 %collective-permute-done.31 = bf16[1,48,1280]{2,1,0:T(8,128)(2,1)S(1)} collective-permute-done((bf16[1,48,1280]{2,1,0:T(8,128)(2,1)S(1)}, bf16[1,48,1280]{2,1,0:T(8,128)(2,1)S(1)}, u32[]{:S(2)}, u32[]{:S(2)}) %collective-permute-start.31) | collective-permute-done | bytes 122912 | tf_op jit(solution)/shard_map/ppermute | solution.py:812
  (180 shorter events, 63.8 us)
Async XLA Ops:
  7.6 10.3 %collective-permute-start.1 = (bf16[1,48,1280]{2,1,0:T(8,128)(2,1)S(1)}, bf16[1,48,1280]{2,1,0:T(8,128)(2,1)S(1)}, u32[]{:S(2)}, u32[]{:S(2)}) collective-permute-start(bf16[1,48,1280]{2,1,0:T(8,128)(2,1)S(1)} %maximum_bitcast_fusion.2), channel_id=1, source_target_pairs={{0,16},{1,17},{2,18},{3,19},{4,20},{5,21},{6,22},{7,23},{8,24},{9,... | collective-permute-start | bytes 368648 | tf_op jit(solution)/shard_map/ppermute | solution.py:812
  18.0 7.6 %collective-permute-start.2 = (bf16[2,48,1280]{2,1,0:T(8,128)(2,1)S(1)}, bf16[2,48,1280]{2,1,0:T(8,128)(2,1)S(1)}, u32[]{:S(2)}, u32[]{:S(2)}) collective-permute-start(bf16[2,48,1280]{2,1,0:T(8,128)(2,1)S(1)} %pad_maximum_fusion.6), channel_id=1, source_target_pairs={{0,8},{1,9},{2,10},{3,11},{4,12},{5,13},{6,14},{7,15},{8,0},{9,1},... | collective-permute-start | bytes 737288 | tf_op jit(solution)/shard_map/ppermute | solution.py:812
  25.6 12.6 %collective-permute-start.3 = (bf16[4,48,1280]{2,1,0:T(8,128)(2,1)S(1)}, bf16[4,48,1280]{2,1,0:T(8,128)(2,1)S(1)}, u32[]{:S(2)}, u32[]{:S(2)}) collective-permute-start(bf16[4,48,1280]{2,1,0:T(8,128)(2,1)S(1)} %pad_maximum_fusion.2), channel_id=1, source_target_pairs={{0,2},{1,5},{2,0},{3,7},{4,6},{5,1},{6,4},{7,3},{8,10},{9,13},{10,... | collective-permute-start | bytes 1474568 | tf_op jit(solution)/shard_map/ppermute | solution.py:812
  27.0 11.0 %collective-permute-start.4 = (bf16[1,48,1920]{2,1,0:T(8,128)(2,1)S(1)}, bf16[1,48,1920]{2,1,0:T(8,128)(2,1)S(1)}, u32[]{:S(2)}, u32[]{:S(2)}) collective-permute-start(bf16[1,48,1920]{2,1,0:T(8,128)(2,1)S(1)} %maximum_bitcast_fusion), channel_id=1, source_target_pairs={{0,16},{1,17},{2,18},{3,19},{4,20},{5,21},{6,22},{7,23},{8,24},{9,... | collective-permute-start | bytes 552968 | tf_op jit(solution)/shard_map/ppermute | solution.py:812
  38.3 14.2 %collective-permute-start.5 = (bf16[8,48,1280]{2,1,0:T(8,128)(2,1)S(1)}, bf16[8,48,1280]{2,1,0:T(8,128)(2,1)S(1)}, u32[]{:S(2)}, u32[]{:S(2)}) collective-permute-start(bf16[8,48,1280]{2,1,0:T(8,128)(2,1)S(1)} %pad_maximum_fusion.own_low), channel_id=1, source_target_pairs={{0,4},{1,3},{2,6},{3,1},{4,0},{5,7},{6,2},{7,5},{8,12},{9,11},{10,... | collective-permute-start | bytes 2949128 | tf_op jit(solution)/shard_map/ppermute | solution.py:812
  38.9 10.7 %collective-permute-start.6 = (bf16[2,48,1920]{2,1,0:T(8,128)(2,1)S(1)}, bf16[2,48,1920]{2,1,0:T(8,128)(2,1)S(1)}, u32[]{:S(2)}, u32[]{:S(2)}) collective-permute-start(bf16[2,48,1920]{2,1,0:T(8,128)(2,1)S(1)} %pad_maximum_fusion.3), channel_id=1, source_target_pairs={{0,8},{1,9},{2,10},{3,11},{4,12},{5,13},{6,14},{7,15},{8,0},{9,1},... | collective-permute-start | bytes 1105928 | tf_op jit(solution)/shard_map/ppermute | solution.py:812
  41.8 12.2 %collective-permute-start.7 = (bf16[8,48,1280]{2,1,0:T(8,128)(2,1)S(1)}, bf16[8,48,1280]{2,1,0:T(8,128)(2,1)S(1)}, u32[]{:S(2)}, u32[]{:S(2)}) collective-permute-start(bf16[8,48,1280]{2,1,0:T(8,128)(2,1)S(1)} %pad_maximum_fusion.own_low), channel_id=1, source_target_pairs={{0,1},{1,0},{2,3},{3,2},{4,5},{5,4},{6,7},{7,6},{8,9},{9,8},{10,11... | collective-permute-start | bytes 2949128 | tf_op jit(solution)/shard_map/ppermute | solution.py:812
  52.4 13.9 %collective-permute-start.9 = (bf16[4,48,1920]{2,1,0:T(8,128)(2,1)S(1)}, bf16[4,48,1920]{2,1,0:T(8,128)(2,1)}, u32[]{:S(2)}, u32[]{:S(2)}) collective-permute-start(bf16[4,48,1920]{2,1,0:T(8,128)(2,1)S(1)} %pad_maximum_fusion.1), channel_id=1, source_target_pairs={{0,2},{1,5},{2,0},{3,7},{4,6},{5,1},{6,4},{7,3},{8,10},{9,13},{10,... | collective-permute-start | bytes 2211848 | tf_op jit(solution)/shard_map/ppermute | solution.py:812
  54.0 12.4 %collective-permute-start.10 = (bf16[1,192,384]{2,1,0:T(8,128)(2,1)S(1)}, bf16[1,192,384]{2,1,0:T(8,128)(2,1)}, u32[]{:S(2)}, u32[]{:S(2)}) collective-permute-start(bf16[1,192,384]{2,1,0:T(8,128)(2,1)S(1)} %maximum_bitcast_fusion.1), channel_id=1, source_target_pairs={{0,16},{1,17},{2,18},{3,19},{4,20},{5,21},{6,22},{7,23},{8,24},{9,... | collective-permute-start | bytes 442376 | tf_op jit(solution)/shard_map/ppermute | solution.py:812
  69.4 14.3 %collective-permute-start.11 = (bf16[8,48,1920]{2,1,0:T(8,128)(2,1)}, bf16[8,48,1920]{2,1,0:T(8,128)(2,1)}, u32[]{:S(2)}, u32[]{:S(2)}) collective-permute-start(bf16[8,48,1920]{2,1,0:T(8,128)(2,1)} %constant_dynamic-update-slice_fusion.ua), channel_id=1, source_target_pairs={{0,1},{1,0},{2,3},{3,2},{4,5},{5,4},{6,7},{7,6},{8,9},{9,8},{10,11... | collective-permute-start | bytes 4423688 | tf_op jit(solution)/shard_map/ppermute | solution.py:812
  69.5 26.2 %collective-permute-start.13 = (bf16[8,48,1920]{2,1,0:T(8,128)(2,1)}, bf16[8,48,1920]{2,1,0:T(8,128)(2,1)}, u32[]{:S(2)}, u32[]{:S(2)}) collective-permute-start(bf16[8,48,1920]{2,1,0:T(8,128)(2,1)} %constant_dynamic-update-slice_fusion.ua), channel_id=1, source_target_pairs={{0,4},{1,3},{2,6},{3,1},{4,0},{5,7},{6,2},{7,5},{8,12},{9,11},{10,... | collective-permute-start | bytes 4423688 | tf_op jit(solution)/shard_map/ppermute | solution.py:812
  71.0 12.7 %collective-permute-start.12 = (bf16[2,192,384]{2,1,0:T(8,128)(2,1)S(1)}, bf16[2,192,384]{2,1,0:T(8,128)(2,1)S(1)}, u32[]{:S(2)}, u32[]{:S(2)}) collective-permute-start(bf16[2,192,384]{2,1,0:T(8,128)(2,1)S(1)} %constant_dynamic-update-slice_fusion.2), channel_id=1, source_target_pairs={{0,8},{1,9},{2,10},{3,11},{4,12},{5,13},{6,14},{7,15},{8,0},{9,1},... | collective-permute-start | bytes 884744 | tf_op jit(solution)/shard_map/ppermute | solution.py:812
  85.4 10.3 %collective-permute-start.14 = (bf16[4,192,384]{2,1,0:T(8,128)(2,1)S(1)}, bf16[4,192,384]{2,1,0:T(8,128)(2,1)}, u32[]{:S(2)}, u32[]{:S(2)}) collective-permute-start(bf16[4,192,384]{2,1,0:T(8,128)(2,1)S(1)} %constant_dynamic-update-slice_fusion.4), channel_id=1, source_target_pairs={{0,2},{1,5},{2,0},{3,7},{4,6},{5,1},{6,4},{7,3},{8,10},{9,13},{10,... | collective-permute-start | bytes 1769480 | tf_op jit(solution)/shard_map/ppermute | solution.py:812
  95.8 5.8 %collective-permute-start.15 = (bf16[8,48,1920]{2,1,0:T(8,128)(2,1)}, bf16[8,48,1920]{2,1,0:T(8,128)(2,1)}, u32[]{:S(2)}, u32[]{:S(2)}) collective-permute-start(bf16[8,48,1920]{2,1,0:T(8,128)(2,1)} %collective-permute-done.13.ub), channel_id=1, source_target_pairs={{0,1},{1,0},{2,3},{3,2},{4,5},{5,4},{6,7},{7,6},{8,9},{9,8},{10,11... | collective-permute-start | bytes 4423688 | tf_op jit(solution)/shard_map/ppermute | solution.py:812
  98.7 21.3 %collective-permute-start.16 = (bf16[8,192,384]{2,1,0:T(8,128)(2,1)}, bf16[8,192,384]{2,1,0:T(8,128)(2,1)}, u32[]{:S(2)}, u32[]{:S(2)}) collective-permute-start(bf16[8,192,384]{2,1,0:T(8,128)(2,1)} %constant_dynamic-update-slice_fusion.6.da), channel_id=1, source_target_pairs={{0,4},{1,3},{2,6},{3,1},{4,0},{5,7},{6,2},{7,5},{8,12},{9,11},{10,... | collective-permute-start | bytes 3538952 | tf_op jit(solution)/shard_map/ppermute | solution.py:812
  101.4 19.0 %collective-permute-start.17 = (bf16[8,192,384]{2,1,0:T(8,128)(2,1)}, bf16[8,192,384]{2,1,0:T(8,128)(2,1)}, u32[]{:S(2)}, u32[]{:S(2)}) collective-permute-start(bf16[8,192,384]{2,1,0:T(8,128)(2,1)} %constant_dynamic-update-slice_fusion.6.da), channel_id=1, source_target_pairs={{0,1},{1,0},{2,3},{3,2},{4,5},{5,4},{6,7},{7,6},{8,9},{9,8},{10,11... | collective-permute-start | bytes 3538952 | tf_op jit(solution)/shard_map/ppermute | solution.py:812
  163.7 10.3 %collective-permute-start.19 = (bf16[16,192,384]{2,1,0:T(8,128)(2,1)}, bf16[16,192,384]{2,1,0:T(8,128)(2,1)}, u32[]{:S(2)}, u32[]{:S(2)}) collective-permute-start(bf16[16,192,384]{2,1,0:T(8,128)(2,1)} %get-tuple-element.203), channel_id=1, source_target_pairs={{0,1},{1,0},{2,3},{3,2},{4,5},{5,4},{6,7},{7,6},{8,9},{9,8},{10,11... | collective-permute-start | bytes 7077896 | tf_op jit(solution)/shard_map/ppermute | solution.py:812
  174.0 5.8 %collective-permute-start.20 = (bf16[16,48,1920]{2,1,0:T(8,128)(2,1)}, bf16[16,48,1920]{2,1,0:T(8,128)(2,1)}, u32[]{:S(2)}, u32[]{:S(2)}) collective-permute-start(bf16[16,48,1920]{2,1,0:T(8,128)(2,1)} %up_other.1), channel_id=1, source_target_pairs={{0,1},{1,0},{2,3},{3,2},{4,5},{5,4},{6,7},{7,6},{8,9},{9,8},{10,11... | collective-permute-start | bytes 8847368 | tf_op jit(solution)/shard_map/ppermute | solution.py:812
  179.7 24.3 %collective-permute-start.21 = (bf16[8,192,384]{2,1,0:T(8,128)(2,1)}, bf16[8,192,384]{2,1,0:T(8,128)(2,1)}, u32[]{:S(2)}, u32[]{:S(2)}) collective-permute-start(bf16[8,192,384]{2,1,0:T(8,128)(2,1)} %get-tuple-element.216), channel_id=1, source_target_pairs={{0,4},{1,3},{2,6},{3,1},{4,0},{5,7},{6,2},{7,5},{8,12},{9,11},{10,... | collective-permute-start | bytes 3538952 | tf_op jit(solution)/shard_map/ppermute | solution.py:812
  192.0 26.9 %collective-permute-start.23 = (bf16[8,48,1920]{2,1,0:T(8,128)(2,1)}, bf16[8,48,1920]{2,1,0:T(8,128)(2,1)}, u32[]{:S(2)}, u32[]{:S(2)}) collective-permute-start(bf16[8,48,1920]{2,1,0:T(8,128)(2,1)} %get-tuple-element.226), channel_id=1, source_target_pairs={{0,4},{1,3},{2,6},{3,1},{4,0},{5,7},{6,2},{7,5},{8,12},{9,11},{10,... | collective-permute-start | bytes 4423688 | tf_op jit(solution)/shard_map/ppermute | solution.py:812
  207.0 11.9 %collective-permute-start.22 = (bf16[4,192,384]{2,1,0:T(8,128)(2,1)}, bf16[4,192,384]{2,1,0:T(8,128)(2,1)S(1)}, u32[]{:S(2)}, u32[]{:S(2)}) collective-permute-start(bf16[4,192,384]{2,1,0:T(8,128)(2,1)} %get-tuple-element.224), channel_id=1, source_target_pairs={{0,2},{1,5},{2,0},{3,7},{4,6},{5,1},{6,4},{7,3},{8,10},{9,13},{10,... | collective-permute-start | bytes 1769480 | tf_op jit(solution)/shard_map/ppermute | solution.py:812
  223.7 13.0 %collective-permute-start.24 = (bf16[4,48,1920]{2,1,0:T(8,128)(2,1)}, bf16[4,48,1920]{2,1,0:T(8,128)(2,1)}, u32[]{:S(2)}, u32[]{:S(2)}) collective-permute-start(bf16[4,48,1920]{2,1,0:T(8,128)(2,1)} %get-tuple-element.242), channel_id=1, source_target_pairs={{0,2},{1,5},{2,0},{3,7},{4,6},{5,1},{6,4},{7,3},{8,10},{9,13},{10,... | collective-permute-start | bytes 2211848 | tf_op jit(solution)/shard_map/ppermute | solution.py:812
  224.8 11.9 %collective-permute-start.25 = (bf16[2,192,384]{2,1,0:T(8,128)(2,1)}, bf16[2,192,384]{2,1,0:T(8,128)(2,1)}, u32[]{:S(2)}, u32[]{:S(2)}) collective-permute-start(bf16[2,192,384]{2,1,0:T(8,128)(2,1)} %get-tuple-element.244), channel_id=1, source_target_pairs={{0,8},{1,9},{2,10},{3,11},{4,12},{5,13},{6,14},{7,15},{8,0},{9,1},... | collective-permute-start | bytes 884744 | tf_op jit(solution)/shard_map/ppermute | solution.py:812
  236.7 4.4 %collective-permute-start.26 = (bf16[16,48,1280]{2,1,0:T(8,128)(2,1)}, bf16[16,48,1280]{2,1,0:T(8,128)(2,1)}, u32[]{:S(2)}, u32[]{:S(2)}) collective-permute-start(bf16[16,48,1280]{2,1,0:T(8,128)(2,1)} %get-tuple-element.247), channel_id=1, source_target_pairs={{0,1},{1,0},{2,3},{3,2},{4,5},{5,4},{6,7},{7,6},{8,9},{9,8},{10,11... | collective-permute-start | bytes 5898248 | tf_op jit(solution)/shard_map/ppermute | solution.py:812
  241.1 11.0 %collective-permute-start.27 = (bf16[2,48,1920]{2,1,0:T(8,128)(2,1)}, bf16[2,48,1920]{2,1,0:T(8,128)(2,1)S(1)}, u32[]{:S(2)}, u32[]{:S(2)}) collective-permute-start(bf16[2,48,1920]{2,1,0:T(8,128)(2,1)} %get-tuple-element.256), channel_id=1, source_target_pairs={{0,8},{1,9},{2,10},{3,11},{4,12},{5,13},{6,14},{7,15},{8,0},{9,1},... | collective-permute-start | bytes 1105928 | tf_op jit(solution)/shard_map/ppermute | solution.py:812
  252.1 14.4 %collective-permute-start.28 = (bf16[8,48,1280]{2,1,0:T(8,128)(2,1)}, bf16[8,48,1280]{2,1,0:T(8,128)(2,1)}, u32[]{:S(2)}, u32[]{:S(2)}) collective-permute-start(bf16[8,48,1280]{2,1,0:T(8,128)(2,1)} %get-tuple-element.263), channel_id=1, source_target_pairs={{0,4},{1,3},{2,6},{3,1},{4,0},{5,7},{6,2},{7,5},{8,12},{9,11},{10,... | collective-permute-start | bytes 2949128 | tf_op jit(solution)/shard_map/ppermute | solution.py:812
  254.5 17.1 %collective-permute-start.33 = (bf16[1,48,1920]{2,1,0:T(8,128)(2,1)}, bf16[1,48,1920]{2,1,0:T(8,128)(2,1)}, u32[]{:S(2)}, u32[]{:S(2)}) collective-permute-start(bf16[1,48,1920]{2,1,0:T(8,128)(2,1)} %get-tuple-element.268), channel_id=1, source_target_pairs={{0,16},{1,17},{2,18},{3,19},{4,20},{5,21},{6,22},{7,23},{8,24},{9,... | collective-permute-start | bytes 552968 | tf_op jit(solution)/shard_map/ppermute | solution.py:812
  254.8 16.8 %collective-permute-start.34 = (bf16[1,192,384]{2,1,0:T(8,128)(2,1)}, bf16[1,192,384]{2,1,0:T(8,128)(2,1)}, u32[]{:S(2)}, u32[]{:S(2)}) collective-permute-start(bf16[1,192,384]{2,1,0:T(8,128)(2,1)} %get-tuple-element.270), channel_id=1, source_target_pairs={{0,16},{1,17},{2,18},{3,19},{4,20},{5,21},{6,22},{7,23},{8,24},{9,... | collective-permute-start | bytes 442376 | tf_op jit(solution)/shard_map/ppermute | solution.py:812
  268.0 8.9 %collective-permute-start.29 = (bf16[4,48,1280]{2,1,0:T(8,128)(2,1)S(1)}, bf16[4,48,1280]{2,1,0:T(8,128)(2,1)S(1)}, u32[]{:S(2)}, u32[]{:S(2)}) collective-permute-start(bf16[4,48,1280]{2,1,0:T(8,128)(2,1)S(1)} %get-tuple-element.291), channel_id=1, source_target_pairs={{0,2},{1,5},{2,0},{3,7},{4,6},{5,1},{6,4},{7,3},{8,10},{9,13},{10,... | collective-permute-start | bytes 1474568 | tf_op jit(solution)/shard_map/ppermute | solution.py:812
  273.6 5.2 %collective-permute-start.35 = (bf16[24,1920]{1,0:T(8,128)(2,1)S(1)}, bf16[24,1920]{1,0:T(8,128)(2,1)S(1)}, u32[]{:S(2)}, u32[]{:S(2)}) collective-permute-start(bf16[24,1920]{1,0:T(8,128)(2,1)S(1)} %fusion.1), channel_id=1, source_target_pairs={{0,1},{1,0},{2,3},{3,2},{4,5},{5,4},{6,7},{7,6},{8,9},{9,8},{10,11... | collective-permute-start | bytes 276488 | tf_op jit(solution)/shard_map/ppermute | solution.py:812
  277.0 6.8 %collective-permute-start.30 = (bf16[2,48,1280]{2,1,0:T(8,128)(2,1)S(1)}, bf16[2,48,1280]{2,1,0:T(8,128)(2,1)S(1)}, u32[]{:S(2)}, u32[]{:S(2)}) collective-permute-start(bf16[2,48,1280]{2,1,0:T(8,128)(2,1)S(1)} %get-tuple-element.297), channel_id=1, source_target_pairs={{0,8},{1,9},{2,10},{3,11},{4,12},{5,13},{6,14},{7,15},{8,0},{9,1},... | collective-permute-start | bytes 737288 | tf_op jit(solution)/shard_map/ppermute | solution.py:812
  283.8 5.8 %collective-permute-start.31 = (bf16[1,48,1280]{2,1,0:T(8,128)(2,1)S(1)}, bf16[1,48,1280]{2,1,0:T(8,128)(2,1)S(1)}, u32[]{:S(2)}, u32[]{:S(2)}) collective-permute-start(bf16[1,48,1280]{2,1,0:T(8,128)(2,1)S(1)} %add_convert_fusion.18), channel_id=1, source_target_pairs={{0,16},{1,17},{2,18},{3,19},{4,20},{5,21},{6,22},{7,23},{8,24},{9,... | collective-permute-start | bytes 368648 | tf_op jit(solution)/shard_map/ppermute | solution.py:812
  (21 other events, 154.3 us)
